TPU v7x, 32 devices: a whole 2x2x4 slice. The times are simulated.
32 devices in a mesh: gx: 4 (over x, core), gy: 2 (over y), gz: 4 (over z).
Axes of the slice: x: 2, y: 2, z: 4, core: 2. Of those that a mesh axis runs over, the one named last changes fastest.
Arguments:
- features: bfloat16 [32, 64, 32, 512], P(None, 'gx', 'gy', 'gz'), may hold values from -6 to 6
- weight: bfloat16 [27, 32], replicated, may hold values from -0.21875 to 0.21875
- bias: float32 [1], replicated, may hold values from -2 to 2
- label: int32 [64, 32, 512], P('gx', 'gy', 'gz'), may hold values from 0 to 1, as said below
Outputs:
- loss: float32 [1], replicated
- grad_features: bfloat16 [32, 64, 32, 512], P(None, 'gx', 'gy', 'gz')
- grad_weight: float32 [27, 32], replicated
- grad_bias: float32 [1], replicated
Inputs may be any that keep to these rules, and one draw needn't show every extreme that they name: label is 1 at vessel voxels and 0 elsewhere.
All inputs are finite; a program needn't handle non-finite values.
Results may differ from a plain program's by a relative error of at most 0.005.
Values may be sent and summed in bfloat16 or wider, within the bound.
No kernel may reach another device: no remote copies, remote signals or barrier semaphores. Data moves between devices by JAX's collectives and lax.ppermute only.
A program may use at most 128 MiB of HBM per device.

v0:
```python
import jax
import jax.numpy as jnp
from jax import lax
from jax.sharding import PartitionSpec as P

ITERS = 10


temper = 20.0
sharpness = 40.0


def padded(block, sides, width):
    for axis, dim in sides:
        count = lax.axis_size(axis)
        forward = [(i, i + 1) for i in range(count - 1)]
        backward = [(target, source) for source, target in forward]
        low = lax.ppermute(
            lax.slice_in_dim(block, block.shape[dim] - width, None, axis=dim), axis, forward
        )
        high = lax.ppermute(lax.slice_in_dim(block, 0, width, axis=dim), axis, backward)
        block = jnp.concatenate([low, block, high], axis=dim)
    return block


def tap_offsets():
    return [(i - 1, j - 1, k - 1) for i in range(3) for j in range(3) for k in range(3)]


def cross_inner(extended):
    total = (
        extended[:, 1:-1, 1:-1, 1:-1] + extended[:, 2:, 1:-1, 1:-1] + extended[:, :-2, 1:-1, 1:-1]
    )
    total = total + extended[:, 1:-1, 2:, 1:-1] + extended[:, 1:-1, :-2, 1:-1]
    return total + extended[:, 1:-1, 1:-1, 2:] + extended[:, 1:-1, 1:-1, :-2]


def box_inner(extended):
    part = extended[:, 2:] + extended[:, 1:-1] + extended[:, :-2]
    part = part[:, :, 2:] + part[:, :, 1:-1] + part[:, :, :-2]
    return part[:, :, :, 2:] + part[:, :, :, 1:-1] + part[:, :, :, :-2]


def cross_remote(field):
    return cross_inner(padded(field, (("gx", 1), ("gy", 2), ("gz", 3)), 1))


def box_remote(field):
    return box_inner(
        padded(field.astype(jnp.bfloat16), (("gx", 1), ("gy", 2), ("gz", 3)), 1).astype(field.dtype)
    )


def axis_counts(devices_along, position, local, margin):
    total = local * devices_along
    spot = position * local - margin + jnp.arange(local + 2 * margin, dtype=jnp.int32)
    inside = (spot >= 0) & (spot < total)
    count = 3.0 - (spot == 0).astype(jnp.float32) - (spot == total - 1).astype(jnp.float32)
    return (inside, count)


def grid_counts(cells_x, cells_y, cells_z, margin):
    in_x, count_x = axis_counts(lax.axis_size("gx"), lax.axis_index("gx"), cells_x, margin)
    in_y, count_y = axis_counts(lax.axis_size("gy"), lax.axis_index("gy"), cells_y, margin)
    in_z, count_z = axis_counts(lax.axis_size("gz"), lax.axis_index("gz"), cells_z, margin)
    inside = in_x[:, None, None] & in_y[None, :, None] & in_z[None, None, :]
    box_count = count_x[:, None, None] * count_y[None, :, None] * count_z[None, None, :]
    cross_count = count_x[:, None, None] + count_y[None, :, None] + count_z[None, None, :] - 2.0
    return (inside, jnp.maximum(box_count, 1.0), jnp.maximum(cross_count, 1.0))


def section(field, cross_fn, box_fn, inside, box_count, cross_count):
    shrink_exp = jnp.where(inside, jnp.exp(-temper * field), 0.0)
    cross_sum = cross_fn(shrink_exp)
    eroded = -jnp.log(cross_sum / cross_count) / temper
    grow_exp = jnp.where(inside, jnp.exp(temper * eroded), 0.0)
    box_sum = box_fn(grow_exp)
    opened = jnp.log(box_sum / box_count) / temper
    gap_scaled = sharpness * (field - opened)
    thinned = jax.nn.softplus(gap_scaled) / sharpness
    record = (shrink_exp, cross_sum, grow_exp, box_sum, jax.nn.sigmoid(gap_scaled), thinned)
    return (eroded, thinned, record)


def back_section(grad_thin, grad_next, record):
    shrink_exp, cross_sum, grow_exp, box_sum, slope_field, thinned = record
    grad_open = grad_thin * slope_field
    push_back = padded(
        (-grad_open / box_sum).astype(jnp.bfloat16), (("gx", 1), ("gy", 2), ("gz", 3)), 1
    ).astype(jnp.float32)
    grad_eroded = grad_next + grow_exp * box_inner(push_back)
    pull_back = padded(grad_eroded / cross_sum, (("gx", 1), ("gy", 2), ("gz", 3)), 1)
    return grad_open + shrink_exp * cross_inner(pull_back)


def skeleton_backward(cotangent, first_record, later_records, later_extras):

    def reverse_step(carry, inputs):
        weight_field, grad_next = carry
        record, extras = inputs
        skel_prev, lift_rate = extras
        thinned = record[5]
        grad_thin = weight_field * lift_rate * (1.0 - skel_prev)
        weight_field = weight_field * (1.0 - lift_rate * thinned)
        return ((weight_field, back_section(grad_thin, grad_next, record)), None)

    start = (cotangent, jnp.zeros_like(cotangent))
    (weight_field, grad_next), unused = lax.scan(
        reverse_step, start, (later_records, later_extras), reverse=True
    )
    return back_section(weight_field, grad_next, first_record)


def global_stats(local_totals):
    return lax.psum(local_totals, ("gx", "gy", "gz"))


def loss_from(totals):
    precision_term = (totals[0] + 1.0) / (totals[1] + 1.0)
    sensitivity = (totals[2] + 1.0) / (totals[3] + 1.0)
    cl_loss = 1.0 - 2.0 * precision_term * sensitivity / (precision_term + sensitivity)
    dice_loss = 1.0 - (2.0 * totals[4] + 1.0) / (totals[5] + totals[6] + 1.0)
    return 0.5 * dice_loss + 0.5 * cl_loss


def per_device(features, weight, bias, label):
    channels, cells_x, cells_y, cells_z = features.shape
    extended = padded(features, (("gx", 1), ("gy", 2), ("gz", 3)), 1)
    tap_maps = jnp.dot(weight, extended.reshape(channels, -1), preferred_element_type=jnp.float32)
    tap_maps = tap_maps.reshape(27, cells_x + 2, cells_y + 2, cells_z + 2)
    logits = jnp.zeros((cells_x, cells_y, cells_z), jnp.float32) + bias[0]
    for index, offset in enumerate(tap_offsets()):
        logits = (
            logits
            + tap_maps[
                index,
                1 + offset[0] : 1 + offset[0] + cells_x,
                1 + offset[1] : 1 + offset[1] + cells_y,
                1 + offset[2] : 1 + offset[2] + cells_z,
            ]
        )
    predict = jax.nn.sigmoid(logits)
    target = label.astype(jnp.float32)
    fields = jnp.stack([predict, target])
    inside, box_count, cross_count = grid_counts(cells_x, cells_y, cells_z, 0)

    def pred_part(record):
        return tuple((member[0] for member in record))

    eroded, skeleton, first_full = section(
        fields, cross_remote, box_remote, inside, box_count, cross_count
    )
    first_record = pred_part(first_full)

    def forward_step(carry, unused):
        current, skel_prev = carry
        eroded_next, thinned, record = section(
            current, cross_remote, box_remote, inside, box_count, cross_count
        )
        lift_scaled = sharpness * (thinned - skel_prev * thinned)
        skel_next = skel_prev + jax.nn.softplus(lift_scaled) / sharpness
        extras = (skel_prev[0], jax.nn.sigmoid(lift_scaled[0]))
        return ((eroded_next, skel_next), (pred_part(record), extras))

    (eroded, skeleton), (later_records, later_extras) = lax.scan(
        forward_step, (eroded, skeleton), None, length=ITERS
    )
    pred_skel = skeleton[0]
    target_skel = skeleton[1]
    local_totals = jnp.stack(
        [
            jnp.sum(pred_skel * target),
            jnp.sum(pred_skel),
            jnp.sum(target_skel * predict),
            jnp.sum(target_skel),
            jnp.sum(predict * target),
            jnp.sum(predict),
            jnp.sum(target),
        ]
    )
    totals = global_stats(local_totals)
    loss_grads = jax.grad(loss_from)(totals)
    cotangent = (loss_grads[0] * target + loss_grads[1])[None]
    grad_skel = skeleton_backward(cotangent, first_record, later_records, later_extras)[0]
    grad_predict = grad_skel + loss_grads[2] * target_skel + loss_grads[4] * target + loss_grads[5]
    grad_logits = grad_predict * predict * (1.0 - predict)
    grad_extended = padded(grad_logits, (("gx", 0), ("gy", 1), ("gz", 2)), 1)
    moved = jnp.stack(
        [
            grad_extended[
                1 - offset[0] : 1 - offset[0] + cells_x,
                1 - offset[1] : 1 - offset[1] + cells_y,
                1 - offset[2] : 1 - offset[2] + cells_z,
            ]
            for offset in tap_offsets()
        ]
    )
    moved = moved.reshape(27, -1)
    flat = features.reshape(channels, -1)
    weight_local = jnp.dot(
        moved, flat.T, precision=lax.Precision.HIGHEST, preferred_element_type=jnp.float32
    )
    bias_local = jnp.sum(grad_logits).reshape(1)
    grad_weight, grad_bias = lax.psum((weight_local, bias_local), ("gx", "gy", "gz"))
    grad_features = jnp.dot(
        weight.T.astype(jnp.float32),
        moved,
        precision=lax.Precision.HIGHEST,
        preferred_element_type=jnp.float32,
    )
    grad_features = grad_features.reshape(channels, cells_x, cells_y, cells_z).astype(jnp.bfloat16)
    return (loss_from(totals).reshape(1), grad_features, grad_weight, grad_bias)


def solution(mesh):
    in_specs = (P(None, "gx", "gy", "gz"), P(), P(), P("gx", "gy", "gz"))
    out_specs = (P(), P(None, "gx", "gy", "gz"), P(), P())
    return jax.shard_map(
        per_device, mesh=mesh, in_specs=in_specs, out_specs=out_specs, check_vma=False
    )
```

profile of v0, /device:TPU:0, one launch (start us, length us, event | category | flops | bytes accessed | tf_op | source)
XLA Modules:
  0.0 1476.0 jit_solution(10644458822682034129)
XLA Ops:
  16.6 4.6 collective-permute-done.27
  47.4 6.0 pad_maximum_fusion.52
  53.4 6.2 copy.69
  59.6 7.6 reshape.322
  70.3 9.5 reshape.323
  98.2 4.6 collective-permute-start.35
  102.9 8.7 collective-permute-done.34
  144.7 575.0 %while.50 = (s32[]{:T(128)}, f32[2,16,16,128]{3,2,1,0:T(8,128)S(1)}, f32[2,16,16,128]{3,2,1,0:T(8,128)S(1)}, f32[10,16,16,128]{3,2,1,0:T(8,128)}, f32[10,16,16,1...) while((s32[]{:T(128)}, ...), condition=%wide.region_1.2_spmd.clone.clone, body=%wide.region_0.1_spmd.clone.clone.sunk | while | flops 7481314 | bytes 12865269 | solution.py:165
  162.6 8.1 collective-permute-done.16
  189.3 4.6 collective-permute-start.23
  219.2 8.5 collective-permute-done.16
  246.3 4.6 collective-permute-start.23
  276.3 8.8 collective-permute-done.16
  334.1 8.8 collective-permute-done.16
  361.5 4.6 collective-permute-start.23
  391.9 8.8 collective-permute-done.16
  419.3 4.6 collective-permute-start.23
  449.6 8.8 collective-permute-done.16
  477.0 4.6 collective-permute-start.23
  507.4 8.8 collective-permute-done.16
  565.1 8.8 collective-permute-done.16
  622.9 8.8 collective-permute-done.16
  650.3 4.6 collective-permute-start.23
  680.7 8.8 collective-permute-done.16
  727.9 42.7 %psum.21 = f32[7]{0:T(128)S(1)} all-reduce(f32[7]{0:T(128)S(1)} %stack.180), channel_id=1, replica_groups=mesh['gx'=4,'gy'=2,'gz'=4] {'gx','gy','gz'}, use_global_device_ids=true, to_apply=%region_9.10 | all-reduce | flops 7 | bytes 56 | tf_op jit(solution)/shard_map/psum | solution.py:115
  778.1 523.2 %while.49 = (s32[]{:T(128)}, f32[1,16,16,128]{3,2,1,0:T(8,128)S(1)}, f32[1,16,16,128]{3,2,1,0:T(8,128)S(1)}, f32[10,16,16,128]{3,2,1,0:T(8,128)}, f32[10,16,16,1...) while((s32[]{:T(128)}, ...), condition=%wide.region_11.12_spmd.clone, body=%wide.region_10.11_spmd.clone.sunk | while | flops 2724852 | bytes 5006071 | solution.py:108
  824.1 4.7 collective-permute-done.11
  875.0 4.7 collective-permute-done.11
  934.4 4.8 collective-permute-start.1
  958.3 5.0 collective-permute-start.7
  987.2 4.8 collective-permute-start.1
  1011.1 5.0 collective-permute-start.7
  1040.0 4.8 collective-permute-start.1
  1063.9 5.0 collective-permute-start.7
  1092.8 4.8 collective-permute-start.1
  1116.7 5.0 collective-permute-start.7
  1145.6 4.8 collective-permute-start.1
  1169.5 5.0 collective-permute-start.7
  1198.4 4.8 collective-permute-start.1
  1222.3 5.0 collective-permute-start.7
  1251.2 4.8 collective-permute-start.1
  1275.1 5.0 collective-permute-start.7
  1307.1 6.1 collective-permute-done.43
  1378.3 5.0 collective-permute-start.59
  1391.5 15.0 %stack.236 = f32[27,16,16,128]{3,0,2,1:T(8,128)} concatenate(f32[1,16,16,128]{3,0,2,1:T(1,128)} %bitcast.284, f32[1,16,16,128]{3,0,2,1:T(1,128)} %bitcast.296, f32[1,16,16,128]{3,0,2,1:T(1,128)} %bitcast.266, f32[1,16,16,128]{3,0,2,1:T(1,128)} %bitcast.282, f32[1,16,16,128]{3,0,2,1:T(1,128)S(1)} %bitcast.248, f32[1,16,16,128]{3,0,2,1:T(1,128)S(1)} %bitcast.264, ...), dimensions={0} | concatenate | bytes 7077888 | tf_op jit(solution)/shard_map/stack | solution.py:188
  1406.4 6.3 convolution_bitcast_fusion.1
  1412.8 14.5 stack.208
  1433.5 40.9 %all-reduce.7 = (f32[27,32]{1,0:T(8,128)}, f32[1]{0:T(128)}) all-reduce(f32[27,32]{1,0:T(8,128)S(1)} %copy-done.4, f32[1]{0:T(128)} %bitcast.127), channel_id=1, replica_groups=mesh['gx'=4,'gy'=2,'gz'=4] {'gx','gy','gz'}, use_global_device_ids=true, to_apply=%region_12.13 | all-reduce | flops 865 | bytes 6920 | tf_op jit(solution)/shard_map/psum | solution.py:204
  (967 shorter events, 1092.9 us)
Async XLA Ops:
  29.0 9.6 collective-permute-start.28
  96.9 14.7 collective-permute-start.34
  98.2 15.1 %collective-permute-start.35 = (f32[2,18,18,1]{3,2,1,0:T(8,128)S(1)}, f32[2,18,18,1]{3,2,1,0:T(8,128)S(1)}, u32[]{:S(2)}, u32[]{:S(2)}) collective-permute-start(f32[2,18,18,1]{3,2,1,0:T(8,128)S(1)} %get-tuple-element.676), channel_id=1, source_target_pairs={{0,1},{1,2},{2,3},{4,5},{5,6},{6,7},{8,9},{9,10},{10,11},{12,13},{... | collective-permute-start | bytes 7784 | tf_op jit(solution)/shard_map/ppermute | solution.py:18
  129.4 10.2 collective-permute-start.40
  133.8 9.9 collective-permute-start.41
  157.6 13.0 collective-permute-start.16
  161.1 13.7 collective-permute-start.17
  213.3 14.3 collective-permute-start.16
  217.7 14.1 collective-permute-start.17
  270.4 14.7 collective-permute-start.16
  274.9 14.4 collective-permute-start.17
  302.4 8.9 collective-permute-start.22
  303.7 8.7 collective-permute-start.23
  328.2 14.7 collective-permute-start.16
  332.6 14.4 collective-permute-start.17
  360.2 8.9 collective-permute-start.22
  361.5 8.7 collective-permute-start.23
  386.0 14.7 collective-permute-start.16
  390.4 14.4 collective-permute-start.17
  418.0 8.9 collective-permute-start.22
  419.3 8.7 collective-permute-start.23
  443.8 14.7 collective-permute-start.16
  448.2 14.4 collective-permute-start.17
  475.7 8.9 collective-permute-start.22
  477.0 8.7 collective-permute-start.23
  501.5 14.7 collective-permute-start.16
  506.0 14.4 collective-permute-start.17
  533.5 8.9 collective-permute-start.22
  534.8 8.7 collective-permute-start.23
  559.3 14.7 collective-permute-start.16
  563.7 14.4 collective-permute-start.17
  591.3 8.9 collective-permute-start.22
  592.6 8.7 collective-permute-start.23
  617.1 14.7 collective-permute-start.16
  621.5 14.4 collective-permute-start.17
  649.0 8.9 collective-permute-start.22
  650.3 8.7 collective-permute-start.23
  674.9 14.7 collective-permute-start.16
  679.3 14.4 collective-permute-start.17
  706.8 8.9 collective-permute-start.22
  708.1 8.7 collective-permute-start.23
  814.7 9.4 collective-permute-start.10
  819.1 9.6 collective-permute-start.11
  871.0 8.7 collective-permute-start.11
  1346.3 9.1 collective-permute-start.52
  1347.6 9.0 collective-permute-start.53
  1377.0 10.4 collective-permute-start.58
  1378.3 10.8 collective-permute-start.59
  (233 other events, 2004.3 us)
where the time goes:
time: 1490 us; the launch traced here: 1480 us
  starting transfers between devices  752 us (50%)
  waiting for transfers between devices  407 us (27%)
  local copies, waits for them, and re-layouts  107 us (7%)
  other arithmetic  100 us (7%)
  blocking collectives  83.5 us (6%)
    ppermute x138, starting transfers between devices, padded(): lax.ppermute(lax.slice_in_dim(block, block.shape[dim] - width, None, axis...  573 us
    ppermute x138, waiting for transfers between devices, padded(): lax.ppermute(lax.slice_in_dim(block, block.shape[dim] - width, None, axis...  235 us
    ppermute x138, starting transfers between devices, padded(): lax.ppermute(lax.slice_in_dim(block, 0, width, axis=dim), axis, backward)  179 us
    ppermute x138, waiting for transfers between devices, padded(): lax.ppermute(lax.slice_in_dim(block, 0, width, axis=dim), axis, backward)  172 us
    psum x1, blocking collectives, global_stats(): return lax.psum(local_totals, ('gx', 'gy', 'gz'))  42.7 us
    psum x1, blocking collectives, per_device(): lax.psum((weight_local, bias_local), ('gx', 'gy', 'gz'))  40.9 us
  transfers between devices with their start and end apart: 276, of which 185 were waited for; matrix products, arithmetic and copies ran while one was open for 2% of the time, Pallas kernels for 0%

commit v1 on v0

v1 whole, which is shorter than its diff:
```python
import functools

import jax
import jax.numpy as jnp
from jax import lax
from jax.experimental import pallas as pl
from jax.experimental.pallas import tpu as pltpu
from jax.sharding import PartitionSpec as P

ITERS = 10
SECTIONS = ITERS + 1
LANES = 128
REACH = SECTIONS + 2
HALO = 2 * SECTIONS + 3

temper = 20.0
sharpness = 40.0

GROUP = ("gx", "gy")
ALL_AXES = ("gx", "gy", "gz")
f32 = jnp.float32
bf16 = jnp.bfloat16


def up8(value):
    return -(-value // 8) * 8


class Plan:
    def __init__(self, mesh_shape, block):
        self.ch, self.nx, self.ny, self.nz = block
        self.gx, self.gy, self.gz = (mesh_shape[a] for a in ALL_AXES)
        self.members = self.gx * self.gy
        self.ranks = self.members * self.gz
        self.X = self.nx * self.gx
        self.Y = self.ny * self.gy
        self.Z = self.nz * self.gz
        assert LANES % self.Y == 0 and self.nz == LANES
        assert self.nz % self.members == 0
        self.zc = self.nz // self.members
        self.per = LANES // self.Y
        assert self.nx % self.per == 0
        self.tiles = self.X // self.per
        self.own = self.nx // self.per
        self.shared = self.per > 1
        self.sent = self.own + (1 if self.shared else 2)
        self.R = up8(self.zc + 2)
        self.base = 8 + up8(HALO)
        self.top = self.base + up8(self.zc + HALO)
        self.rows = self.top + 8
        self.lo = self.base - up8(REACH)
        self.hi = self.base + up8(self.zc + REACH)
        self.win = self.hi - self.lo
        self.at = self.base - self.lo
        self.tlo = self.base - 8
        self.thi = self.base + up8(self.zc + 1)
        self.hops = -(-HALO // self.zc)
        self.label_hops = -(-REACH // self.zc)

    def slot(self, x):
        if 0 <= x < self.nx:
            return x // self.per, (x % self.per) * self.Y
        if x == self.nx:
            return self.own, 0
        return self.sent - 1, LANES - self.Y


def lane_iota(shape):
    return lax.broadcasted_iota(jnp.int32, shape, len(shape) - 1)


def row_iota(shape):
    return lax.broadcasted_iota(jnp.int32, shape, len(shape) - 2)


def x_shift(plan, prev, cur, nxt):
    if plan.Y == LANES:
        return prev, nxt
    lane = lane_iota(cur.shape)
    lower = pltpu.roll(jnp.where(lane >= LANES - plan.Y, prev, cur), plan.Y, 1)
    upper = pltpu.roll(jnp.where(lane < plan.Y, nxt, cur), LANES - plan.Y, 1)
    return lower, upper


def y_shift(plan, cur):
    spot = lane_iota(cur.shape) % plan.Y
    lower = jnp.where(spot == 0, 0.0, pltpu.roll(cur, 1, 1))
    upper = jnp.where(spot == plan.Y - 1, 0.0, pltpu.roll(cur, LANES - 1, 1))
    return lower, upper


def cross_at(plan, load, tile, lo, hi):
    cur = load(tile, lo, hi)
    x_lower, x_upper = x_shift(plan, load(tile - 1, lo, hi), cur, load(tile + 1, lo, hi))
    y_lower, y_upper = y_shift(plan, cur)
    total = cur + load(tile, lo - 1, hi - 1) + load(tile, lo + 1, hi + 1)
    return total + x_lower + x_upper + y_lower + y_upper


def plane_sum(plan, ref, lo, hi):
    part = ref[lo - 1 : hi - 1] + ref[lo:hi] + ref[lo + 1 : hi + 1]
    lower, upper = y_shift(plan, part)
    return part + lower + upper


def x_sum(plan, ref, tile):
    cur = ref[tile]
    lower, upper = x_shift(plan, ref[tile - 1], cur, ref[tile + 1])
    return cur + lower + upper


def counts(plan, rank, tile, lo, hi):
    shape = (hi - lo, LANES)
    z = rank * plan.zc + row_iota(shape) + (lo - plan.base)
    flat = tile * LANES + lane_iota(shape)
    y = flat % plan.Y
    x = flat // plan.Y

    def along(spot, size):
        return 3.0 - (spot == 0).astype(f32) - (spot == size - 1).astype(f32)

    inside = ((z >= 0) & (z < plan.Z)).astype(f32)
    return along(x, plan.X), along(y, plan.Y), along(z, plan.Z), inside


def cross_inverse(plan, rank, tile, lo, hi):
    cx, cy, cz, inside = counts(plan, rank, tile, lo, hi)
    return inside / (cx + cy + cz - 2.0)


def box_inverse(plan, rank, tile, lo, hi):
    cx, cy, cz, inside = counts(plan, rank, tile, lo, hi)
    return inside / (cx * cy * cz)


def tap_condition(plan, member_y, shape, y_dim, in_dim):
    y = lax.broadcasted_iota(jnp.int32, shape, y_dim) % plan.Y
    own = lax.broadcasted_iota(jnp.int32, shape, in_dim) % plan.ny
    return own + member_y * plan.ny - y + 1


def conv_kernel(plan, pos_ref, w_ref, f_ref, out_ref, wide_ref, acc_ref):
    rows, inner = plan.Y, plan.ch * plan.ny
    spread = (
        lax.broadcasted_iota(jnp.int32, (plan.ch, inner), 0)
        == lax.broadcasted_iota(jnp.int32, (plan.ch, inner), 1) // plan.ny
    ).astype(f32)
    taps = jnp.dot(w_ref[...].astype(f32), spread, preferred_element_type=f32)
    tap_y = tap_condition(plan, pos_ref[1], (rows, inner), 0, 1)
    for i in range(3):
        for k in range(3):
            band = jnp.zeros((rows, inner), f32)
            for j in range(3):
                t = 9 * i + 3 * j + k
                band = jnp.where(tap_y == j, taps[t : t + 1], band)
            at = (3 * i + k) * rows
            wide_ref[at : at + rows] = band.astype(bf16)
    acc_ref[...] = jnp.zeros_like(acc_ref)

    def at_x(x, carry):
        block = f_ref[:, x].reshape(inner, plan.nz)
        out = jnp.dot(wide_ref[...], block, preferred_element_type=f32)
        for i in range(3):
            acc_ref[x + 2 - i] += out[3 * i * rows : 3 * (i + 1) * rows]
        return carry

    lax.fori_loop(0, plan.nx, at_x, 0)

    out_ref[...] = jnp.zeros_like(out_ref)
    places = {}
    for x in range(-1, plan.nx + 1):
        tile, lane = plan.slot(x)
        places.setdefault(tile, {})[lane] = x
    lane = lane_iota((rows, plan.nz))
    for tile in range(plan.sent):
        parts, spills = [], []
        for first in range(0, LANES, rows):
            x = places[tile].get(first)
            if x is None:
                parts.append(jnp.zeros((rows, plan.nz), f32))
                spills.append(jnp.zeros((rows, plan.nz), f32))
                continue
            low = acc_ref[x + 1, 0:rows]
            mid = acc_ref[x + 1, rows : 2 * rows]
            high = acc_ref[x + 1, 2 * rows : 3 * rows]
            total = mid + jnp.where(lane == 0, 0.0, pltpu.roll(low, 1, 1))
            total = total + jnp.where(lane == plan.nz - 1, 0.0, pltpu.roll(high, plan.nz - 1, 1))
            parts.append(total)
            spill = jnp.where(lane == 1, pltpu.roll(low, 2, 1), 0.0)
            spills.append(jnp.where(lane == 0, high, spill))
        turned = jnp.concatenate(parts, axis=0).T
        spill = jnp.concatenate(spills, axis=0).T
        for p in range(plan.members):
            out_ref[p, tile, 0 : plan.zc] = turned[p * plan.zc : (p + 1) * plan.zc]
        out_ref[0, tile, plan.zc : plan.zc + 1] = spill[0:1]
        out_ref[plan.members - 1, tile, plan.zc + 1 : plan.zc + 2] = spill[1:2]


def label_kernel(plan, pos_ref, l_ref, out_ref):
    rows = plan.Y
    sub = lax.broadcasted_iota(jnp.int32, (plan.gy, plan.ny, plan.nz), 0)
    for tile in range(plan.own):
        parts = []
        for n in range(plan.per):
            block = l_ref[tile * plan.per + n].astype(f32)[None]
            wide = jnp.where(sub == pos_ref[1], block, 0.0)
            parts.append(wide.reshape(rows, plan.nz))
        turned = jnp.concatenate(parts, axis=0).T
        for p in range(plan.members):
            out_ref[p, tile] = turned[p * plan.zc : (p + 1) * plan.zc].astype(bf16)


def gather_kernel(plan, got_ref, out_ref):
    lane = lane_iota((plan.R, LANES))
    out_ref[...] = jnp.zeros_like(out_ref)
    for a in range(plan.gx):
        for b in range(plan.gy):
            p = a * plan.gy + b
            for q in range(plan.own):
                out_ref[a * plan.own + q] += got_ref[p, q]
            if a > 0:
                out_ref[a * plan.own - 1] += jnp.where(
                    lane >= LANES - plan.Y, got_ref[p, plan.sent - 1], 0.0
                )
            if a < plan.gx - 1:
                out_ref[(a + 1) * plan.own] += jnp.where(lane < plan.Y, got_ref[p, plan.own], 0.0)


def label_gather_kernel(plan, got_ref, out_ref):
    for a in range(plan.gx):
        for q in range(plan.own):
            total = got_ref[a * plan.gy, q].astype(f32)
            for b in range(1, plan.gy):
                total = total + got_ref[a * plan.gy + b, q].astype(f32)
            out_ref[a * plan.own + q] = total.astype(bf16)


def erode(plan, load, store, g_ref, zy_ref, tile, inverse, first, last, wlo, whi):
    nxt = cross_at(plan, load, tile + 1, first, last) * inverse
    store(nxt)
    g_ref[first:last] = jnp.where(nxt > 0.0, 1.0 / nxt, 0.0)
    zy_ref[tile + 1] = plane_sum(plan, g_ref, wlo, whi)


def thin(e, box, inverse, s):
    ok = (e > 0.0) & (box > 0.0) & (inverse > 0.0)
    ratio = jnp.where(ok, e * box * inverse, 1.0)
    square = ratio * ratio
    slope = 1.0 / (1.0 + square)
    scaled = -jnp.log(square * slope)
    lift = scaled * (1.0 - s)
    small = jnp.exp(-jnp.abs(lift))
    part = 1.0 / (1.0 + small)
    rate = jnp.where(lift >= 0.0, part, small * part)
    grown = s + (jnp.maximum(lift, 0.0) - jnp.log(part)) * (1.0 / sharpness)
    thinned = scaled * (1.0 / sharpness)
    return ok, slope, rate, thinned, grown


def target_kernel(plan, *refs):
    hops = plan.label_hops
    pos_ref, own_ref = refs[:2]
    below, above = refs[2 : 2 + hops], refs[2 + hops : 2 + 2 * hops]
    target_ref, ts_ref = refs[2 + 2 * hops : 4 + 2 * hops]
    e_ref, inv7_ref, g_ref, zy_ref = refs[4 + 2 * hops :]
    lo, hi, win = plan.lo, plan.hi, plan.win
    wlo, whi = plan.tlo - lo + 8, plan.thi - lo + 8
    rank = pos_ref[0]
    e_ref[...] = jnp.zeros_like(e_ref)
    zy_ref[...] = jnp.zeros_like(zy_ref)
    g_ref[...] = jnp.zeros_like(g_ref)
    ts_ref[...] = jnp.zeros_like(ts_ref)
    target_ref[...] = jnp.zeros_like(target_ref)

    def fill(tile, carry):
        chunks = {0: own_ref}
        for h in range(1, hops + 1):
            chunks[-h] = below[h - 1]
            chunks[h] = above[h - 1]
        for h, ref in chunks.items():
            at = plan.at + h * plan.zc
            first, last = max(at, 0), min(at + plan.zc, win)
            if first < last:
                piece = ref[tile].astype(f32)
                target_ref[tile, first:last] = piece[first - at : last - at]
        cx, cy, cz, inside = counts(plan, rank, tile, lo, hi)
        e_ref[0, tile + 1, 8 : 8 + win] = jnp.exp(-temper * target_ref[tile]) * inside
        inv7_ref[tile] = inside / (cx + cy + cz - 2.0)
        return carry

    lax.fori_loop(0, plan.tiles, fill, 0)

    def section(step, carry):
        now = step % 2

        def first_pass(tile, carry):
            def load(n, a, b):
                return e_ref[now, n, a:b]

            def store(value):
                e_ref[1 - now, tile + 1, 8 : 8 + win] = value

            erode(plan, load, store, g_ref, zy_ref, tile, inv7_ref[tile], 8, 8 + win, wlo, whi)
            return carry

        lax.fori_loop(0, plan.tiles, first_pass, 0)

        def second_pass(tile, carry):
            box = x_sum(plan, zy_ref, tile + 1)
            inverse = box_inverse(plan, rank, tile, plan.tlo, plan.thi)
            s = ts_ref[tile]
            _, _, _, thinned, grown = thin(e_ref[now, tile + 1, wlo:whi], box, inverse, s)
            ts_ref[tile] = jnp.where(step == 0, thinned, grown)
            return carry

        lax.fori_loop(0, plan.tiles, second_pass, 0)
        return carry

    lax.fori_loop(0, SECTIONS, section, 0)


def forward_kernel(plan, *refs):
    hops = plan.hops
    pos_ref, bias_ref, target_ref, ts_ref, own_ref = refs[:5]
    refs = refs[5:]
    below, above = refs[:hops], refs[hops : 2 * hops]
    refs = refs[2 * hops :]
    m_ref, q_ref, t_ref, g2_ref, p_ref, sums_ref = refs[:6]
    e_ref, inv7_ref, inv27_ref, g_ref, zy_ref, s_ref = refs[6:]
    base, top, lo, hi, zc = plan.base, plan.top, plan.lo, plan.hi, plan.zc
    rank = pos_ref[0]
    step = pl.program_id(0)
    tiles = plan.tiles

    @pl.when(step == 0)
    def _():
        e_ref[...] = jnp.zeros_like(e_ref)
        zy_ref[...] = jnp.zeros_like(zy_ref)
        g_ref[...] = jnp.zeros_like(g_ref)
        s_ref[...] = jnp.zeros_like(s_ref)

        def fill(tile, carry):
            chunks = {0: own_ref}
            for h in range(1, hops + 1):
                chunks[-h] = below[h - 1]
                chunks[h] = above[h - 1]
            u = e_ref.at[0, tile + 1]
            for h, ref in chunks.items():
                at = base + h * zc
                first, last = max(at, 8), min(at + zc, top)
                if first < last:
                    u[first:last] = ref[tile, first - at : last - at]
            for h, ref in chunks.items():
                at = base + h * zc
                if 8 <= at - 1 < top:
                    u[at - 1 : at] += ref[tile, zc : zc + 1]
                if 8 <= at + zc < top:
                    u[at + zc : at + zc + 1] += ref[tile, zc + 1 : zc + 2]
            logits = u[8:top] + bias_ref[0]
            small = jnp.exp(-jnp.abs(logits))
            part = 1.0 / (1.0 + small)
            predict = jnp.where(logits >= 0, part, small * part)
            cx, cy, cz, inside = counts(plan, rank, tile, 8, top)
            u[8:top] = jnp.exp(-temper * predict) * inside
            inv7_ref[tile] = inside / (cx + cy + cz - 2.0)
            inv27_ref[tile] = (inside / (cx * cy * cz))[lo - 8 : hi - 8]
            p_ref[tile] = predict[plan.tlo - 8 : plan.thi - 8]
            return carry

        lax.fori_loop(0, tiles, fill, 0)

    now = step % 2

    def first_pass(tile, carry):
        def load(n, a, b):
            return e_ref[now, n, a:b]

        def store(value):
            e_ref[1 - now, tile + 1, 8:top] = value

        erode(plan, load, store, g_ref, zy_ref, tile, inv7_ref[tile], 8, top, lo, hi)
        grown = g_ref[lo:hi]
        g2_ref[0, tile] = grown * grown
        return carry

    lax.fori_loop(0, tiles, first_pass, 0)
    opening = step == 0

    def second_pass(tile, carry):
        e = e_ref[now, tile + 1, lo:hi]
        box = x_sum(plan, zy_ref, tile + 1)
        s = s_ref[tile]
        ok, slope, rate, thinned, grown = thin(e, box, inv27_ref[tile], s)
        s_ref[tile] = jnp.where(opening, thinned, grown)
        a = jnp.where(opening, slope, rate * (1.0 - s) * slope)
        m_ref[0, tile] = 1.0 - rate * thinned
        q_ref[0, tile] = jnp.where(ok, a / box, 0.0)
        t_ref[0, tile] = jnp.where(ok, a / e, 0.0)
        return carry

    lax.fori_loop(0, tiles, second_pass, 0)

    @pl.when(step == SECTIONS - 1)
    def _():
        at = plan.at
        span = up8(zc)
        mine = row_iota((span, LANES)) < zc

        def add(tile, totals):
            def own(value):
                return jnp.where(mine, value, 0.0)

            ps = own(s_ref[tile, at : at + span])
            ts = own(ts_ref[tile, 8 : 8 + span])
            predict = own(p_ref[tile, 8 : 8 + span])
            target = own(target_ref[tile, at : at + span])
            terms = (ps * target, ps, ts * predict, ts, predict * target, predict, target)
            return tuple(
                total + jnp.sum(term.reshape(-1, 8, LANES), axis=0)
                for total, term in zip(totals, terms)
            )

        totals = lax.fori_loop(0, tiles, add, (jnp.zeros((8, LANES), f32),) * 7)
        lines = [jnp.sum(total, axis=0, keepdims=True) for total in totals]
        lines.append(jnp.zeros((1, LANES), f32))
        sums_ref[...] = jnp.broadcast_to(
            jnp.concatenate(lines, axis=0)[None], (plan.ranks, 8, LANES)
        )


def backward_kernel(plan, *refs):
    (
        pos_ref, sums_ref, m_ref, q_ref, t_ref, g2_ref, p_ref, target_ref, ts_ref,
        out_ref, loss_ref,
        w_ref, h_ref, push_ref, zy_ref, pull_ref, inv7_ref, grad_ref,
    ) = refs
    step = pl.program_id(0)
    rank = pos_ref[0]
    win, lo, hi, zc, at = plan.win, plan.lo, plan.hi, plan.zc, plan.at
    tiles = plan.tiles

    lines = jnp.sum(jnp.sum(sums_ref[...], axis=0), axis=1, keepdims=True)
    s1, s2, s3, s4, s5, s6, s7 = (lines[n : n + 1] for n in range(7))
    prec = (s1 + 1.0) / (s2 + 1.0)
    sens = (s3 + 1.0) / (s4 + 1.0)

    @pl.when(step == 0)
    def _():
        zy_ref[...] = jnp.zeros_like(zy_ref)
        pull_ref[...] = jnp.zeros_like(pull_ref)
        push_ref[...] = jnp.zeros_like(push_ref)
        h_ref[...] = jnp.zeros_like(h_ref)

        def fill(tile, carry):
            w_ref[tile] = target_ref[tile] - prec
            inv7_ref[tile] = cross_inverse(plan, rank, tile, lo, hi)
            return carry

        lax.fori_loop(0, tiles, fill, 0)

    def first_pass(tile, carry):
        push_ref[8 : 8 + win] = w_ref[tile] * q_ref[0, tile]
        zy_ref[tile + 1] = plane_sum(plan, push_ref, 8, 8 + win)
        return carry

    lax.fori_loop(0, tiles, first_pass, 0)

    def second_pass(tile, carry):
        box = x_sum(plan, zy_ref, tile + 1)
        pull_ref[tile + 1, 8 : 8 + win] = (h_ref[tile] - g2_ref[0, tile] * box) * inv7_ref[tile]
        return carry

    lax.fori_loop(0, tiles, second_pass, 0)

    def third_pass(tile, carry):
        def load(n, a, b):
            return pull_ref[n, a:b]

        w = w_ref[tile]
        h_ref[tile] = w * t_ref[0, tile] + cross_at(plan, load, tile + 1, 8, 8 + win)
        w_ref[tile] = w * m_ref[0, tile]
        return carry

    lax.fori_loop(0, tiles, third_pass, 0)

    @pl.when(step == SECTIONS - 1)
    def _():
        both = prec + sens
        volume = s6 + s7 + 1.0
        cl_loss = 1.0 - 2.0 * prec * sens / both
        dice_loss = 1.0 - (2.0 * s5 + 1.0) / volume
        loss_ref[...] = jnp.broadcast_to(0.5 * dice_loss + 0.5 * cl_loss, (8, LANES))
        l0 = -(sens / both) * (sens / both) / (s2 + 1.0)
        l2 = -(prec / both) * (prec / both) / (s4 + 1.0)
        l4 = -1.0 / volume
        l5 = 0.5 * (2.0 * s5 + 1.0) / (volume * volume)
        grad_ref[...] = jnp.zeros_like(grad_ref)
        span = plan.thi - plan.tlo
        first = plan.tlo - lo

        def finish(tile, carry):
            z = rank * zc + row_iota((span, LANES)) + (plan.tlo - plan.base)
            inside = (z >= 0) & (z < plan.Z)
            rows = slice(first, first + span)
            predict = p_ref[tile]
            skel = l0 * jnp.exp(-temper * predict) * h_ref[tile, rows]
            whole = skel + l2 * ts_ref[tile] + l4 * target_ref[tile, rows] + l5
            grad = jnp.where(inside, whole * predict * (1.0 - predict), 0.0)
            grad_ref[tile + 1, 0:zc] = grad[8 : 8 + zc]
            grad_ref[tile + 1, zc : zc + 1] = grad[7:8]
            grad_ref[tile + 1, zc + 1 : zc + 2] = grad[8 + zc : 9 + zc]
            return carry

        lax.fori_loop(0, tiles, finish, 0)
        lane = lane_iota((plan.R, LANES))
        for a in range(plan.gx):
            pieces = [grad_ref[a * plan.own + q + 1] for q in range(plan.own)]
            after = grad_ref[(a + 1) * plan.own + 1]
            before = grad_ref[a * plan.own]
            if plan.shared:
                edge = jnp.where(lane < plan.Y, after, 0.0)
                pieces.append(jnp.where(lane >= LANES - plan.Y, before, edge))
            else:
                pieces += [after, before]
            for q, piece in enumerate(pieces):
                for b in range(plan.gy):
                    out_ref[a * plan.gy + b, q] = piece


def grad_kernel(plan, pos_ref, wt_ref, f_ref, got_ref, gf_ref, gw_ref, wide_ref, g_ref, dw_ref):
    rows, inner, bands = plan.Y, plan.ch * plan.ny, 9 * plan.Y
    spread = (
        lax.broadcasted_iota(jnp.int32, (inner, plan.ch), 0) // plan.ny
        == lax.broadcasted_iota(jnp.int32, (inner, plan.ch), 1)
    ).astype(f32)
    tap_y = tap_condition(plan, pos_ref[1], (inner, bands), 1, 0)
    wide = jnp.zeros((inner, bands), f32)
    tap = lax.broadcasted_iota(jnp.int32, (27, bands), 0)
    band = lax.broadcasted_iota(jnp.int32, (27, bands), 1) // rows
    for j in range(3):
        pick = (tap == 9 * (band // 3) + 3 * j + band % 3).astype(f32)
        chosen = jnp.dot(wt_ref[...].astype(f32), pick, preferred_element_type=f32)
        full = jnp.dot(spread, chosen, preferred_element_type=f32)
        wide = jnp.where(tap_y == j, full, wide)
    wide_ref[...] = wide.astype(bf16)

    zc = plan.zc
    lane = lane_iota((rows, plan.nz))
    bias = jnp.zeros((rows, plan.nz), f32)
    places = {}
    for x in range(-1, plan.nx + 1):
        tile, first = plan.slot(x)
        places.setdefault(tile, {})[first] = x
    for tile in range(plan.sent):
        stack = [got_ref[p, tile, 0:zc] for p in range(plan.members)]
        turned = jnp.concatenate(stack, axis=0).T
        low = got_ref[0, tile, zc : zc + 1]
        high = got_ref[plan.members - 1, tile, zc + 1 : zc + 2]
        ends = jnp.concatenate([low, high, jnp.zeros((LANES - 2, LANES), f32)], axis=0).T
        for first, x in places[tile].items():
            g = turned[first : first + rows]
            end = ends[first : first + rows]
            down = jnp.where(lane == plan.nz - 1, pltpu.roll(end, plan.nz - 2, 1), pltpu.roll(g, plan.nz - 1, 1))
            up = jnp.where(lane == 0, end, pltpu.roll(g, 1, 1))
            g_ref[x + 1] = jnp.concatenate([down, g, up], axis=0).astype(bf16)
            if 0 <= x < plan.nx:
                bias = bias + g
    y_own = lax.broadcasted_iota(jnp.int32, (rows, plan.nz), 0) // plan.ny == pos_ref[1]
    bias = jnp.sum(jnp.where(y_own, bias, 0.0))

    dw_ref[...] = jnp.zeros_like(dw_ref)

    def at_x(x, carry):
        block = f_ref[:, x].reshape(inner, plan.nz)
        moved = jnp.concatenate([g_ref[x + 2], g_ref[x + 1], g_ref[x]], axis=0)
        out = jnp.dot(wide_ref[...], moved, preferred_element_type=f32)
        gf_ref[:, x] = out.astype(bf16).reshape(plan.ch, plan.ny, plan.nz)
        dw_ref[...] += lax.dot_general(
            moved, block, (((1,), (1,)), ((), ())), preferred_element_type=f32
        )
        return carry

    lax.fori_loop(0, plan.nx, at_x, 0)

    tap_y = tap_condition(plan, pos_ref[1], (rows, inner), 0, 1)
    taps = []
    for t in range(27):
        i, j, k = t // 9, t // 3 % 3, t % 3
        at = (3 * i + k) * rows
        taps.append(jnp.sum(jnp.where(tap_y == j, dw_ref[at : at + rows], 0.0), axis=0, keepdims=True))
    taps += [jnp.zeros((1, inner), f32)] * 5
    total = jnp.zeros((8, LANES), f32)
    for n in range(4):
        place = (
            lax.broadcasted_iota(jnp.int32, (inner, LANES), 0) // plan.ny + 32 * n
            == lax.broadcasted_iota(jnp.int32, (inner, LANES), 1)
        ).astype(f32)
        total = total + jnp.dot(
            jnp.concatenate(taps[8 * n : 8 * n + 8], axis=0),
            place,
            precision=lax.Precision.HIGHEST,
            preferred_element_type=f32,
        )
    spot = (row_iota((8, LANES)) == 3) & (lane_iota((8, LANES)) == 96)
    total = jnp.where(spot, bias, total)
    gw_ref[...] = jnp.broadcast_to(total[None], (plan.ranks, 8, LANES))


def final_kernel(plan, got_ref, gw_ref, gb_ref):
    total = jnp.sum(got_ref[...], axis=0)
    for n in range(4):
        count = min(8, 27 - 8 * n)
        gw_ref[8 * n : 8 * n + count] = total[:count, 32 * n : 32 * n + plan.ch]
    gb_ref[...] = total[3:4, 96:97]


VMEM = pl.BlockSpec(memory_space=pltpu.VMEM)
SMEM = pl.BlockSpec(memory_space=pltpu.SMEM)
BIG = pltpu.CompilerParams(vmem_limit_bytes=63 * 1024 * 1024)


def shape(dims, dtype=f32):
    return jax.ShapeDtypeStruct(dims, dtype)


def per_device(mesh_shape, features, weight, bias, label):
    plan = Plan(mesh_shape, features.shape)
    members, sent, own, R, tiles = plan.members, plan.sent, plan.own, plan.R, plan.tiles
    inner, bands = plan.ch * plan.ny, 9 * plan.Y
    place = (lax.axis_index("gz") * members + lax.axis_index(GROUP)).astype(jnp.int32)
    pos = jnp.stack([place, lax.axis_index("gy").astype(jnp.int32)])

    def call(kernel, out_shape, in_specs, scratch=(), params=BIG):
        return pl.pallas_call(
            functools.partial(kernel, plan),
            out_shape=out_shape,
            in_specs=in_specs,
            out_specs=jax.tree.map(lambda s: VMEM, out_shape),
            scratch_shapes=list(scratch),
            compiler_params=params,
        )

    def exchange(array):
        return lax.all_to_all(array, GROUP, 0, 0, tiled=True)

    def everywhere(array):
        return lax.all_to_all(array, ALL_AXES, 0, 0, tiled=True)

    def hop(array, distance):
        def device(r):
            return (r % members) * plan.gz + r // members

        pairs = [
            (device(r), device(r + distance))
            for r in range(plan.ranks)
            if 0 <= r + distance < plan.ranks
        ]
        return lax.ppermute(array, ALL_AXES, pairs)

    label_sent = call(label_kernel, shape((members, own, plan.zc, LANES), bf16), [SMEM, VMEM])(
        pos, label
    )
    sent_logits = call(
        conv_kernel,
        shape((members, sent, R, LANES)),
        [SMEM, VMEM, VMEM],
        [
            pltpu.VMEM((bands, inner), bf16),
            pltpu.VMEM((plan.nx + 2, 3 * plan.Y, plan.nz), f32),
        ],
    )(pos, weight, features)
    label_chunk = call(label_gather_kernel, shape((tiles, plan.zc, LANES), bf16), [VMEM])(
        exchange(label_sent)
    )
    chunk = call(gather_kernel, shape((tiles, R, LANES)), [VMEM])(exchange(sent_logits))
    below = [hop(chunk, h) for h in range(1, plan.hops + 1)]
    above = [hop(chunk, -h) for h in range(1, plan.hops + 1)]
    label_below = [hop(label_chunk, h) for h in range(1, plan.label_hops + 1)]
    label_above = [hop(label_chunk, -h) for h in range(1, plan.label_hops + 1)]

    window = (tiles, plan.win, LANES)
    tspan = plan.thi - plan.tlo
    target, ts = call(
        target_kernel,
        [shape(window), shape((tiles, tspan, LANES))],
        [SMEM] + [VMEM] * (1 + 2 * plan.label_hops),
        [
            pltpu.VMEM((2, tiles + 2, plan.win + 16, LANES), f32),
            pltpu.VMEM(window, f32),
            pltpu.VMEM((plan.win + 16, LANES), f32),
            pltpu.VMEM((tiles + 2, tspan, LANES), f32),
        ],
    )(pos, label_chunk, *label_below, *label_above)
    record = pl.BlockSpec((1,) + window, lambda n: (n, 0, 0, 0))
    outs = pl.pallas_call(
        functools.partial(forward_kernel, plan),
        grid=(SECTIONS,),
        out_shape=[shape((SECTIONS,) + window)] * 4
        + [shape((tiles, tspan, LANES)), shape((plan.ranks, 8, LANES))],
        in_specs=[SMEM, SMEM] + [VMEM] * (3 + 2 * plan.hops),
        out_specs=[record] * 4 + [VMEM] * 2,
        scratch_shapes=[
            pltpu.VMEM((2, tiles + 2, plan.rows, LANES), f32),
            pltpu.VMEM((tiles, plan.top - 8, LANES), f32),
            pltpu.VMEM(window, f32),
            pltpu.VMEM((plan.rows, LANES), f32),
            pltpu.VMEM((tiles + 2, plan.win, LANES), f32),
            pltpu.VMEM(window, f32),
        ],
        compiler_params=BIG,
    )(pos, bias, target, ts, chunk, *below, *above)
    m, q, t, g2, predict, sums = outs
    sums = everywhere(sums)

    back = pl.BlockSpec((1,) + window, lambda n: (SECTIONS - 1 - n, 0, 0, 0))
    grad_sent, loss = pl.pallas_call(
        functools.partial(backward_kernel, plan),
        grid=(SECTIONS,),
        out_shape=[shape((members, sent, R, LANES)), shape((8, LANES))],
        in_specs=[SMEM, VMEM] + [back] * 4 + [VMEM] * 3,
        out_specs=[VMEM, VMEM],
        scratch_shapes=[
            pltpu.VMEM(window, f32),
            pltpu.VMEM(window, f32),
            pltpu.VMEM((plan.win + 16, LANES), f32),
            pltpu.VMEM((tiles + 2, plan.win, LANES), f32),
            pltpu.VMEM((tiles + 2, plan.win + 16, LANES), f32),
            pltpu.VMEM(window, f32),
            pltpu.VMEM((tiles + 2, R, LANES), f32),
        ],
        compiler_params=BIG,
    )(pos, sums, m, q, t, g2, predict, target, ts)

    grad_features, partial = call(
        grad_kernel,
        [shape(features.shape, bf16), shape((plan.ranks, 8, LANES))],
        [SMEM, VMEM, VMEM, VMEM],
        [
            pltpu.VMEM((inner, bands), bf16),
            pltpu.VMEM((plan.nx + 2, 3 * plan.Y, plan.nz), bf16),
            pltpu.VMEM((bands, inner), f32),
        ],
    )(pos, weight.T, features, exchange(grad_sent))
    grad_weight, grad_bias = call(
        final_kernel, [shape((27, plan.ch)), shape((1, 1))], [VMEM]
    )(everywhere(partial))
    return (loss[0, :1], grad_features, grad_weight, grad_bias.reshape(1))


def solution(mesh):
    in_specs = (P(None, "gx", "gy", "gz"), P(), P(), P("gx", "gy", "gz"))
    out_specs = (P(), P(None, "gx", "gy", "gz"), P(), P())
    return jax.shard_map(
        functools.partial(per_device, dict(mesh.shape)),
        mesh=mesh,
        in_specs=in_specs,
        out_specs=out_specs,
        check_vma=False,
    )
```

time: 1490 us -> 280 us (0.19)
  starting transfers between devices: 752 us -> 28.6 us
  waiting for transfers between devices: 407 us -> 28 us
  Pallas kernels: 0 us -> 199 us
  local copies, waits for them, and re-layouts: 107 us -> 5.42 us
  other arithmetic: 100 us -> 0.6 us
  blocking collectives: 83.5 us -> 16.5 us
    ppermute x276 -> x6, starting transfers between devices: 752 us -> 14 us  [hop(): return lax.ppermute(array, ALL_AXES, pairs)]
    ppermute x276 -> x6, waiting for transfers between devices: 407 us -> 6.87 us  [hop(): return lax.ppermute(array, ALL_AXES, pairs)]
    pallas_call x0 -> x9, Pallas kernels: none -> 199 us  [the longest x1 63.5 us: per_device(): pl.pallas_call(functools.partial(forward_kernel, plan), grid=(SECTIONS,),...]
    psum x2 -> x0, blocking collectives: 83.5 us -> none  [the longest x1 42.7 us: global_stats(): return lax.psum(local_totals, ('gx', 'gy', 'gz'))]
    another operation x3 -> x0, local copies, waits for them, and re-layouts: 34 us -> none  [the longest x2 29.5 us: per_device(): jnp.stack([grad_extended[1 - offset[0]:1 - offset[0] + cells_x, 1 - offse...]
    convert_element_type x44 -> x0, other arithmetic: 25.4 us -> none  [the longest x11 13 us: back_section(): (-grad_open / box_sum).astype(jnp.bfloat16)]
    slice x101 -> x1, local copies, waits for them, and re-layouts: 23.7 us -> 1.2 us  [per_device(): return (loss[0, :1], grad_features, grad_weight, grad_bias.reshape(1))]
    all_to_all x0 -> x4, waiting for transfers between devices: none -> 21.1 us  [the longest x3 14.5 us: exchange(): return lax.all_to_all(array, GROUP, 0, 0, tiled=True)]
  transfers between devices with their start and end apart: 276 -> 10, of which waited for: 185 -> 5; matrix products, arithmetic and copies ran while one was open for 2% -> 1% of each run, Pallas kernels for 0% -> 22%
where the time goes in v1:
time: 280 us
  Pallas kernels  199 us (71%)
  starting transfers between devices  28.6 us (10%)
  waiting for transfers between devices  28 us (10%)
  blocking collectives  16.5 us (6%)
  local copies, waits for them, and re-layouts  5.42 us (2%)
    pallas_call x1, Pallas kernels, per_device(): pl.pallas_call(functools.partial(forward_kernel, plan), grid=(SECTIONS,),...  63.5 us
    pallas_call x1, Pallas kernels, per_device(): call(target_kernel, [shape(window), shape((tiles, tspan, LANES))], [SMEM]...  57.9 us
    pallas_call x1, Pallas kernels, per_device(): pl.pallas_call(functools.partial(backward_kernel, plan), grid=(SECTIONS,)...  54.7 us
    all_to_all x1, blocking collectives, everywhere(): return lax.all_to_all(array, ALL_AXES, 0, 0, tiled=True)  16.5 us
    all_to_all x3, waiting for transfers between devices, exchange(): return lax.all_to_all(array, GROUP, 0, 0, tiled=True)  14.5 us
    ppermute x6, starting transfers between devices, hop(): return lax.ppermute(array, ALL_AXES, pairs)  14 us
    all_to_all x3, starting transfers between devices, exchange(): return lax.all_to_all(array, GROUP, 0, 0, tiled=True)  12.1 us
    pallas_call x1, Pallas kernels, per_device(): call(grad_kernel, [shape(features.shape, bf16), shape((plan.ranks, 8, LAN...  9.33 us
  transfers between devices with their start and end apart: 10, of which 5 were waited for; matrix products, arithmetic and copies ran while one was open for 1% of the time, Pallas kernels for 22%

profile of v1, /device:TPU:0, one launch (start us, length us, event | category | flops | bytes accessed | tf_op | source)
XLA Modules:
  0.0 279.6 jit_solution(5324549053250793880)
XLA Ops:
  0.6 0.6 pad_add_fusion.pos_ref.refs_0_
  1.2 7.0 %shard_map.78 = f32[8,5,24,128]{3,2,1,0:T(8,128)} custom-call(s32[2]{0:T(128)} %pad_add_fusion.pos_ref.refs_0_, bf16[27,32]{1,0:T(8,128)(2,1)} %w_ref.1, bf16[32,16,16,128]{3,2,1,0:T(8,128)(2,1)} %f_ref.3), custom_call_target="tpu_custom_call" | custom-call | tf_op jit(solution)/shard_map/pallas_call | solution.py:663
  8.3 5.2 %all-to-all-start.1 = ((f32[8,5,24,128]{3,2,1,0:T(8,128)}), f32[8,5,24,128]{3,2,1,0:T(8,128)S(1)}, u32[]{:S(2)}, u32[]{:S(2)}) async-start(f32[8,5,24,128]{3,2,1,0:T(8,128)} %shard_map.78), calls=%async_computation.1 | async-start | bytes 983040 | tf_op jit(solution)/shard_map/all_to_all | solution.py:644
  13.5 1.7 shard_map.75
  15.1 6.8 %all-to-all-done.1.got_ref = f32[8,5,24,128]{3,2,1,0:T(8,128)S(1)} async-done(((f32[8,5,24,128]{3,2,1,0:T(8,128)}), f32[8,5,24,128]{3,2,1,0:T(8,128)S(1)}, u32[]{:S(2)}, u32[]{:S(2)}) %all-to-all-start.1) | async-done | bytes 491552 | tf_op jit(solution)/shard_map/all_to_all | solution.py:644
  21.9 3.4 %all-to-all-start = ((bf16[8,4,16,128]{3,2,1,0:T(8,128)(2,1)}), bf16[8,4,16,128]{3,2,1,0:T(8,128)(2,1)S(1)}, u32[]{:S(2)}, u32[]{:S(2)}) async-start(bf16[8,4,16,128]{3,2,1,0:T(8,128)(2,1)} %shard_map.75), calls=%async_computation | async-start | bytes 262144 | tf_op jit(solution)/shard_map/all_to_all | solution.py:644
  25.3 0.0 copy-done
  25.3 1.7 shard_map.79.refs_4_
  27.1 3.8 %collective-permute-start.2 = (f32[16,24,128]{2,1,0:T(8,128)}, f32[16,24,128]{2,1,0:T(8,128)S(1)}, u32[]{:S(2)}, u32[]{:S(2)}) collective-permute-start(f32[16,24,128]{2,1,0:T(8,128)} %shard_map.79.refs_4_), channel_id=1, source_target_pairs={{0,4},{4,8},{8,12},{12,16},{16,20},{20,24},{24,28},{28,1},{1,5},{5... | collective-permute-start | bytes 589832 | tf_op jit(solution)/shard_map/ppermute | solution.py:658
  30.9 1.8 collective-permute-start.3
  32.6 1.3 collective-permute-start.4
  33.9 1.3 collective-permute-start.5
  35.2 0.0 all-to-all-done.got_ref
  35.3 0.0 copy-start.2
  35.3 0.6 copy-done.2
  35.9 1.5 shard_map.76.refs_1_
  37.5 4.5 %collective-permute-start = (bf16[16,16,128]{2,1,0:T(8,128)(2,1)}, bf16[16,16,128]{2,1,0:T(8,128)(2,1)S(1)}, u32[]{:S(2)}, u32[]{:S(2)}) collective-permute-start(bf16[16,16,128]{2,1,0:T(8,128)(2,1)} %shard_map.76.refs_1_), channel_id=1, source_target_pairs={{0,4},{4,8},{8,12},{12,16},{16,20},{20,24},{24,28},{28,1},{1,5},{5... | collective-permute-start | bytes 196616 | tf_op jit(solution)/shard_map/ppermute | solution.py:658
  42.0 2.2 collective-permute-done.refs_2_
  44.2 1.3 collective-permute-start.1
  46.1 4.7 %collective-permute-done.1.refs_3_ = bf16[16,16,128]{2,1,0:T(8,128)(2,1)S(1)} collective-permute-done((bf16[16,16,128]{2,1,0:T(8,128)(2,1)}, bf16[16,16,128]{2,1,0:T(8,128)(2,1)S(1)}, u32[]{:S(2)}, u32[]{:S(2)}) %collective-permute-start.1) | collective-permute-done | bytes 65568 | tf_op jit(solution)/shard_map/ppermute | solution.py:658
  50.8 0.0 copy-done.8
  50.8 0.6 copy-done.9
  51.4 57.9 %shard_map.77 = (f32[16,48,128]{2,1,0:T(8,128)}, f32[16,32,128]{2,1,0:T(8,128)}) custom-call(s32[2]{0:T(128)} %pad_add_fusion.pos_ref.refs_0_, bf16[16,16,128]{2,1,0:T(8,128)(2,1)} %shard_map.76.refs_1_, bf16[16,16,128]{2,1,0:T(8,128)(2,1)} %copy-done.8, bf16[16,16,128]{2,1,0:T(8,128)(2,1)} %copy-done.9), custom_call_target="tpu_custom_call" | custom-call | tf_op jit(solution)/shard_map/pallas_call | solution.py:683
  109.3 0.0 collective-permute-done.2.refs_5_
  109.3 0.0 collective-permute-done.3.refs_6_
  109.3 0.0 copy-start.5
  109.3 0.0 collective-permute-done.4.refs_7_
  109.3 0.0 copy-start.6
  109.4 0.0 collective-permute-done.5.refs_8_
  109.4 0.0 copy-start.7
  109.4 0.6 copy-done.4
  110.0 0.1 copy-done.5
  110.1 0.1 copy-done.6
  110.1 0.1 copy-done.7
  110.2 63.5 %shard_map.80 = (f32[11,16,48,128]{3,2,1,0:T(8,128)}, f32[11,16,48,128]{3,2,1,0:T(8,128)}, f32[11,16,48,128]{3,2,1,0:T(8,128)}, f32[11,16,48,128]{3,2,1,0:T(8,12...) custom-call(s32[2]{0:T(128)} %pad_add_fusion.pos_ref.refs_0_, f32[1]{0:T(128)S(6)} %copy.9.refs_1_, ...), custom_call_target="tpu_custom_call" | custom-call | tf_op jit(solution)/shard_map/pallas_call | solution.py:695
  173.7 16.5 %all_to_all.25.refs_1_ = f32[32,8,128]{2,1,0:T(8,128)} all-to-all(f32[32,8,128]{2,1,0:T(8,128)} %get-tuple-element.20), channel_id=1, replica_groups=mesh['gx'=4,'gy'=2,'gz'=4] {'gx','gy','gz'}, dimensions={0} | all-to-all | bytes 262144 | tf_op jit(solution)/shard_map/all_to_all | solution.py:647
  190.2 54.7 %shard_map.81 = (f32[8,5,24,128]{3,2,1,0:T(8,128)}, f32[8,128]{1,0:T(8,128)}) custom-call(s32[2]{0:T(128)} %pad_add_fusion.pos_ref.refs_0_, f32[32,8,128]{2,1,0:T(8,128)} %all_to_all.25.refs_1_, f32[11,16,48,128]{3,2,1,0:T(8,128)} %get-tuple-element.21.refs_2_, f32[11,16,48,128]{3,2,1,0:T(8,128)} %get-tuple-element.22.refs_3_, ...), custom_call_target="tpu_custom_call" | custom-call | tf_op jit(solution)/shard_map/pallas_call | solution.py:716
  244.9 3.5 %all-to-all-start.3 = ((f32[8,5,24,128]{3,2,1,0:T(8,128)}), f32[8,5,24,128]{3,2,1,0:T(8,128)S(1)}, u32[]{:S(2)}, u32[]{:S(2)}) async-start(f32[8,5,24,128]{3,2,1,0:T(8,128)} %get-tuple-element.27), calls=%async_computation.3 | async-start | bytes 983040 | tf_op jit(solution)/shard_map/all_to_all | solution.py:644
  248.4 0.0 copy-done.10
  248.4 0.7 copy.8
  249.1 7.7 %all-to-all-done.3.got_ref = f32[8,5,24,128]{3,2,1,0:T(8,128)S(1)} async-done(((f32[8,5,24,128]{3,2,1,0:T(8,128)}), f32[8,5,24,128]{3,2,1,0:T(8,128)S(1)}, u32[]{:S(2)}, u32[]{:S(2)}) %all-to-all-start.3) | async-done | bytes 491552 | tf_op jit(solution)/shard_map/all_to_all | solution.py:644
  256.8 0.8 copy-done.1
  257.6 9.3 %shard_map.82 = (bf16[32,16,16,128]{3,2,1,0:T(8,128)(2,1)}, f32[32,8,128]{2,1,0:T(8,128)}) custom-call(s32[2]{0:T(128)} %pad_add_fusion.pos_ref.refs_0_, bf16[32,27]{1,0:T(8,128)(2,1)} %bitcast.5, bf16[32,16,16,128]{3,2,1,0:T(8,128)(2,1)} %f_ref.3, f32[8,5,24,128]{3,2,1,0:T(8,128)} %copy-done.1), custom_call_target="tpu_custom_call" | custom-call | tf_op jit(solution)/shard_map/pallas_call | solution.py:734
  266.9 2.6 all-to-all-start.4
  269.5 1.2 slice.3
  270.7 6.6 %all-to-all-done.4.got_ref = f32[32,8,128]{2,1,0:T(8,128)S(1)} async-done(((f32[32,8,128]{2,1,0:T(8,128)}), f32[32,8,128]{2,1,0:T(8,128)S(1)}, u32[]{:S(2)}, u32[]{:S(2)}) %all-to-all-start.4) | async-done | bytes 131104 | tf_op jit(solution)/shard_map/all_to_all | solution.py:647
  277.3 0.6 copy-done.3
  277.9 1.6 shard_map.83
  (7 shorter events, 0.0 us)
Async XLA Ops:
  8.3 13.7 %all-to-all-start.1 = ((f32[8,5,24,128]{3,2,1,0:T(8,128)}), f32[8,5,24,128]{3,2,1,0:T(8,128)S(1)}, u32[]{:S(2)}, u32[]{:S(2)}) async-start(f32[8,5,24,128]{3,2,1,0:T(8,128)} %shard_map.78), calls=%async_computation.1 | async-start | bytes 983040 | tf_op jit(solution)/shard_map/all_to_all | solution.py:644
  21.9 3.4 %copy-start = (f32[8,5,24,128]{3,2,1,0:T(8,128)}, f32[8,5,24,128]{3,2,1,0:T(8,128)S(1)}, u32[]{:S(2)}) copy-start(f32[8,5,24,128]{3,2,1,0:T(8,128)S(1)} %all-to-all-done.1.got_ref) | copy-start | bytes 1474564
  21.9 13.3 %all-to-all-start = ((bf16[8,4,16,128]{3,2,1,0:T(8,128)(2,1)}), bf16[8,4,16,128]{3,2,1,0:T(8,128)(2,1)S(1)}, u32[]{:S(2)}, u32[]{:S(2)}) async-start(bf16[8,4,16,128]{3,2,1,0:T(8,128)(2,1)} %shard_map.75), calls=%async_computation | async-start | bytes 262144 | tf_op jit(solution)/shard_map/all_to_all | solution.py:644
  27.1 82.3 %collective-permute-start.2 = (f32[16,24,128]{2,1,0:T(8,128)}, f32[16,24,128]{2,1,0:T(8,128)S(1)}, u32[]{:S(2)}, u32[]{:S(2)}) collective-permute-start(f32[16,24,128]{2,1,0:T(8,128)} %shard_map.79.refs_4_), channel_id=1, source_target_pairs={{0,4},{4,8},{8,12},{12,16},{16,20},{20,24},{24,28},{28,1},{1,5},{5... | collective-permute-start | bytes 589832 | tf_op jit(solution)/shard_map/ppermute | solution.py:658
  30.9 78.4 %collective-permute-start.3 = (f32[16,24,128]{2,1,0:T(8,128)}, f32[16,24,128]{2,1,0:T(8,128)S(1)}, u32[]{:S(2)}, u32[]{:S(2)}) collective-permute-start(f32[16,24,128]{2,1,0:T(8,128)} %shard_map.79.refs_4_), channel_id=1, source_target_pairs={{0,8},{4,12},{8,16},{12,20},{16,24},{20,28},{24,1},{28,5},{1,9},{5... | collective-permute-start | bytes 589832 | tf_op jit(solution)/shard_map/ppermute | solution.py:658
  32.6 76.7 %collective-permute-start.4 = (f32[16,24,128]{2,1,0:T(8,128)}, f32[16,24,128]{2,1,0:T(8,128)S(1)}, u32[]{:S(2)}, u32[]{:S(2)}) collective-permute-start(f32[16,24,128]{2,1,0:T(8,128)} %shard_map.79.refs_4_), channel_id=1, source_target_pairs={{4,0},{8,4},{12,8},{16,12},{20,16},{24,20},{28,24},{1,28},{5,1},{9... | collective-permute-start | bytes 589832 | tf_op jit(solution)/shard_map/ppermute | solution.py:658
  33.9 75.4 %collective-permute-start.5 = (f32[16,24,128]{2,1,0:T(8,128)}, f32[16,24,128]{2,1,0:T(8,128)S(1)}, u32[]{:S(2)}, u32[]{:S(2)}) collective-permute-start(f32[16,24,128]{2,1,0:T(8,128)} %shard_map.79.refs_4_), channel_id=1, source_target_pairs={{8,0},{12,4},{16,8},{20,12},{24,16},{28,20},{1,24},{5,28},{9,1},{1... | collective-permute-start | bytes 589832 | tf_op jit(solution)/shard_map/ppermute | solution.py:658
  35.3 0.7 copy-start.2
  37.5 6.7 %collective-permute-start = (bf16[16,16,128]{2,1,0:T(8,128)(2,1)}, bf16[16,16,128]{2,1,0:T(8,128)(2,1)S(1)}, u32[]{:S(2)}, u32[]{:S(2)}) collective-permute-start(bf16[16,16,128]{2,1,0:T(8,128)(2,1)} %shard_map.76.refs_1_), channel_id=1, source_target_pairs={{0,4},{4,8},{8,12},{12,16},{16,20},{20,24},{24,28},{28,1},{1,5},{5... | collective-permute-start | bytes 196616 | tf_op jit(solution)/shard_map/ppermute | solution.py:658
  44.2 6.6 %copy-start.8 = (bf16[16,16,128]{2,1,0:T(8,128)(2,1)}, bf16[16,16,128]{2,1,0:T(8,128)(2,1)S(1)}, u32[]{:S(2)}) copy-start(bf16[16,16,128]{2,1,0:T(8,128)(2,1)S(1)} %collective-permute-done.refs_2_) | copy-start | bytes 196612
  44.2 6.6 %collective-permute-start.1 = (bf16[16,16,128]{2,1,0:T(8,128)(2,1)}, bf16[16,16,128]{2,1,0:T(8,128)(2,1)S(1)}, u32[]{:S(2)}, u32[]{:S(2)}) collective-permute-start(bf16[16,16,128]{2,1,0:T(8,128)(2,1)} %shard_map.76.refs_1_), channel_id=1, source_target_pairs={{4,0},{8,4},{12,8},{16,12},{20,16},{24,20},{28,24},{1,28},{5,1},{9... | collective-permute-start | bytes 196616 | tf_op jit(solution)/shard_map/ppermute | solution.py:658
  50.8 0.6 copy-start.9
  109.3 0.7 copy-start.4
  109.3 0.7 copy-start.5
  109.3 0.8 copy-start.6
  109.4 0.8 copy-start.7
  190.2 58.2 %copy-start.10 = (bf16[27,32]{1,0:T(8,128)(2,1)S(1)}, bf16[27,32]{1,0:T(8,128)(2,1)}, u32[]{:S(2)}) copy-start(bf16[27,32]{1,0:T(8,128)(2,1)} %w_ref.1) | copy-start | bytes 5188
  244.9 11.9 %all-to-all-start.3 = ((f32[8,5,24,128]{3,2,1,0:T(8,128)}), f32[8,5,24,128]{3,2,1,0:T(8,128)S(1)}, u32[]{:S(2)}, u32[]{:S(2)}) async-start(f32[8,5,24,128]{3,2,1,0:T(8,128)} %get-tuple-element.27), calls=%async_computation.3 | async-start | bytes 983040 | tf_op jit(solution)/shard_map/all_to_all | solution.py:644
  256.8 0.8 copy-start.1
  266.9 10.4 %all-to-all-start.4 = ((f32[32,8,128]{2,1,0:T(8,128)}), f32[32,8,128]{2,1,0:T(8,128)S(1)}, u32[]{:S(2)}, u32[]{:S(2)}) async-start(f32[32,8,128]{2,1,0:T(8,128)} %get-tuple-element.29), calls=%async_computation.4 | async-start | bytes 262144 | tf_op jit(solution)/shard_map/all_to_all | solution.py:647
  277.3 0.7 copy-start.3

commit v2 on v1

v2 whole, which is shorter than its diff:
```python
import functools

import jax
import jax.numpy as jnp
from jax import lax
from jax.experimental import pallas as pl
from jax.experimental.pallas import tpu as pltpu
from jax.sharding import PartitionSpec as P

ITERS = 10
SECTIONS = ITERS + 1
LANES = 128
REACH = SECTIONS + 2
HALO = 2 * SECTIONS + 3

temper = 20.0
sharpness = 40.0

GROUP = ("gx", "gy")
ALL_AXES = ("gx", "gy", "gz")
f32 = jnp.float32
bf16 = jnp.bfloat16


def up8(value):
    return -(-value // 8) * 8


class Plan:
    def __init__(self, mesh_shape, block):
        self.ch, self.nx, self.ny, self.nz = block
        self.gx, self.gy, self.gz = (mesh_shape[a] for a in ALL_AXES)
        self.members = self.gx * self.gy
        self.ranks = self.members * self.gz
        self.X = self.nx * self.gx
        self.Y = self.ny * self.gy
        self.Z = self.nz * self.gz
        assert LANES % self.Y == 0 and self.nz == LANES
        assert self.nz % self.members == 0
        self.zc = self.nz // self.members
        self.per = LANES // self.Y
        assert self.nx % self.per == 0
        self.tiles = self.X // self.per
        self.own = self.nx // self.per
        self.shared = self.per > 1
        self.sent = self.own + (1 if self.shared else 2)
        self.R = up8(self.zc + 2)
        self.pad = self.tiles + 16
        self.win = self.zc + 2 * REACH
        self.span = self.zc + 2
        self.block = self.blocks_of(self.win)
        self.span_block = self.blocks_of(self.span)
        self.base = HALO + 1
        self.planes = self.zc + 2 * HALO + 2 + self.block
        self.hops = -(-HALO // self.zc)
        self.rest = HALO - (self.hops - 1) * self.zc
        self.label_hops = -(-REACH // self.zc)
        self.label_rest = REACH - (self.label_hops - 1) * self.zc

    def blocks_of(self, count):
        fits = [n for n in range(1, count + 1) if count % n == 0 and n * self.tiles <= 128]
        return fits[-1] if fits else 1

    def slot(self, x):
        if 0 <= x < self.nx:
            return x // self.per, (x % self.per) * self.Y
        if x == self.nx:
            return self.own, 0
        return self.sent - 1, LANES - self.Y


def lane_iota(shape):
    return lax.broadcasted_iota(jnp.int32, shape, len(shape) - 1)


def row_iota(shape):
    return lax.broadcasted_iota(jnp.int32, shape, len(shape) - 2)


def masks(plan):
    lane = lane_iota((plan.tiles, LANES))
    return lane, lane % plan.Y == 0, lane % plan.Y == plan.Y - 1


def x_neighbours(plan, mask, load, cur):
    lower, upper = load(-1), load(1)
    if plan.Y == LANES:
        return lower + upper
    lower = pltpu.roll(jnp.where(mask[0] >= LANES - plan.Y, lower, cur), plan.Y, 1)
    upper = pltpu.roll(jnp.where(mask[0] < plan.Y, upper, cur), LANES - plan.Y, 1)
    return lower + upper


def y_neighbours(plan, mask, cur):
    lower = jnp.where(mask[1], 0.0, pltpu.roll(cur, 1, 1))
    upper = jnp.where(mask[2], 0.0, pltpu.roll(cur, LANES - 1, 1))
    return lower + upper


def count_tables(plan, cross_ref, box_ref):
    flat = row_iota((plan.tiles, LANES)) * LANES + lane_iota((plan.tiles, LANES))
    y, x = flat % plan.Y, flat // plan.Y

    def along(spot, size):
        return 3.0 - (spot == 0).astype(f32) - (spot == size - 1).astype(f32)

    cx, cy = along(x, plan.X), along(y, plan.Y)
    for kind, cz in ((1, 2.0), (2, 3.0)):
        if cross_ref is not None:
            cross_ref[kind] = 1.0 / (cx + cy + cz - 2.0)
        if box_ref is not None:
            box_ref[kind] = 1.0 / (cx * cy * cz)
    for ref in (cross_ref, box_ref):
        if ref is not None:
            ref[0] = jnp.zeros((plan.tiles, LANES), f32)


def kind_of(plan, rank, plane):
    z = rank * plan.zc + plane
    inside = (z >= 0) & (z < plan.Z)
    edge = (z == 0) | (z == plan.Z - 1)
    return jnp.where(inside, jnp.where(edge, 1, 2), 0)


def store_all(pairs):
    for ref, at, value in pairs:
        ref[at] = value


def over(first, count, size, body):
    def at(n, carry):
        body(first + n * size)
        return carry

    lax.fori_loop(0, (count + size - 1) // size, at, 0)


def tap_condition(plan, member_y, shape, y_dim, in_dim):
    y = lax.broadcasted_iota(jnp.int32, shape, y_dim) % plan.Y
    own = lax.broadcasted_iota(jnp.int32, shape, in_dim) % plan.ny
    return own + member_y * plan.ny - y + 1


def conv_kernel(plan, pos_ref, w_ref, f_ref, out_ref, wide_ref, acc_ref):
    rows, inner = plan.Y, plan.ch * plan.ny
    spread = (
        lax.broadcasted_iota(jnp.int32, (plan.ch, inner), 0)
        == lax.broadcasted_iota(jnp.int32, (plan.ch, inner), 1) // plan.ny
    ).astype(f32)
    taps = jnp.dot(w_ref[...].astype(f32), spread, preferred_element_type=f32)
    tap_y = tap_condition(plan, pos_ref[1], (rows, inner), 0, 1)
    for i in range(3):
        for k in range(3):
            band = jnp.zeros((rows, inner), f32)
            for j in range(3):
                t = 9 * i + 3 * j + k
                band = jnp.where(tap_y == j, taps[t : t + 1], band)
            at = (3 * i + k) * rows
            wide_ref[at : at + rows] = band.astype(bf16)
    acc_ref[...] = jnp.zeros_like(acc_ref)

    def at_x(x, carry):
        block = f_ref[:, x].reshape(inner, plan.nz)
        out = jnp.dot(wide_ref[...], block, preferred_element_type=f32)
        for i in range(3):
            acc_ref[x + 2 - i] += out[3 * i * rows : 3 * (i + 1) * rows]
        return carry

    lax.fori_loop(0, plan.nx, at_x, 0)

    out_ref[...] = jnp.zeros_like(out_ref)
    places = {}
    for x in range(-1, plan.nx + 1):
        tile, lane = plan.slot(x)
        places.setdefault(tile, {})[lane] = x
    lane = lane_iota((rows, plan.nz))
    for tile in range(plan.sent):
        parts, spills = [], []
        for first in range(0, LANES, rows):
            x = places[tile].get(first)
            if x is None:
                parts.append(jnp.zeros((rows, plan.nz), f32))
                spills.append(jnp.zeros((rows, plan.nz), f32))
                continue
            low = acc_ref[x + 1, 0:rows]
            mid = acc_ref[x + 1, rows : 2 * rows]
            high = acc_ref[x + 1, 2 * rows : 3 * rows]
            total = mid + jnp.where(lane == 0, 0.0, pltpu.roll(low, 1, 1))
            total = total + jnp.where(lane == plan.nz - 1, 0.0, pltpu.roll(high, plan.nz - 1, 1))
            parts.append(total)
            spill = jnp.where(lane == 1, pltpu.roll(low, 2, 1), 0.0)
            spills.append(jnp.where(lane == 0, high, spill))
        turned = jnp.concatenate(parts, axis=0).T
        spill = jnp.concatenate(spills, axis=0).T
        for p in range(plan.members):
            out_ref[p, tile, 0 : plan.zc] = turned[p * plan.zc : (p + 1) * plan.zc]
        out_ref[0, tile, plan.zc : plan.zc + 1] = spill[0:1]
        out_ref[plan.members - 1, tile, plan.zc + 1 : plan.zc + 2] = spill[1:2]


def label_kernel(plan, pos_ref, l_ref, out_ref):
    rows = plan.Y
    sub = lax.broadcasted_iota(jnp.int32, (plan.gy, plan.ny, plan.nz), 0)
    for tile in range(plan.own):
        parts = []
        for n in range(plan.per):
            block = l_ref[tile * plan.per + n].astype(f32)[None]
            wide = jnp.where(sub == pos_ref[1], block, 0.0)
            parts.append(wide.reshape(rows, plan.nz))
        turned = jnp.concatenate(parts, axis=0).T
        for p in range(plan.members):
            out_ref[p, tile] = turned[p * plan.zc : (p + 1) * plan.zc].astype(bf16)


def gather_kernel(plan, got_ref, out_ref, head_ref, tail_ref):
    lane = lane_iota((plan.R, LANES))
    tiles, zc, rest = plan.tiles, plan.zc, plan.rest
    for a in range(plan.gx):
        for q in range(plan.own):
            total = jnp.zeros((plan.R, LANES), f32)
            for b in range(plan.gy):
                total = total + got_ref[a * plan.gy + b, q]
                if q == plan.own - 1 and a < plan.gx - 1:
                    edge = got_ref[(a + 1) * plan.gy + b, plan.sent - 1]
                    total = total + jnp.where(lane >= LANES - plan.Y, edge, 0.0)
                if q == 0 and a > 0:
                    edge = got_ref[(a - 1) * plan.gy + b, plan.own]
                    total = total + jnp.where(lane < plan.Y, edge, 0.0)
            tile = a * plan.own + q
            out_ref[pl.ds(tile, zc + 2, stride=tiles)] = total[: zc + 2]
    head_ref[: rest * tiles] = out_ref[: rest * tiles]
    head_ref[rest * tiles :] = out_ref[zc * tiles : (zc + 1) * tiles]
    tail_ref[: rest * tiles] = out_ref[(zc - rest) * tiles : zc * tiles]
    tail_ref[rest * tiles :] = out_ref[(zc + 1) * tiles :]


def label_gather_kernel(plan, got_ref, out_ref, head_ref, tail_ref, all_ref):
    tiles, zc, rest = plan.tiles, plan.zc, plan.label_rest
    for a in range(plan.gx):
        for q in range(plan.own):
            total = got_ref[a * plan.gy, q].astype(f32)
            for b in range(1, plan.gy):
                total = total + got_ref[a * plan.gy + b, q].astype(f32)
            all_ref[pl.ds(a * plan.own + q, zc, stride=tiles)] = total
    out_ref[...] = all_ref[...].astype(bf16)
    head_ref[...] = all_ref[: rest * tiles].astype(bf16)
    tail_ref[...] = all_ref[(zc - rest) * tiles :].astype(bf16)


def thin(e, box, inverse, s):
    ok = (e > 0.0) & (box > 0.0) & (inverse > 0.0)
    box = jnp.where(ok, box, 1.0)
    ratio = jnp.where(ok, e * box * inverse, 1.0)
    square = ratio * ratio
    more = 1.0 + square
    joint = 1.0 / (box * more)
    slope = joint * box
    scaled = -jnp.log(square * slope)
    lift = scaled * (1.0 - s)
    small = jnp.exp(-jnp.abs(lift))
    part = 1.0 / (1.0 + small)
    rate = jnp.where(lift >= 0.0, part, small * part)
    grown = s + (jnp.maximum(lift, 0.0) - jnp.log(part)) * (1.0 / sharpness)
    thinned = scaled * (1.0 / sharpness)
    return ok, slope, joint * more, rate, thinned, grown


def erode(plan, rank, mask, e_ref, g_ref, table_ref, now, base, first, count, size):
    tiles = slice(8, 8 + plan.tiles)

    def body(plane):
        out = []
        for n in range(size):
            at = plane + n + base
            cur = e_ref[now, at, tiles]

            def load(offset, at=at):
                return e_ref[now, at, 8 + offset : 8 + offset + plan.tiles]

            total = cur + e_ref[now, at - 1, tiles] + e_ref[now, at + 1, tiles]
            total = total + x_neighbours(plan, mask, load, cur) + y_neighbours(plan, mask, cur)
            total = total * table_ref[kind_of(plan, rank, plane + n)]
            out.append((e_ref, (1 - now, at, tiles), total))
            out.append((g_ref, (1 - now, at), jnp.where(total > 0.0, 1.0 / total, 0.0)))
        store_all(out)

    over(first, count, size, body)


def spread(plan, mask, g_ref, now, zy_ref, base, first, count, size):
    tiles = slice(8, 8 + plan.tiles)

    def body(plane):
        out = []
        values = [g_ref[now, plane + n + base] for n in range(-1, size + 1)]
        for n in range(size):
            part = values[n] + values[n + 1] + values[n + 2]
            part = part + y_neighbours(plan, mask, part)
            out.append((zy_ref, (plane + n - first, tiles), part))
        store_all(out)

    over(first, count, size, body)


def x_box(plan, mask, zy_ref, at):
    cur = zy_ref[at, 8 : 8 + plan.tiles]

    def load(offset):
        return zy_ref[at, 8 + offset : 8 + offset + plan.tiles]

    return cur + x_neighbours(plan, mask, load, cur)


def target_kernel(plan, *refs):
    hops = plan.label_hops
    pos_ref, own_ref = refs[:2]
    below, above = refs[2 : 2 + hops], refs[2 + hops : 2 + 2 * hops]
    target_ref, ts_ref = refs[2 + 2 * hops : 4 + 2 * hops]
    e_ref, g_ref, zy_ref, cross_ref, box_ref = refs[4 + 2 * hops :]
    zc, win, span = plan.zc, plan.win, plan.span
    size = plan.span_block
    base = REACH + 1
    tiles = slice(8, 8 + plan.tiles)
    rank = pos_ref[0]
    mask = masks(plan)
    count_tables(plan, cross_ref, box_ref)
    e_ref[...] = jnp.zeros_like(e_ref)
    zy_ref[...] = jnp.zeros_like(zy_ref)
    g_ref[...] = jnp.zeros_like(g_ref)
    target_ref[REACH : REACH + zc] = own_ref[...].astype(f32)
    for h in range(1, hops + 1):
        n = zc if h < hops else plan.label_rest
        first = REACH - (h - 1) * zc - n
        target_ref[first : first + n] = below[h - 1][...].astype(f32)
        first = REACH + h * zc
        target_ref[first : first + n] = above[h - 1][...].astype(f32)

    def fill(plane):
        out = []
        for n in range(plan.block):
            at = plane + n
            z = rank * zc + at - REACH
            inside = ((z >= 0) & (z < plan.Z)).astype(f32)
            out.append((e_ref, (0, at + 1, tiles), jnp.exp(-temper * target_ref[at]) * inside))
        store_all(out)

    over(0, win, plan.block, fill)

    def section(step, carry):
        now = step % 2
        reach = 2 + ITERS - step
        erode(
            plan, rank, mask, e_ref, g_ref, cross_ref, now, base, -reach, zc + 2 * reach, size
        )
        spread(plan, mask, g_ref, 1 - now, zy_ref, base, -1, span, size)

        def point(plane):
            out = []
            for n in range(size):
                at = plane + n
                box = x_box(plan, mask, zy_ref, at)
                s = jnp.where(step == 0, 0.0, ts_ref[at])
                inverse = box_ref[kind_of(plan, rank, at - 1)]
                result = thin(e_ref[now, at - 1 + base, tiles], box, inverse, s)
                out.append((ts_ref, at, jnp.where(step == 0, result[4], result[5])))
            store_all(out)

        over(0, span, size, point)
        return carry

    lax.fori_loop(0, SECTIONS, section, 0)


def forward_kernel(plan, *refs):
    hops = plan.hops
    pos_ref, bias_ref, target_ref, ts_ref, own_ref = refs[:5]
    refs = refs[5:]
    below, above = refs[:hops], refs[hops : 2 * hops]
    refs = refs[2 * hops :]
    m_ref, q_ref, t_ref, g2_ref, p_ref, sums_ref = refs[:6]
    e_ref, g_ref, zy_ref, s_ref, cross_ref, box_ref = refs[6:]
    base, zc, size = plan.base, plan.zc, plan.block
    tiles = slice(8, 8 + plan.tiles)
    rank = pos_ref[0]
    step = pl.program_id(0)
    mask = masks(plan)

    @pl.when(step == 0)
    def _():
        e_ref[...] = jnp.zeros_like(e_ref)
        g_ref[...] = jnp.zeros_like(g_ref)
        zy_ref[...] = jnp.zeros_like(zy_ref)
        s_ref[...] = jnp.zeros_like(s_ref)
        count_tables(plan, cross_ref, box_ref)
        e_ref[0, base : base + zc, tiles] = own_ref[:zc]
        for h in range(1, hops + 1):
            n = zc if h < hops else plan.rest
            first = base - (h - 1) * zc - n
            e_ref[0, first : first + n, tiles] = below[h - 1][:n]
            first = base + h * zc
            e_ref[0, first : first + n, tiles] = above[h - 1][:n]
        e_ref[0, base - 1, tiles] += own_ref[zc]
        e_ref[0, base + zc, tiles] += own_ref[zc + 1]
        for h in range(1, hops + 1):
            if h < hops:
                e_ref[0, base - h * zc - 1, tiles] += below[h - 1][zc]
                e_ref[0, base + (h + 1) * zc, tiles] += above[h - 1][zc + 1]
                e_ref[0, base - (h - 1) * zc, tiles] += below[h - 1][zc + 1]
                e_ref[0, base + h * zc - 1, tiles] += above[h - 1][zc]
            else:
                e_ref[0, base - (h - 1) * zc, tiles] += below[h - 1][plan.rest]
                e_ref[0, base + h * zc - 1, tiles] += above[h - 1][plan.rest]

        def sigmoid(logits):
            small = jnp.exp(-jnp.abs(logits))
            part = 1.0 / (1.0 + small)
            return jnp.where(logits >= 0, part, small * part)

        for n in range(plan.span):
            p_ref[n] = sigmoid(e_ref[0, base - 1 + n, tiles] + bias_ref[0])

        def fill(plane):
            out = []
            for n in range(size):
                at = plane + n
                z = rank * zc + at - base
                inside = ((z >= 0) & (z < plan.Z)).astype(f32)
                predict = sigmoid(e_ref[0, at, tiles] + bias_ref[0])
                out.append((e_ref, (0, at, tiles), jnp.exp(-temper * predict) * inside))
            store_all(out)

        over(1, zc + 2 * HALO, size, fill)

    now = step % 2
    reach = REACH + 1 + ITERS - step
    erode(plan, rank, mask, e_ref, g_ref, cross_ref, now, base, -reach, zc + 2 * reach, size)
    spread(plan, mask, g_ref, 1 - now, zy_ref, base, -REACH, plan.win, size)
    opening = step == 0

    def point(at):
        out = []
        for n in range(size):
            spot = at + n
            plane = spot - REACH
            e = e_ref[now, plane + base, tiles]
            s = s_ref[spot]
            box = x_box(plan, mask, zy_ref, spot)
            inverse = box_ref[kind_of(plan, rank, plane)]
            ok, slope, over_box, rate, thinned, grown = thin(e, box, inverse, s)
            a = jnp.where(opening, slope, rate * (1.0 - s) * slope)
            a = jnp.where(ok, a, 0.0)
            before = jnp.where(opening, jnp.where(e > 0.0, 1.0 / e, 0.0), g_ref[now, plane + base])
            after = g_ref[1 - now, plane + base]
            out.append((s_ref, spot, jnp.where(opening, thinned, grown)))
            out.append((m_ref, (0, spot), 1.0 - rate * thinned))
            out.append((q_ref, (0, spot), a * over_box))
            out.append((t_ref, (0, spot), a * before))
            out.append((g2_ref, (0, spot), after * after))
        store_all(out)

    over(0, plan.win, size, point)

    @pl.when(step == SECTIONS - 1)
    def _():
        def add(n, totals):
            ps, ts = s_ref[REACH + n], ts_ref[1 + n]
            predict, target = p_ref[1 + n], target_ref[REACH + n]
            terms = (ps * target, ps, ts * predict, ts, predict * target, predict, target)
            return tuple(total + term for total, term in zip(totals, terms))

        start = (jnp.zeros((plan.tiles, LANES), f32),) * 7
        totals = lax.fori_loop(0, zc, add, start)
        lines = [jnp.sum(total, axis=0, keepdims=True) for total in totals]
        lines.append(jnp.zeros((1, LANES), f32))
        sums_ref[...] = jnp.broadcast_to(
            jnp.concatenate(lines, axis=0)[None], (plan.ranks, 8, LANES)
        )


def backward_kernel(plan, *refs):
    (
        pos_ref, sums_ref, m_ref, q_ref, t_ref, g2_ref, p_ref, target_ref, ts_ref,
        out_ref, loss_ref,
        w_ref, h_ref, zy_ref, pull_ref, cross_ref, grad_ref,
    ) = refs
    step = pl.program_id(0)
    rank = pos_ref[0]
    win, zc, size = plan.win, plan.zc, plan.block
    tiles = slice(8, 8 + plan.tiles)
    mask = masks(plan)

    lines = jnp.sum(jnp.sum(sums_ref[...], axis=0), axis=1, keepdims=True)
    s1, s2, s3, s4, s5, s6, s7 = (lines[n : n + 1] for n in range(7))
    prec = (s1 + 1.0) / (s2 + 1.0)
    sens = (s3 + 1.0) / (s4 + 1.0)

    @pl.when(step == 0)
    def _():
        zy_ref[...] = jnp.zeros_like(zy_ref)
        pull_ref[...] = jnp.zeros_like(pull_ref)
        h_ref[...] = jnp.zeros_like(h_ref)
        count_tables(plan, cross_ref, None)
        w_ref[...] = target_ref[...] - prec[None]

    def within(reach, body):
        count = (zc + 2 * reach + size - 1) // size
        first = jnp.minimum(REACH - reach, win - count * size)
        over(first, count * size, size, body)

    left = SECTIONS - 1 - step

    def push(at):
        values = []
        for n in range(-1, size + 1):
            spot = jnp.clip(at + n, 0, win - 1)
            values.append(w_ref[spot] * q_ref[0, spot])
        out = []
        for n in range(size):
            part = values[n] + values[n + 1] + values[n + 2]
            part = part + y_neighbours(plan, mask, part)
            out.append((zy_ref, (at + n, tiles), part))
        store_all(out)

    within(left + 2, push)

    def pull(at):
        out = []
        for n in range(size):
            spot = at + n
            box = x_box(plan, mask, zy_ref, spot)
            inverse = cross_ref[kind_of(plan, rank, spot - REACH)]
            value = (h_ref[spot] - g2_ref[0, spot] * box) * inverse
            out.append((pull_ref, (spot + 1, tiles), value))
        store_all(out)

    within(left + 2, pull)

    def join(at):
        out = []
        for n in range(size):
            spot = at + n
            cur = pull_ref[spot + 1, tiles]

            def load(offset, spot=spot):
                return pull_ref[spot + 1, 8 + offset : 8 + offset + plan.tiles]

            total = cur + pull_ref[spot, tiles] + pull_ref[spot + 2, tiles]
            total = total + x_neighbours(plan, mask, load, cur) + y_neighbours(plan, mask, cur)
            w = w_ref[spot]
            out.append((h_ref, spot, w * t_ref[0, spot] + total))
            out.append((w_ref, spot, w * m_ref[0, spot]))
        store_all(out)

    within(left + 2, join)

    @pl.when(step == SECTIONS - 1)
    def _():
        both = prec + sens
        volume = s6 + s7 + 1.0
        cl_loss = 1.0 - 2.0 * prec * sens / both
        dice_loss = 1.0 - (2.0 * s5 + 1.0) / volume
        loss_ref[...] = jnp.broadcast_to(0.5 * dice_loss + 0.5 * cl_loss, (8, LANES))
        l0 = -(sens / both) * (sens / both) / (s2 + 1.0)
        l2 = -(prec / both) * (prec / both) / (s4 + 1.0)
        l4 = -1.0 / volume
        l5 = 0.5 * (2.0 * s5 + 1.0) / (volume * volume)

        def finish(n, carry):
            z = rank * zc + n - 1
            inside = ((z >= 0) & (z < plan.Z)).astype(f32)
            at = n + REACH - 1
            predict = p_ref[n]
            skel = l0 * jnp.exp(-temper * predict) * h_ref[at]
            whole = skel + l2 * ts_ref[n] + l4 * target_ref[at] + l5
            grad = whole * predict * (1.0 - predict) * inside
            grad_ref[pl.ds(pl.multiple_of(n * plan.tiles, 8), plan.tiles)] = grad
            return carry

        lax.fori_loop(0, plan.span, finish, 0)
        lane = lane_iota((zc, LANES))
        fill = plan.R - zc - 2

        def column(tile):
            return [
                grad_ref[pl.ds(plan.tiles + tile, zc, stride=plan.tiles)],
                grad_ref[tile : tile + 1],
                grad_ref[(zc + 1) * plan.tiles + tile : (zc + 1) * plan.tiles + tile + 1],
            ]

        def place(a, q, pieces):
            for b in range(plan.gy):
                p = a * plan.gy + b
                out_ref[p, q, 0:zc] = pieces[0]
                out_ref[p, q, zc : zc + 1] = pieces[1]
                out_ref[p, q, zc + 1 : zc + 2] = pieces[2]
                if fill:
                    out_ref[p, q, zc + 2 :] = jnp.zeros((fill, LANES), f32)

        for a in range(plan.gx):
            for q in range(plan.own):
                place(a, q, column(a * plan.own + q))
            zero = [jnp.zeros((zc, LANES), f32)] + [jnp.zeros((1, LANES), f32)] * 2
            after = column((a + 1) * plan.own) if a < plan.gx - 1 else zero
            before = column(a * plan.own - 1) if a > 0 else zero
            if plan.shared:
                edge = [
                    jnp.where(lane[: x.shape[0]] < plan.Y, x, 0.0)
                    + jnp.where(lane[: y.shape[0]] >= LANES - plan.Y, y, 0.0)
                    for x, y in zip(after, before)
                ]
                place(a, plan.own, edge)
            else:
                place(a, plan.own, after)
                place(a, plan.own + 1, before)


def grad_kernel(plan, pos_ref, wt_ref, f_ref, got_ref, gf_ref, gw_ref, wide_ref, g_ref, dw_ref):
    rows, inner, bands = plan.Y, plan.ch * plan.ny, 9 * plan.Y
    spread = (
        lax.broadcasted_iota(jnp.int32, (inner, plan.ch), 0) // plan.ny
        == lax.broadcasted_iota(jnp.int32, (inner, plan.ch), 1)
    ).astype(f32)
    tap_y = tap_condition(plan, pos_ref[1], (inner, bands), 1, 0)
    wide = jnp.zeros((inner, bands), f32)
    tap = lax.broadcasted_iota(jnp.int32, (27, bands), 0)
    band = lax.broadcasted_iota(jnp.int32, (27, bands), 1) // rows
    for j in range(3):
        pick = (tap == 9 * (band // 3) + 3 * j + band % 3).astype(f32)
        chosen = jnp.dot(wt_ref[...].astype(f32), pick, preferred_element_type=f32)
        full = jnp.dot(spread, chosen, preferred_element_type=f32)
        wide = jnp.where(tap_y == j, full, wide)
    wide_ref[...] = wide.astype(bf16)

    zc = plan.zc
    lane = lane_iota((rows, plan.nz))
    bias = jnp.zeros((rows, plan.nz), f32)
    places = {}
    for x in range(-1, plan.nx + 1):
        tile, first = plan.slot(x)
        places.setdefault(tile, {})[first] = x
    for tile in range(plan.sent):
        stack = [got_ref[p, tile, 0:zc] for p in range(plan.members)]
        turned = jnp.concatenate(stack, axis=0).T
        low = got_ref[0, tile, zc : zc + 1]
        high = got_ref[plan.members - 1, tile, zc + 1 : zc + 2]
        ends = jnp.concatenate([low, high, jnp.zeros((LANES - 2, LANES), f32)], axis=0).T
        for first, x in places[tile].items():
            g = turned[first : first + rows]
            end = ends[first : first + rows]
            down = jnp.where(lane == plan.nz - 1, pltpu.roll(end, plan.nz - 2, 1), pltpu.roll(g, plan.nz - 1, 1))
            up = jnp.where(lane == 0, end, pltpu.roll(g, 1, 1))
            g_ref[x + 1] = jnp.concatenate([down, g, up], axis=0).astype(bf16)
            if 0 <= x < plan.nx:
                bias = bias + g
    y_own = lax.broadcasted_iota(jnp.int32, (rows, plan.nz), 0) // plan.ny == pos_ref[1]
    bias = jnp.sum(jnp.where(y_own, bias, 0.0))

    dw_ref[...] = jnp.zeros_like(dw_ref)

    def at_x(x, carry):
        block = f_ref[:, x].reshape(inner, plan.nz)
        moved = jnp.concatenate([g_ref[x + 2], g_ref[x + 1], g_ref[x]], axis=0)
        out = jnp.dot(wide_ref[...], moved, preferred_element_type=f32)
        gf_ref[:, x] = out.astype(bf16).reshape(plan.ch, plan.ny, plan.nz)
        dw_ref[...] += lax.dot_general(
            moved, block, (((1,), (1,)), ((), ())), preferred_element_type=f32
        )
        return carry

    lax.fori_loop(0, plan.nx, at_x, 0)

    tap_y = tap_condition(plan, pos_ref[1], (rows, inner), 0, 1)
    taps = []
    for t in range(27):
        i, j, k = t // 9, t // 3 % 3, t % 3
        at = (3 * i + k) * rows
        taps.append(jnp.sum(jnp.where(tap_y == j, dw_ref[at : at + rows], 0.0), axis=0, keepdims=True))
    taps += [jnp.zeros((1, inner), f32)] * 5
    total = jnp.zeros((8, LANES), f32)
    for n in range(4):
        place = (
            lax.broadcasted_iota(jnp.int32, (inner, LANES), 0) // plan.ny + 32 * n
            == lax.broadcasted_iota(jnp.int32, (inner, LANES), 1)
        ).astype(f32)
        total = total + jnp.dot(
            jnp.concatenate(taps[8 * n : 8 * n + 8], axis=0),
            place,
            precision=lax.Precision.HIGHEST,
            preferred_element_type=f32,
        )
    spot = (row_iota((8, LANES)) == 3) & (lane_iota((8, LANES)) == 96)
    total = jnp.where(spot, bias, total)
    gw_ref[...] = jnp.broadcast_to(total[None], (plan.ranks, 8, LANES))


def final_kernel(plan, got_ref, gw_ref, gb_ref):
    total = jnp.sum(got_ref[...], axis=0)
    for n in range(4):
        count = min(8, 27 - 8 * n)
        gw_ref[8 * n : 8 * n + count] = total[:count, 32 * n : 32 * n + plan.ch]
    gb_ref[...] = total[3:4, 96:97]


VMEM = pl.BlockSpec(memory_space=pltpu.VMEM)
SMEM = pl.BlockSpec(memory_space=pltpu.SMEM)
BIG = pltpu.CompilerParams(vmem_limit_bytes=63 * 1024 * 1024)


def shape(dims, dtype=f32):
    return jax.ShapeDtypeStruct(dims, dtype)


def per_device(mesh_shape, features, weight, bias, label):
    plan = Plan(mesh_shape, features.shape)
    members, sent, own, R, tiles = plan.members, plan.sent, plan.own, plan.R, plan.tiles
    inner, bands = plan.ch * plan.ny, 9 * plan.Y
    place = (lax.axis_index("gz") * members + lax.axis_index(GROUP)).astype(jnp.int32)
    pos = jnp.stack([place, lax.axis_index("gy").astype(jnp.int32)])

    def call(kernel, out_shape, in_specs, scratch=(), params=BIG):
        return pl.pallas_call(
            functools.partial(kernel, plan),
            out_shape=out_shape,
            in_specs=in_specs,
            out_specs=jax.tree.map(lambda s: VMEM, out_shape),
            scratch_shapes=list(scratch),
            compiler_params=params,
        )

    def exchange(array):
        return lax.all_to_all(array, GROUP, 0, 0, tiled=True)

    def everywhere(array):
        return lax.all_to_all(array, ALL_AXES, 0, 0, tiled=True)

    def hop(array, distance):
        def device(r):
            return (r % members) * plan.gz + r // members

        pairs = [
            (device(r), device(r + distance))
            for r in range(plan.ranks)
            if 0 <= r + distance < plan.ranks
        ]
        return lax.ppermute(array, ALL_AXES, pairs)

    label_sent = call(label_kernel, shape((members, own, plan.zc, LANES), bf16), [SMEM, VMEM])(
        pos, label
    )
    sent_logits = call(
        conv_kernel,
        shape((members, sent, R, LANES)),
        [SMEM, VMEM, VMEM],
        [
            pltpu.VMEM((bands, inner), bf16),
            pltpu.VMEM((plan.nx + 2, 3 * plan.Y, plan.nz), f32),
        ],
    )(pos, weight, features)
    def planes(array):
        return array.reshape(-1, tiles, LANES)

    def hops_of(parts, count):
        whole, head, tail = parts
        below = [hop(whole if h < count else tail, h) for h in range(1, count + 1)]
        above = [hop(whole if h < count else head, -h) for h in range(1, count + 1)]
        return below + above

    zc = plan.zc
    short = plan.label_rest * tiles
    label_parts = call(
        label_gather_kernel,
        [shape((zc * tiles, LANES), bf16)] + [shape((short, LANES), bf16)] * 2,
        [VMEM],
        [pltpu.VMEM((zc * tiles, LANES), f32)],
    )(exchange(label_sent))
    label_parts = [planes(part) for part in label_parts]
    short = (plan.rest + 1) * tiles
    parts = call(
        gather_kernel,
        [shape(((zc + 2) * tiles, LANES))] + [shape((short, LANES))] * 2,
        [VMEM],
    )(exchange(sent_logits))
    parts = [planes(part) for part in parts]
    around = hops_of(parts, plan.hops)
    label_around = hops_of(label_parts, plan.label_hops)

    window = (plan.win, tiles, LANES)
    span = (plan.span, tiles, LANES)
    table = pltpu.VMEM((3, tiles, LANES), f32)
    room = plan.win + 2 + plan.span_block
    target, ts = call(
        target_kernel,
        [shape(window), shape(span)],
        [SMEM] + [VMEM] * (1 + 2 * plan.label_hops),
        [
            pltpu.VMEM((2, room, plan.pad, LANES), f32),
            pltpu.VMEM((2, room, tiles, LANES), f32),
            pltpu.VMEM((plan.span, plan.pad, LANES), f32),
            table,
            table,
        ],
    )(pos, label_parts[0], *label_around)
    record = pl.BlockSpec((1,) + window, lambda n: (n, 0, 0, 0))
    outs = pl.pallas_call(
        functools.partial(forward_kernel, plan),
        grid=(SECTIONS,),
        out_shape=[shape((SECTIONS,) + window)] * 4
        + [shape(span), shape((plan.ranks, 8, LANES))],
        in_specs=[SMEM, SMEM] + [VMEM] * (3 + 2 * plan.hops),
        out_specs=[record] * 4 + [VMEM] * 2,
        scratch_shapes=[
            pltpu.VMEM((2, plan.planes, plan.pad, LANES), f32),
            pltpu.VMEM((2, plan.planes, tiles, LANES), f32),
            pltpu.VMEM((plan.win, plan.pad, LANES), f32),
            pltpu.VMEM(window, f32),
            table,
            table,
        ],
        compiler_params=BIG,
    )(pos, bias, target, ts, parts[0], *around)
    m, q, t, g2, predict, sums = outs
    sums = everywhere(sums)

    back = pl.BlockSpec((1,) + window, lambda n: (SECTIONS - 1 - n, 0, 0, 0))
    grad_sent, loss = pl.pallas_call(
        functools.partial(backward_kernel, plan),
        grid=(SECTIONS,),
        out_shape=[shape((members, sent, R, LANES)), shape((8, LANES))],
        in_specs=[SMEM, VMEM] + [back] * 4 + [VMEM] * 3,
        out_specs=[VMEM, VMEM],
        scratch_shapes=[
            pltpu.VMEM(window, f32),
            pltpu.VMEM(window, f32),
            pltpu.VMEM((plan.win, plan.pad, LANES), f32),
            pltpu.VMEM((plan.win + 2, plan.pad, LANES), f32),
            table,
            pltpu.VMEM((plan.span * tiles, LANES), f32),
        ],
        compiler_params=BIG,
    )(pos, sums, m, q, t, g2, predict, target, ts)

    grad_features, partial = call(
        grad_kernel,
        [shape(features.shape, bf16), shape((plan.ranks, 8, LANES))],
        [SMEM, VMEM, VMEM, VMEM],
        [
            pltpu.VMEM((inner, bands), bf16),
            pltpu.VMEM((plan.nx + 2, 3 * plan.Y, plan.nz), bf16),
            pltpu.VMEM((bands, inner), f32),
        ],
    )(pos, weight.T, features, exchange(grad_sent))
    grad_weight, grad_bias = call(
        final_kernel, [shape((27, plan.ch)), shape((1, 1))], [VMEM]
    )(everywhere(partial))
    return (loss[0, :1], grad_features, grad_weight, grad_bias.reshape(1))


def solution(mesh):
    in_specs = (P(None, "gx", "gy", "gz"), P(), P(), P("gx", "gy", "gz"))
    out_specs = (P(), P(None, "gx", "gy", "gz"), P(), P())
    return jax.shard_map(
        functools.partial(per_device, dict(mesh.shape)),
        mesh=mesh,
        in_specs=in_specs,
        out_specs=out_specs,
        check_vma=False,
    )
```

time: 280 us -> 179 us (0.64)
  Pallas kernels: 199 us -> 101 us
    pallas_call x3, Pallas kernels: 61.2 us -> 21.5 us  [the longest x1 18.1 us: per_device(): call(target_kernel, [shape(window), shape(span)], [SMEM] + [VMEM] * (1 +...]
    pallas_call x1, Pallas kernels: 54.7 us -> 23.3 us  [per_device(): pl.pallas_call(functools.partial(backward_kernel, plan), grid=(SECTIONS,)...]
    pallas_call x1, Pallas kernels: 63.5 us -> 36.6 us  [per_device(): pl.pallas_call(functools.partial(forward_kernel, plan), grid=(SECTIONS,),...]
  transfers between devices with their start and end apart: 10 -> 10, of which waited for: 5 -> 4; matrix products, arithmetic and copies ran while one was open for 1% -> 1% of each run, Pallas kernels for 22% -> 13%
where the time goes in v2:
time: 179 us; the launch traced here: 178 us
  Pallas kernels  101 us (56%)
  starting transfers between devices  28.1 us (16%)
  waiting for transfers between devices  26.2 us (15%)
  blocking collectives  15.7 us (9%)
  local copies, waits for them, and re-layouts  5.3 us (3%)
    pallas_call x1, Pallas kernels, per_device(): pl.pallas_call(functools.partial(forward_kernel, plan), grid=(SECTIONS,),...  36.6 us
    pallas_call x1, Pallas kernels, per_device(): pl.pallas_call(functools.partial(backward_kernel, plan), grid=(SECTIONS,)...  23.3 us
    pallas_call x1, Pallas kernels, per_device(): call(target_kernel, [shape(window), shape(span)], [SMEM] + [VMEM] * (1 +...  18.1 us
    all_to_all x1, blocking collectives, everywhere(): return lax.all_to_all(array, ALL_AXES, 0, 0, tiled=True)  15.7 us
    all_to_all x3, waiting for transfers between devices, exchange(): return lax.all_to_all(array, GROUP, 0, 0, tiled=True)  14.5 us
    ppermute x6, starting transfers between devices, hop(): return lax.ppermute(array, ALL_AXES, pairs)  13.5 us
    all_to_all x3, starting transfers between devices, exchange(): return lax.all_to_all(array, GROUP, 0, 0, tiled=True)  12.1 us
    pallas_call x1, Pallas kernels, per_device(): call(grad_kernel, [shape(features.shape, bf16), shape((plan.ranks, 8, LAN...  9.33 us
  transfers between devices with their start and end apart: 10, of which 4 were waited for; matrix products, arithmetic and copies ran while one was open for 1% of the time, Pallas kernels for 13%

profile of v2, /device:TPU:0, one launch (start us, length us, event | category | flops | bytes accessed | tf_op | source)
XLA Modules:
  0.0 178.5 jit_solution(1756628408444425885)
XLA Ops:
  0.6 0.6 pad_add_fusion.pos_ref.refs_0_
  1.2 7.0 %shard_map.78 = f32[8,5,24,128]{3,2,1,0:T(8,128)} custom-call(s32[2]{0:T(128)} %pad_add_fusion.pos_ref.refs_0_, bf16[27,32]{1,0:T(8,128)(2,1)} %w_ref.1, bf16[32,16,16,128]{3,2,1,0:T(8,128)(2,1)} %f_ref.3), custom_call_target="tpu_custom_call" | custom-call | tf_op jit(solution)/shard_map/pallas_call | solution.py:750
  8.3 5.2 %all-to-all-start.1 = ((f32[8,5,24,128]{3,2,1,0:T(8,128)}), f32[8,5,24,128]{3,2,1,0:T(8,128)S(1)}, u32[]{:S(2)}, u32[]{:S(2)}) async-start(f32[8,5,24,128]{3,2,1,0:T(8,128)} %shard_map.78), calls=%async_computation.1 | async-start | bytes 983040 | tf_op jit(solution)/shard_map/all_to_all | solution.py:731
  13.5 1.7 shard_map.75
  15.1 6.8 %all-to-all-done.1.got_ref = f32[8,5,24,128]{3,2,1,0:T(8,128)S(1)} async-done(((f32[8,5,24,128]{3,2,1,0:T(8,128)}), f32[8,5,24,128]{3,2,1,0:T(8,128)S(1)}, u32[]{:S(2)}, u32[]{:S(2)}) %all-to-all-start.1) | async-done | bytes 491552 | tf_op jit(solution)/shard_map/all_to_all | solution.py:731
  21.9 3.4 %all-to-all-start = ((bf16[8,4,16,128]{3,2,1,0:T(8,128)(2,1)}), bf16[8,4,16,128]{3,2,1,0:T(8,128)(2,1)S(1)}, u32[]{:S(2)}, u32[]{:S(2)}) async-start(bf16[8,4,16,128]{3,2,1,0:T(8,128)(2,1)} %shard_map.75), calls=%async_computation | async-start | bytes 262144 | tf_op jit(solution)/shard_map/all_to_all | solution.py:731
  25.3 0.0 copy-done
  25.3 1.8 %shard_map.79 = (f32[288,128]{1,0:T(8,128)}, f32[160,128]{1,0:T(8,128)}, f32[160,128]{1,0:T(8,128)}) custom-call(f32[8,5,24,128]{3,2,1,0:T(8,128)} %copy-done), custom_call_target="tpu_custom_call" | custom-call | tf_op jit(solution)/shard_map/pallas_call | solution.py:778
  27.1 3.8 %collective-permute-start.2 = (f32[18,16,128]{2,1,0:T(8,128)}, f32[18,16,128]{2,1,0:T(8,128)S(1)}, u32[]{:S(2)}, u32[]{:S(2)}) collective-permute-start(f32[18,16,128]{2,1,0:T(8,128)} %bitcast.11), channel_id=1, source_target_pairs={{0,4},{4,8},{8,12},{12,16},{16,20},{20,24},{24,28},{28,1},{1,5},{5... | collective-permute-start | bytes 442376 | tf_op jit(solution)/shard_map/ppermute | solution.py:745
  30.9 1.3 collective-permute-start.4
  32.2 0.0 all-to-all-done.got_ref
  32.3 0.0 copy-start.2
  32.3 0.6 copy-done.2
  32.9 1.6 shard_map.76
  34.6 4.5 %collective-permute-start = (bf16[13,16,128]{2,1,0:T(8,128)(2,1)}, bf16[13,16,128]{2,1,0:T(8,128)(2,1)S(1)}, u32[]{:S(2)}, u32[]{:S(2)}) collective-permute-start(bf16[13,16,128]{2,1,0:T(8,128)(2,1)} %bitcast.19), channel_id=1, source_target_pairs={{0,4},{4,8},{8,12},{12,16},{16,20},{20,24},{24,28},{28,1},{1,5},{5... | collective-permute-start | bytes 159752 | tf_op jit(solution)/shard_map/ppermute | solution.py:745
  39.1 1.3 collective-permute-start.3
  40.4 1.3 collective-permute-start.5
  41.7 0.0 collective-permute-done.refs_2_
  41.7 0.0 copy-start.8
  41.7 1.3 collective-permute-start.1
  43.7 5.1 %collective-permute-done.1.refs_3_ = bf16[13,16,128]{2,1,0:T(8,128)(2,1)S(1)} collective-permute-done((bf16[13,16,128]{2,1,0:T(8,128)(2,1)}, bf16[13,16,128]{2,1,0:T(8,128)(2,1)S(1)}, u32[]{:S(2)}, u32[]{:S(2)}) %collective-permute-start.1) | collective-permute-done | bytes 53280 | tf_op jit(solution)/shard_map/ppermute | solution.py:745
  48.8 0.0 copy-done.8
  48.8 0.6 copy-done.9
  49.4 18.1 %shard_map.77 = (f32[42,16,128]{2,1,0:T(8,128)}, f32[18,16,128]{2,1,0:T(8,128)}) custom-call(s32[2]{0:T(128)} %pad_add_fusion.pos_ref.refs_0_, bf16[16,16,128]{2,1,0:T(8,128)(2,1)} %bitcast.14, bf16[13,16,128]{2,1,0:T(8,128)(2,1)} %copy-done.8, bf16[13,16,128]{2,1,0:T(8,128)(2,1)} %copy-done.9), custom_call_target="tpu_custom_call" | custom-call | tf_op jit(solution)/shard_map/pallas_call | solution.py:791
  67.5 0.0 collective-permute-done.3.refs_6_
  67.5 0.0 collective-permute-done.5.refs_8_
  67.5 0.0 copy-start.7
  67.5 0.0 collective-permute-done.2.refs_5_
  67.5 0.0 copy-start.4
  67.5 0.0 collective-permute-done.4.refs_7_
  67.5 0.0 copy-start.5
  67.6 0.6 copy-done.6
  68.1 0.0 copy-done.7
  68.2 0.0 copy-done.4
  68.2 0.0 copy-done.5
  68.2 36.6 %shard_map.80 = (f32[11,42,16,128]{3,2,1,0:T(8,128)}, f32[11,42,16,128]{3,2,1,0:T(8,128)}, f32[11,42,16,128]{3,2,1,0:T(8,128)}, f32[11,42,16,128]{3,2,1,0:T(8,12...) custom-call(s32[2]{0:T(128)} %pad_add_fusion.pos_ref.refs_0_, f32[1]{0:T(128)S(6)} %copy.9.refs_1_, ...), custom_call_target="tpu_custom_call" | custom-call | tf_op jit(solution)/shard_map/pallas_call | solution.py:804
  104.8 15.7 %all_to_all.25.refs_1_ = f32[32,8,128]{2,1,0:T(8,128)} all-to-all(f32[32,8,128]{2,1,0:T(8,128)} %get-tuple-element.32), channel_id=1, replica_groups=mesh['gx'=4,'gy'=2,'gz'=4] {'gx','gy','gz'}, dimensions={0} | all-to-all | bytes 262144 | tf_op jit(solution)/shard_map/all_to_all | solution.py:734
  120.5 23.3 %shard_map.81 = (f32[8,5,24,128]{3,2,1,0:T(8,128)}, f32[8,128]{1,0:T(8,128)}) custom-call(s32[2]{0:T(128)} %pad_add_fusion.pos_ref.refs_0_, f32[32,8,128]{2,1,0:T(8,128)} %all_to_all.25.refs_1_, f32[11,42,16,128]{3,2,1,0:T(8,128)} %get-tuple-element.33.refs_2_, f32[11,42,16,128]{3,2,1,0:T(8,128)} %get-tuple-element.34.refs_3_, ...), custom_call_target="tpu_custom_call" | custom-call | tf_op jit(solution)/shard_map/pallas_call | solution.py:825
  143.8 3.5 %all-to-all-start.3 = ((f32[8,5,24,128]{3,2,1,0:T(8,128)}), f32[8,5,24,128]{3,2,1,0:T(8,128)S(1)}, u32[]{:S(2)}, u32[]{:S(2)}) async-start(f32[8,5,24,128]{3,2,1,0:T(8,128)} %get-tuple-element.39), calls=%async_computation.3 | async-start | bytes 983040 | tf_op jit(solution)/shard_map/all_to_all | solution.py:731
  147.3 0.7 copy.8
  148.0 7.7 %all-to-all-done.3.got_ref = f32[8,5,24,128]{3,2,1,0:T(8,128)S(1)} async-done(((f32[8,5,24,128]{3,2,1,0:T(8,128)}), f32[8,5,24,128]{3,2,1,0:T(8,128)S(1)}, u32[]{:S(2)}, u32[]{:S(2)}) %all-to-all-start.3) | async-done | bytes 491552 | tf_op jit(solution)/shard_map/all_to_all | solution.py:731
  155.7 0.8 copy-done.1
  156.5 9.3 %shard_map.82 = (bf16[32,16,16,128]{3,2,1,0:T(8,128)(2,1)}, f32[32,8,128]{2,1,0:T(8,128)}) custom-call(s32[2]{0:T(128)} %pad_add_fusion.pos_ref.refs_0_, bf16[32,27]{1,0:T(8,128)(2,1)} %bitcast.15, bf16[32,16,16,128]{3,2,1,0:T(8,128)(2,1)} %f_ref.3, f32[8,5,24,128]{3,2,1,0:T(8,128)} %copy-done.1), custom_call_target="tpu_custom_call" | custom-call | tf_op jit(solution)/shard_map/pallas_call | solution.py:842
  165.8 2.6 %all-to-all-start.4 = ((f32[32,8,128]{2,1,0:T(8,128)}), f32[32,8,128]{2,1,0:T(8,128)S(1)}, u32[]{:S(2)}, u32[]{:S(2)}) async-start(f32[32,8,128]{2,1,0:T(8,128)} %get-tuple-element.41), calls=%async_computation.4 | async-start | bytes 262144 | tf_op jit(solution)/shard_map/all_to_all | solution.py:734
  168.4 1.2 slice.3
  169.6 6.6 %all-to-all-done.4.got_ref = f32[32,8,128]{2,1,0:T(8,128)S(1)} async-done(((f32[32,8,128]{2,1,0:T(8,128)}), f32[32,8,128]{2,1,0:T(8,128)S(1)}, u32[]{:S(2)}, u32[]{:S(2)}) %all-to-all-start.4) | async-done | bytes 131104 | tf_op jit(solution)/shard_map/all_to_all | solution.py:734
  176.2 0.6 copy-done.3
  176.9 1.6 shard_map.83
  (7 shorter events, 0.0 us)
Async XLA Ops:
  8.3 13.7 %all-to-all-start.1 = ((f32[8,5,24,128]{3,2,1,0:T(8,128)}), f32[8,5,24,128]{3,2,1,0:T(8,128)S(1)}, u32[]{:S(2)}, u32[]{:S(2)}) async-start(f32[8,5,24,128]{3,2,1,0:T(8,128)} %shard_map.78), calls=%async_computation.1 | async-start | bytes 983040 | tf_op jit(solution)/shard_map/all_to_all | solution.py:731
  21.9 3.4 %copy-start = (f32[8,5,24,128]{3,2,1,0:T(8,128)}, f32[8,5,24,128]{3,2,1,0:T(8,128)S(1)}, u32[]{:S(2)}) copy-start(f32[8,5,24,128]{3,2,1,0:T(8,128)S(1)} %all-to-all-done.1.got_ref) | copy-start | bytes 1474564
  21.9 10.3 %all-to-all-start = ((bf16[8,4,16,128]{3,2,1,0:T(8,128)(2,1)}), bf16[8,4,16,128]{3,2,1,0:T(8,128)(2,1)S(1)}, u32[]{:S(2)}, u32[]{:S(2)}) async-start(bf16[8,4,16,128]{3,2,1,0:T(8,128)(2,1)} %shard_map.75), calls=%async_computation | async-start | bytes 262144 | tf_op jit(solution)/shard_map/all_to_all | solution.py:731
  27.1 40.4 %collective-permute-start.2 = (f32[18,16,128]{2,1,0:T(8,128)}, f32[18,16,128]{2,1,0:T(8,128)S(1)}, u32[]{:S(2)}, u32[]{:S(2)}) collective-permute-start(f32[18,16,128]{2,1,0:T(8,128)} %bitcast.11), channel_id=1, source_target_pairs={{0,4},{4,8},{8,12},{12,16},{16,20},{20,24},{24,28},{28,1},{1,5},{5... | collective-permute-start | bytes 442376 | tf_op jit(solution)/shard_map/ppermute | solution.py:745
  30.9 36.6 %collective-permute-start.4 = (f32[18,16,128]{2,1,0:T(8,128)}, f32[18,16,128]{2,1,0:T(8,128)S(1)}, u32[]{:S(2)}, u32[]{:S(2)}) collective-permute-start(f32[18,16,128]{2,1,0:T(8,128)} %bitcast.12), channel_id=1, source_target_pairs={{4,0},{8,4},{12,8},{16,12},{20,16},{24,20},{28,24},{1,28},{5,1},{9... | collective-permute-start | bytes 442376 | tf_op jit(solution)/shard_map/ppermute | solution.py:745
  32.3 0.7 copy-start.2
  34.6 7.1 %collective-permute-start = (bf16[13,16,128]{2,1,0:T(8,128)(2,1)}, bf16[13,16,128]{2,1,0:T(8,128)(2,1)S(1)}, u32[]{:S(2)}, u32[]{:S(2)}) collective-permute-start(bf16[13,16,128]{2,1,0:T(8,128)(2,1)} %bitcast.19), channel_id=1, source_target_pairs={{0,4},{4,8},{8,12},{12,16},{16,20},{20,24},{24,28},{28,1},{1,5},{5... | collective-permute-start | bytes 159752 | tf_op jit(solution)/shard_map/ppermute | solution.py:745
  39.1 28.4 %collective-permute-start.3 = (f32[10,16,128]{2,1,0:T(8,128)}, f32[10,16,128]{2,1,0:T(8,128)S(1)}, u32[]{:S(2)}, u32[]{:S(2)}) collective-permute-start(f32[10,16,128]{2,1,0:T(8,128)} %bitcast.17), channel_id=1, source_target_pairs={{0,8},{4,12},{8,16},{12,20},{16,24},{20,28},{24,1},{28,5},{1,9},{5... | collective-permute-start | bytes 245768 | tf_op jit(solution)/shard_map/ppermute | solution.py:745
  40.4 27.1 %collective-permute-start.5 = (f32[10,16,128]{2,1,0:T(8,128)}, f32[10,16,128]{2,1,0:T(8,128)S(1)}, u32[]{:S(2)}, u32[]{:S(2)}) collective-permute-start(f32[10,16,128]{2,1,0:T(8,128)} %bitcast.16), channel_id=1, source_target_pairs={{8,0},{12,4},{16,8},{20,12},{24,16},{28,20},{1,24},{5,28},{9,1},{1... | collective-permute-start | bytes 245768 | tf_op jit(solution)/shard_map/ppermute | solution.py:745
  41.7 7.1 %copy-start.8 = (bf16[13,16,128]{2,1,0:T(8,128)(2,1)}, bf16[13,16,128]{2,1,0:T(8,128)(2,1)S(1)}, u32[]{:S(2)}) copy-start(bf16[13,16,128]{2,1,0:T(8,128)(2,1)S(1)} %collective-permute-done.refs_2_) | copy-start | bytes 159748
  41.7 7.1 %collective-permute-start.1 = (bf16[13,16,128]{2,1,0:T(8,128)(2,1)}, bf16[13,16,128]{2,1,0:T(8,128)(2,1)S(1)}, u32[]{:S(2)}, u32[]{:S(2)}) collective-permute-start(bf16[13,16,128]{2,1,0:T(8,128)(2,1)} %bitcast.18), channel_id=1, source_target_pairs={{4,0},{8,4},{12,8},{16,12},{20,16},{24,20},{28,24},{1,28},{5,1},{9... | collective-permute-start | bytes 159752 | tf_op jit(solution)/shard_map/ppermute | solution.py:745
  48.8 0.6 copy-start.9
  67.5 0.6 copy-start.6
  67.5 0.7 copy-start.7
  67.5 0.7 copy-start.4
  67.5 0.7 copy-start.5
  120.5 26.8 %copy-start.10 = (bf16[27,32]{1,0:T(8,128)(2,1)S(1)}, bf16[27,32]{1,0:T(8,128)(2,1)}, u32[]{:S(2)}) copy-start(bf16[27,32]{1,0:T(8,128)(2,1)} %w_ref.1) | copy-start | bytes 5188
  143.8 11.9 %all-to-all-start.3 = ((f32[8,5,24,128]{3,2,1,0:T(8,128)}), f32[8,5,24,128]{3,2,1,0:T(8,128)S(1)}, u32[]{:S(2)}, u32[]{:S(2)}) async-start(f32[8,5,24,128]{3,2,1,0:T(8,128)} %get-tuple-element.39), calls=%async_computation.3 | async-start | bytes 983040 | tf_op jit(solution)/shard_map/all_to_all | solution.py:731
  155.7 0.8 copy-start.1
  165.8 10.4 %all-to-all-start.4 = ((f32[32,8,128]{2,1,0:T(8,128)}), f32[32,8,128]{2,1,0:T(8,128)S(1)}, u32[]{:S(2)}, u32[]{:S(2)}) async-start(f32[32,8,128]{2,1,0:T(8,128)} %get-tuple-element.41), calls=%async_computation.4 | async-start | bytes 262144 | tf_op jit(solution)/shard_map/all_to_all | solution.py:734
  176.2 0.7 copy-start.3

commit v3 on v2

--- a/solution.py
+++ b/solution.py
@@ -44,7 +44,10 @@
         self.own = self.nx // self.per
         self.shared = self.per > 1
         self.sent = self.own + (1 if self.shared else 2)
-        self.R = up8(self.zc + 2)
+        self.R = up8(self.zc)
+        self.extra = -(-2 * self.sent // self.R)
+        self.R16 = -(-self.zc // 16) * 16
+        self.extra16 = -(-2 * self.sent // self.R16)
         self.pad = self.tiles + 16
         self.win = self.zc + 2 * REACH
         self.span = self.zc + 2
@@ -58,7 +61,7 @@
         self.label_rest = REACH - (self.label_hops - 1) * self.zc
 
     def blocks_of(self, count):
-        fits = [n for n in range(1, count + 1) if count % n == 0 and n * self.tiles <= 128]
+        fits = [n for n in range(1, count + 1) if count % n == 0 and n * self.tiles <= 256]
         return fits[-1] if fits else 1
 
     def slot(self, x):
@@ -119,7 +122,7 @@
     z = rank * plan.zc + plane
     inside = (z >= 0) & (z < plan.Z)
     edge = (z == 0) | (z == plan.Z - 1)
-    return jnp.where(inside, jnp.where(edge, 1, 2), 0)
+    return jnp.where(inside, jnp.where(edge, 1, 2), 0), jnp.where(inside, 0.0, 1.0)
 
 
 def store_all(pairs):
@@ -141,7 +144,8 @@
     return own + member_y * plan.ny - y + 1
 
 
-def conv_kernel(plan, pos_ref, w_ref, f_ref, out_ref, wide_ref, acc_ref):
+def conv_kernel(plan, pos_ref, w_ref, f_ref, label_ref, out_ref, wide_ref, acc_ref):
+    del label_ref
     rows, inner = plan.Y, plan.ch * plan.ny
     spread = (
         lax.broadcasted_iota(jnp.int32, (plan.ch, inner), 0)
@@ -194,8 +198,10 @@
         spill = jnp.concatenate(spills, axis=0).T
         for p in range(plan.members):
             out_ref[p, tile, 0 : plan.zc] = turned[p * plan.zc : (p + 1) * plan.zc]
-        out_ref[0, tile, plan.zc : plan.zc + 1] = spill[0:1]
-        out_ref[plan.members - 1, tile, plan.zc + 1 : plan.zc + 2] = spill[1:2]
+        for end, p in ((0, 0), (1, plan.members - 1)):
+            n = 2 * tile + end
+            at = plan.sent + n // plan.R
+            out_ref[p, at, n % plan.R : n % plan.R + 1] = spill[end : end + 1]
 
 
 def label_kernel(plan, pos_ref, l_ref, out_ref):
@@ -213,21 +219,33 @@
 
 
 def gather_kernel(plan, got_ref, out_ref, head_ref, tail_ref):
-    lane = lane_iota((plan.R, LANES))
     tiles, zc, rest = plan.tiles, plan.zc, plan.rest
+    lane = lane_iota((1, LANES))
+
+    def part(p, q):
+        values = [got_ref[p, q, 0:zc]]
+        for end in range(2):
+            n = 2 * q + end
+            at = plan.sent + n // plan.R
+            values.append(got_ref[p, at, n % plan.R : n % plan.R + 1])
+        return values
+
     for a in range(plan.gx):
         for q in range(plan.own):
-            total = jnp.zeros((plan.R, LANES), f32)
+            parts = []
             for b in range(plan.gy):
-                total = total + got_ref[a * plan.gy + b, q]
+                parts.append(part(a * plan.gy + b, q))
                 if q == plan.own - 1 and a < plan.gx - 1:
-                    edge = got_ref[(a + 1) * plan.gy + b, plan.sent - 1]
-                    total = total + jnp.where(lane >= LANES - plan.Y, edge, 0.0)
+                    edge = part((a + 1) * plan.gy + b, plan.sent - 1)
+                    parts.append([jnp.where(lane >= LANES - plan.Y, v, 0.0) for v in edge])
                 if q == 0 and a > 0:
-                    edge = got_ref[(a - 1) * plan.gy + b, plan.own]
-                    total = total + jnp.where(lane < plan.Y, edge, 0.0)
+                    edge = part((a - 1) * plan.gy + b, plan.own)
+                    parts.append([jnp.where(lane < plan.Y, v, 0.0) for v in edge])
+            whole, low, high = (functools.reduce(jnp.add, vs) for vs in zip(*parts))
             tile = a * plan.own + q
-            out_ref[pl.ds(tile, zc + 2, stride=tiles)] = total[: zc + 2]
+            out_ref[pl.ds(tile, zc, stride=tiles)] = whole
+            out_ref[zc * tiles + tile : zc * tiles + tile + 1] = low
+            out_ref[(zc + 1) * tiles + tile : (zc + 1) * tiles + tile + 1] = high
     head_ref[: rest * tiles] = out_ref[: rest * tiles]
     head_ref[rest * tiles :] = out_ref[zc * tiles : (zc + 1) * tiles]
     tail_ref[: rest * tiles] = out_ref[(zc - rest) * tiles : zc * tiles]
@@ -247,22 +265,23 @@
     tail_ref[...] = all_ref[(zc - rest) * tiles :].astype(bf16)
 
 
-def thin(e, box, inverse, s):
-    ok = (e > 0.0) & (box > 0.0) & (inverse > 0.0)
-    box = jnp.where(ok, box, 1.0)
-    ratio = jnp.where(ok, e * box * inverse, 1.0)
+LOG = 1.0 / sharpness
+
+
+def thin(e, box, inverse, outside):
+    box = box + outside
+    ratio = e * box * inverse + outside
     square = ratio * ratio
     more = 1.0 + square
     joint = 1.0 / (box * more)
     slope = joint * box
-    scaled = -jnp.log(square * slope)
-    lift = scaled * (1.0 - s)
-    small = jnp.exp(-jnp.abs(lift))
-    part = 1.0 / (1.0 + small)
-    rate = jnp.where(lift >= 0.0, part, small * part)
-    grown = s + (jnp.maximum(lift, 0.0) - jnp.log(part)) * (1.0 / sharpness)
-    thinned = scaled * (1.0 / sharpness)
-    return ok, slope, joint * more, rate, thinned, grown
+    return joint * more, slope, jnp.log(square * slope)
+
+
+def lift(scaled, s):
+    small = jnp.exp(scaled * (s - 1.0))
+    more = 1.0 + small
+    return s + jnp.log(more) * LOG, small * (1.0 / more)
 
 
 def erode(plan, rank, mask, e_ref, g_ref, table_ref, now, base, first, count, size):
@@ -279,9 +298,10 @@
 
             total = cur + e_ref[now, at - 1, tiles] + e_ref[now, at + 1, tiles]
             total = total + x_neighbours(plan, mask, load, cur) + y_neighbours(plan, mask, cur)
-            total = total * table_ref[kind_of(plan, rank, plane + n)]
+            kind, outside = kind_of(plan, rank, plane + n)
+            total = total * table_ref[kind]
             out.append((e_ref, (1 - now, at, tiles), total))
-            out.append((g_ref, (1 - now, at), jnp.where(total > 0.0, 1.0 / total, 0.0)))
+            out.append((g_ref, (1 - now, at), 1.0 / (total + outside) - outside))
         store_all(out)
 
     over(first, count, size, body)
@@ -354,18 +374,26 @@
         )
         spread(plan, mask, g_ref, 1 - now, zy_ref, base, -1, span, size)
 
-        def point(plane):
+        def point(plane, opening):
             out = []
             for n in range(size):
                 at = plane + n
                 box = x_box(plan, mask, zy_ref, at)
-                s = jnp.where(step == 0, 0.0, ts_ref[at])
-                inverse = box_ref[kind_of(plan, rank, at - 1)]
-                result = thin(e_ref[now, at - 1 + base, tiles], box, inverse, s)
-                out.append((ts_ref, at, jnp.where(step == 0, result[4], result[5])))
+                kind, outside = kind_of(plan, rank, at - 1)
+                e = e_ref[now, at - 1 + base, tiles]
+                _, _, scaled = thin(e, box, box_ref[kind], outside)
+                value = scaled * -LOG if opening else lift(scaled, ts_ref[at])[0]
+                out.append((ts_ref, at, value))
             store_all(out)
 
-        over(0, span, size, point)
+        @pl.when(step == 0)
+        def _():
+            over(0, span, size, lambda plane: point(plane, True))
+
+        @pl.when(step > 0)
+        def _():
+            over(0, span, size, lambda plane: point(plane, False))
+
         return carry
 
     lax.fori_loop(0, SECTIONS, section, 0)
@@ -427,6 +455,7 @@
                 inside = ((z >= 0) & (z < plan.Z)).astype(f32)
                 predict = sigmoid(e_ref[0, at, tiles] + bias_ref[0])
                 out.append((e_ref, (0, at, tiles), jnp.exp(-temper * predict) * inside))
+                out.append((g_ref, (0, at), jnp.exp(temper * predict) * inside))
             store_all(out)
 
         over(1, zc + 2 * HALO, size, fill)
@@ -435,30 +464,37 @@
     reach = REACH + 1 + ITERS - step
     erode(plan, rank, mask, e_ref, g_ref, cross_ref, now, base, -reach, zc + 2 * reach, size)
     spread(plan, mask, g_ref, 1 - now, zy_ref, base, -REACH, plan.win, size)
-    opening = step == 0
-
-    def point(at):
+    def point(at, opening):
         out = []
         for n in range(size):
             spot = at + n
             plane = spot - REACH
+            box = x_box(plan, mask, zy_ref, spot)
+            kind, outside = kind_of(plan, rank, plane)
             e = e_ref[now, plane + base, tiles]
-            s = s_ref[spot]
-            box = x_box(plan, mask, zy_ref, spot)
-            inverse = box_ref[kind_of(plan, rank, plane)]
-            ok, slope, over_box, rate, thinned, grown = thin(e, box, inverse, s)
-            a = jnp.where(opening, slope, rate * (1.0 - s) * slope)
-            a = jnp.where(ok, a, 0.0)
-            before = jnp.where(opening, jnp.where(e > 0.0, 1.0 / e, 0.0), g_ref[now, plane + base])
+            over_box, slope, scaled = thin(e, box, box_ref[kind], outside)
+            if opening:
+                grown, a = scaled * -LOG, slope
+            else:
+                s = s_ref[spot]
+                grown, rate = lift(scaled, s)
+                a = rate * (1.0 - s) * slope
+                out.append((m_ref, (0, spot), 1.0 + rate * scaled * LOG))
             after = g_ref[1 - now, plane + base]
-            out.append((s_ref, spot, jnp.where(opening, thinned, grown)))
-            out.append((m_ref, (0, spot), 1.0 - rate * thinned))
+            out.append((s_ref, spot, grown))
             out.append((q_ref, (0, spot), a * over_box))
-            out.append((t_ref, (0, spot), a * before))
+            out.append((t_ref, (0, spot), a * g_ref[now, plane + base]))
             out.append((g2_ref, (0, spot), after * after))
         store_all(out)
 
-    over(0, plan.win, size, point)
+    @pl.when(step == 0)
+    def _():
+        over(0, plan.win, size, lambda at: point(at, True))
+        m_ref[...] = jnp.ones_like(m_ref)
+
+    @pl.when(step > 0)
+    def _():
+        over(0, plan.win, size, lambda at: point(at, False))
 
     @pl.when(step == SECTIONS - 1)
     def _():
@@ -480,7 +516,7 @@
 def backward_kernel(plan, *refs):
     (
         pos_ref, sums_ref, m_ref, q_ref, t_ref, g2_ref, p_ref, target_ref, ts_ref,
-        out_ref, loss_ref,
+        out_ref, loss_ref, bias_ref,
         w_ref, h_ref, zy_ref, pull_ref, cross_ref, grad_ref,
     ) = refs
     step = pl.program_id(0)
@@ -500,7 +536,10 @@
         pull_ref[...] = jnp.zeros_like(pull_ref)
         h_ref[...] = jnp.zeros_like(h_ref)
         count_tables(plan, cross_ref, None)
-        w_ref[...] = target_ref[...] - prec[None]
+        for n in range(win):
+            z = rank * zc + n - REACH
+            inside = ((z >= 0) & (z < plan.Z)).astype(f32)
+            w_ref[n] = (target_ref[n] - prec) * inside
 
     def within(reach, body):
         count = (zc + 2 * reach + size - 1) // size
@@ -528,7 +567,7 @@
         for n in range(size):
             spot = at + n
             box = x_box(plan, mask, zy_ref, spot)
-            inverse = cross_ref[kind_of(plan, rank, spot - REACH)]
+            inverse = cross_ref[kind_of(plan, rank, spot - REACH)[0]]
             value = (h_ref[spot] - g2_ref[0, spot] * box) * inverse
             out.append((pull_ref, (spot + 1, tiles), value))
         store_all(out)
@@ -565,7 +604,7 @@
         l4 = -1.0 / volume
         l5 = 0.5 * (2.0 * s5 + 1.0) / (volume * volume)
 
-        def finish(n, carry):
+        def finish(n, total):
             z = rank * zc + n - 1
             inside = ((z >= 0) & (z < plan.Z)).astype(f32)
             at = n + REACH - 1
@@ -574,11 +613,12 @@
             whole = skel + l2 * ts_ref[n] + l4 * target_ref[at] + l5
             grad = whole * predict * (1.0 - predict) * inside
             grad_ref[pl.ds(pl.multiple_of(n * plan.tiles, 8), plan.tiles)] = grad
-            return carry
-
-        lax.fori_loop(0, plan.span, finish, 0)
-        lane = lane_iota((zc, LANES))
-        fill = plan.R - zc - 2
+            mine = ((n >= 1) & (n <= zc)).astype(f32)
+            return total + grad * mine
+
+        total = lax.fori_loop(0, plan.span, finish, jnp.zeros((plan.tiles, LANES), f32))
+        bias_ref[...] = jnp.sum(total.reshape(-1, 8, LANES), axis=0)
+        lane = lane_iota((1, LANES))
 
         def column(tile):
             return [
@@ -587,81 +627,67 @@
                 grad_ref[(zc + 1) * plan.tiles + tile : (zc + 1) * plan.tiles + tile + 1],
             ]
 
-        def place(a, q, pieces):
-            for b in range(plan.gy):
-                p = a * plan.gy + b
-                out_ref[p, q, 0:zc] = pieces[0]
-                out_ref[p, q, zc : zc + 1] = pieces[1]
-                out_ref[p, q, zc + 1 : zc + 2] = pieces[2]
-                if fill:
-                    out_ref[p, q, zc + 2 :] = jnp.zeros((fill, LANES), f32)
-
         for a in range(plan.gx):
-            for q in range(plan.own):
-                place(a, q, column(a * plan.own + q))
+            pieces = [column(a * plan.own + q) for q in range(plan.own)]
             zero = [jnp.zeros((zc, LANES), f32)] + [jnp.zeros((1, LANES), f32)] * 2
             after = column((a + 1) * plan.own) if a < plan.gx - 1 else zero
             before = column(a * plan.own - 1) if a > 0 else zero
             if plan.shared:
-                edge = [
-                    jnp.where(lane[: x.shape[0]] < plan.Y, x, 0.0)
-                    + jnp.where(lane[: y.shape[0]] >= LANES - plan.Y, y, 0.0)
-                    for x, y in zip(after, before)
-                ]
-                place(a, plan.own, edge)
+                pieces.append(
+                    [
+                        jnp.where(lane < plan.Y, x, 0.0)
+                        + jnp.where(lane >= LANES - plan.Y, y, 0.0)
+                        for x, y in zip(after, before)
+                    ]
+                )
             else:
-                place(a, plan.own, after)
-                place(a, plan.own + 1, before)
-
-
-def grad_kernel(plan, pos_ref, wt_ref, f_ref, got_ref, gf_ref, gw_ref, wide_ref, g_ref, dw_ref):
-    rows, inner, bands = plan.Y, plan.ch * plan.ny, 9 * plan.Y
-    spread = (
-        lax.broadcasted_iota(jnp.int32, (inner, plan.ch), 0) // plan.ny
-        == lax.broadcasted_iota(jnp.int32, (inner, plan.ch), 1)
-    ).astype(f32)
-    tap_y = tap_condition(plan, pos_ref[1], (inner, bands), 1, 0)
-    wide = jnp.zeros((inner, bands), f32)
-    tap = lax.broadcasted_iota(jnp.int32, (27, bands), 0)
-    band = lax.broadcasted_iota(jnp.int32, (27, bands), 1) // rows
-    for j in range(3):
-        pick = (tap == 9 * (band // 3) + 3 * j + band % 3).astype(f32)
-        chosen = jnp.dot(wt_ref[...].astype(f32), pick, preferred_element_type=f32)
-        full = jnp.dot(spread, chosen, preferred_element_type=f32)
-        wide = jnp.where(tap_y == j, full, wide)
-    wide_ref[...] = wide.astype(bf16)
-
-    zc = plan.zc
-    lane = lane_iota((rows, plan.nz))
-    bias = jnp.zeros((rows, plan.nz), f32)
+                pieces += [after, before]
+            edges = [edge for piece in pieces for edge in piece[1:]]
+            rows = plan.R16
+            edges += [jnp.zeros((1, LANES), f32)] * (plan.extra16 * rows - len(edges))
+            whole = [piece[0] for piece in pieces]
+            if rows > zc:
+                fill = jnp.zeros((rows - zc, LANES), f32)
+                whole = [jnp.concatenate([piece, fill], axis=0) for piece in whole]
+            whole += [
+                jnp.concatenate(edges[n * rows : (n + 1) * rows], axis=0)
+                for n in range(plan.extra16)
+            ]
+            for q, piece in enumerate(whole):
+                piece = piece.astype(bf16)
+                for b in range(plan.gy):
+                    out_ref[a * plan.gy + b, q] = piece
+
+
+def weight_kernel(plan, pos_ref, f_ref, bias_ref, got_ref, gw_ref, g_ref, dw_ref):
+    rows, inner = plan.Y, plan.ch * plan.ny
+    zc, nz = plan.zc, plan.nz
+    lane = lane_iota((rows, nz))
     places = {}
     for x in range(-1, plan.nx + 1):
         tile, first = plan.slot(x)
         places.setdefault(tile, {})[first] = x
     for tile in range(plan.sent):
-        stack = [got_ref[p, tile, 0:zc] for p in range(plan.members)]
+        stack = [got_ref[p, tile].astype(f32)[:zc] for p in range(plan.members)]
         turned = jnp.concatenate(stack, axis=0).T
-        low = got_ref[0, tile, zc : zc + 1]
-        high = got_ref[plan.members - 1, tile, zc + 1 : zc + 2]
-        ends = jnp.concatenate([low, high, jnp.zeros((LANES - 2, LANES), f32)], axis=0).T
+        ends = []
+        for end, p in ((0, 0), (1, plan.members - 1)):
+            n = 2 * tile + end
+            row = got_ref[p, plan.sent + n // plan.R16].astype(f32)
+            ends.append(row[n % plan.R16 : n % plan.R16 + 1])
+        ends = jnp.concatenate(ends + [jnp.zeros((LANES - 2, LANES), f32)], axis=0).T
         for first, x in places[tile].items():
             g = turned[first : first + rows]
             end = ends[first : first + rows]
-            down = jnp.where(lane == plan.nz - 1, pltpu.roll(end, plan.nz - 2, 1), pltpu.roll(g, plan.nz - 1, 1))
+            down = jnp.where(lane == nz - 1, pltpu.roll(end, nz - 2, 1), pltpu.roll(g, nz - 1, 1))
             up = jnp.where(lane == 0, end, pltpu.roll(g, 1, 1))
             g_ref[x + 1] = jnp.concatenate([down, g, up], axis=0).astype(bf16)
-            if 0 <= x < plan.nx:
-                bias = bias + g
-    y_own = lax.broadcasted_iota(jnp.int32, (rows, plan.nz), 0) // plan.ny == pos_ref[1]
-    bias = jnp.sum(jnp.where(y_own, bias, 0.0))
 
     dw_ref[...] = jnp.zeros_like(dw_ref)
 
     def at_x(x, carry):
-        block = f_ref[:, x].reshape(inner, plan.nz)
+        block = f_ref[:, x].reshape(inner, nz)
         moved = jnp.concatenate([g_ref[x + 2], g_ref[x + 1], g_ref[x]], axis=0)
-        out = jnp.dot(wide_ref[...], moved, preferred_element_type=f32)
-        gf_ref[:, x] = out.astype(bf16).reshape(plan.ch, plan.ny, plan.nz)
         dw_ref[...] += lax.dot_general(
             moved, block, (((1,), (1,)), ((), ())), preferred_element_type=f32
         )
@@ -689,8 +715,35 @@
             preferred_element_type=f32,
         )
     spot = (row_iota((8, LANES)) == 3) & (lane_iota((8, LANES)) == 96)
-    total = jnp.where(spot, bias, total)
+    total = jnp.where(spot, jnp.sum(bias_ref[...]), total)
     gw_ref[...] = jnp.broadcast_to(total[None], (plan.ranks, 8, LANES))
+
+
+def feature_kernel(plan, pos_ref, wt_ref, g_ref, after_ref, gf_ref, wide_ref):
+    del after_ref
+    rows, inner, bands = plan.Y, plan.ch * plan.ny, 9 * plan.Y
+    spread = (
+        lax.broadcasted_iota(jnp.int32, (inner, plan.ch), 0) // plan.ny
+        == lax.broadcasted_iota(jnp.int32, (inner, plan.ch), 1)
+    ).astype(f32)
+    tap_y = tap_condition(plan, pos_ref[1], (inner, bands), 1, 0)
+    wide = jnp.zeros((inner, bands), f32)
+    tap = lax.broadcasted_iota(jnp.int32, (27, bands), 0)
+    band = lax.broadcasted_iota(jnp.int32, (27, bands), 1) // rows
+    for j in range(3):
+        pick = (tap == 9 * (band // 3) + 3 * j + band % 3).astype(f32)
+        chosen = jnp.dot(wt_ref[...].astype(f32), pick, preferred_element_type=f32)
+        full = jnp.dot(spread, chosen, preferred_element_type=f32)
+        wide = jnp.where(tap_y == j, full, wide)
+    wide_ref[...] = wide.astype(bf16)
+
+    def at_x(x, carry):
+        moved = jnp.concatenate([g_ref[x + 2], g_ref[x + 1], g_ref[x]], axis=0)
+        out = jnp.dot(wide_ref[...], moved, preferred_element_type=f32)
+        gf_ref[:, x] = out.astype(bf16).reshape(plan.ch, plan.ny, plan.nz)
+        return carry
+
+    lax.fori_loop(0, plan.nx, at_x, 0)
 
 
 def final_kernel(plan, got_ref, gw_ref, gb_ref):
@@ -703,29 +756,55 @@
 
 VMEM = pl.BlockSpec(memory_space=pltpu.VMEM)
 SMEM = pl.BlockSpec(memory_space=pltpu.SMEM)
-BIG = pltpu.CompilerParams(vmem_limit_bytes=63 * 1024 * 1024)
+ANY = pl.BlockSpec(memory_space=pl.ANY)
+MIB = 1024 * 1024
 
 
 def shape(dims, dtype=f32):
     return jax.ShapeDtypeStruct(dims, dtype)
 
 
+def held(dims, dtype):
+    if len(dims) < 2:
+        return 4096
+    size = jnp.dtype(dtype).itemsize
+    rows = 8 * 4 // size
+    total = -(-dims[-2] // rows) * rows * -(-dims[-1] // LANES) * LANES * size
+    for n in dims[:-2]:
+        total *= n
+    return total
+
+
+def limits(arrays, scratch, micros):
+    total = sum(held(a.shape, a.dtype) for a in arrays)
+    total += sum(held(a.shape, a.dtype) for a in scratch)
+    limit = min(63 * MIB, total + total // 8 + 4 * MIB)
+    return dict(
+        compiler_params=pltpu.CompilerParams(vmem_limit_bytes=limit),
+        cost_estimate=pl.CostEstimate(
+            flops=0, transcendentals=0, bytes_accessed=int(micros * 2.5e6)
+        ),
+    )
+
+
 def per_device(mesh_shape, features, weight, bias, label):
     plan = Plan(mesh_shape, features.shape)
-    members, sent, own, R, tiles = plan.members, plan.sent, plan.own, plan.R, plan.tiles
+    members, sent, own, tiles = plan.members, plan.sent, plan.own, plan.tiles
     inner, bands = plan.ch * plan.ny, 9 * plan.Y
     place = (lax.axis_index("gz") * members + lax.axis_index(GROUP)).astype(jnp.int32)
     pos = jnp.stack([place, lax.axis_index("gy").astype(jnp.int32)])
 
-    def call(kernel, out_shape, in_specs, scratch=(), params=BIG):
+    def call(kernel, out_shape, in_specs, operands, micros, scratch=()):
+        outs = jax.tree.leaves(out_shape)
+        ins = [a for spec, a in zip(in_specs, operands) if spec is VMEM]
         return pl.pallas_call(
             functools.partial(kernel, plan),
             out_shape=out_shape,
             in_specs=in_specs,
             out_specs=jax.tree.map(lambda s: VMEM, out_shape),
             scratch_shapes=list(scratch),
-            compiler_params=params,
-        )
+            **limits(ins + outs, scratch, micros),
+        )(*operands)
 
     def exchange(array):
         return lax.all_to_all(array, GROUP, 0, 0, tiled=True)
@@ -744,18 +823,21 @@
         ]
         return lax.ppermute(array, ALL_AXES, pairs)
 
-    label_sent = call(label_kernel, shape((members, own, plan.zc, LANES), bf16), [SMEM, VMEM])(
-        pos, label
+    label_sent = call(
+        label_kernel, shape((members, own, plan.zc, LANES), bf16), [SMEM, VMEM], (pos, label), 1.5
     )
     sent_logits = call(
         conv_kernel,
-        shape((members, sent, R, LANES)),
-        [SMEM, VMEM, VMEM],
+        shape((members, sent + plan.extra, plan.R, LANES)),
+        [SMEM, VMEM, VMEM, ANY],
+        (pos, weight, features, label_sent),
+        7,
         [
             pltpu.VMEM((bands, inner), bf16),
             pltpu.VMEM((plan.nx + 2, 3 * plan.Y, plan.nz), f32),
         ],
-    )(pos, weight, features)
+    )
+
     def planes(array):
         return array.reshape(-1, tiles, LANES)
 
@@ -771,15 +853,19 @@
         label_gather_kernel,
         [shape((zc * tiles, LANES), bf16)] + [shape((short, LANES), bf16)] * 2,
         [VMEM],
+        (exchange(label_sent),),
+        1.5,
         [pltpu.VMEM((zc * tiles, LANES), f32)],
-    )(exchange(label_sent))
+    )
     label_parts = [planes(part) for part in label_parts]
     short = (plan.rest + 1) * tiles
     parts = call(
         gather_kernel,
         [shape(((zc + 2) * tiles, LANES))] + [shape((short, LANES))] * 2,
         [VMEM],
-    )(exchange(sent_logits))
+        (exchange(sent_logits),),
+        1.5,
+    )
     parts = [planes(part) for part in parts]
     around = hops_of(parts, plan.hops)
     label_around = hops_of(label_parts, plan.label_hops)
@@ -792,6 +878,8 @@
         target_kernel,
         [shape(window), shape(span)],
         [SMEM] + [VMEM] * (1 + 2 * plan.label_hops),
+        (pos, label_parts[0], *label_around),
+        14,
         [
             pltpu.VMEM((2, room, plan.pad, LANES), f32),
             pltpu.VMEM((2, room, tiles, LANES), f32),
@@ -799,59 +887,80 @@
             table,
             table,
         ],
-    )(pos, label_parts[0], *label_around)
+    )
     record = pl.BlockSpec((1,) + window, lambda n: (n, 0, 0, 0))
+    operands = (pos, bias, target, ts, parts[0], *around)
+    scratch = [
+        pltpu.VMEM((2, plan.planes, plan.pad, LANES), f32),
+        pltpu.VMEM((2, plan.planes, tiles, LANES), f32),
+        pltpu.VMEM((plan.win, plan.pad, LANES), f32),
+        pltpu.VMEM(window, f32),
+        table,
+        table,
+    ]
+    small = [shape(span), shape((plan.ranks, 8, LANES))]
     outs = pl.pallas_call(
         functools.partial(forward_kernel, plan),
         grid=(SECTIONS,),
-        out_shape=[shape((SECTIONS,) + window)] * 4
-        + [shape(span), shape((plan.ranks, 8, LANES))],
-        in_specs=[SMEM, SMEM] + [VMEM] * (3 + 2 * plan.hops),
+        out_shape=[shape((SECTIONS,) + window)] * 4 + small,
+        in_specs=[SMEM, SMEM] + [VMEM] * (len(operands) - 2),
         out_specs=[record] * 4 + [VMEM] * 2,
-        scratch_shapes=[
-            pltpu.VMEM((2, plan.planes, plan.pad, LANES), f32),
-            pltpu.VMEM((2, plan.planes, tiles, LANES), f32),
-            pltpu.VMEM((plan.win, plan.pad, LANES), f32),
-            pltpu.VMEM(window, f32),
-            table,
-            table,
-        ],
-        compiler_params=BIG,
-    )(pos, bias, target, ts, parts[0], *around)
+        scratch_shapes=scratch,
+        **limits([shape(window)] * 8 + small + list(operands[2:]), scratch, 25),
+    )(*operands)
     m, q, t, g2, predict, sums = outs
     sums = everywhere(sums)
 
     back = pl.BlockSpec((1,) + window, lambda n: (SECTIONS - 1 - n, 0, 0, 0))
-    grad_sent, loss = pl.pallas_call(
+    operands = (pos, sums, m, q, t, g2, predict, target, ts)
+    scratch = [
+        pltpu.VMEM(window, f32),
+        pltpu.VMEM(window, f32),
+        pltpu.VMEM((plan.win, plan.pad, LANES), f32),
+        pltpu.VMEM((plan.win + 2, plan.pad, LANES), f32),
+        table,
+        pltpu.VMEM((plan.span * tiles, LANES), f32),
+    ]
+    outs = [
+        shape((members, sent + plan.extra16, plan.R16, LANES), bf16),
+        shape((8, LANES)),
+        shape((8, LANES)),
+    ]
+    arrays = [shape(window)] * 8 + outs + [sums, predict, target, ts]
+    grad_sent, loss, bias_part = pl.pallas_call(
         functools.partial(backward_kernel, plan),
         grid=(SECTIONS,),
-        out_shape=[shape((members, sent, R, LANES)), shape((8, LANES))],
+        out_shape=outs,
         in_specs=[SMEM, VMEM] + [back] * 4 + [VMEM] * 3,
-        out_specs=[VMEM, VMEM],
-        scratch_shapes=[
-            pltpu.VMEM(window, f32),
-            pltpu.VMEM(window, f32),
-            pltpu.VMEM((plan.win, plan.pad, LANES), f32),
-            pltpu.VMEM((plan.win + 2, plan.pad, LANES), f32),
-            table,
-            pltpu.VMEM((plan.span * tiles, LANES), f32),
-        ],
-        compiler_params=BIG,
-    )(pos, sums, m, q, t, g2, predict, target, ts)
-
-    grad_features, partial = call(
-        grad_kernel,
-        [shape(features.shape, bf16), shape((plan.ranks, 8, LANES))],
+        out_specs=[VMEM] * 3,
+        scratch_shapes=scratch,
+        **limits(arrays, scratch, 20),
+    )(*operands)
+
+    moved = shape((plan.nx + 2, 3 * plan.Y, plan.nz), bf16)
+    partial, g = call(
+        weight_kernel,
+        [shape((plan.ranks, 8, LANES)), moved],
         [SMEM, VMEM, VMEM, VMEM],
-        [
-            pltpu.VMEM((inner, bands), bf16),
-            pltpu.VMEM((plan.nx + 2, 3 * plan.Y, plan.nz), bf16),
-            pltpu.VMEM((bands, inner), f32),
-        ],
-    )(pos, weight.T, features, exchange(grad_sent))
+        (pos, features, bias_part, exchange(grad_sent)),
+        5,
+        [pltpu.VMEM((bands, inner), f32)],
+    )
+    grad_features = call(
+        feature_kernel,
+        shape(features.shape, bf16),
+        [SMEM, VMEM, VMEM, ANY],
+        (pos, weight.T, g, partial),
+        5,
+        [pltpu.VMEM((inner, bands), bf16)],
+    )
     grad_weight, grad_bias = call(
-        final_kernel, [shape((27, plan.ch)), shape((1, 1))], [VMEM]
-    )(everywhere(partial))
+        final_kernel,
+        [shape((27, plan.ch)), shape((1, 1))],
+        [VMEM],
+        (everywhere(partial),),
+        1.5,
+    )
     return (loss[0, :1], grad_features, grad_weight, grad_bias.reshape(1))
 
 

time: 179 us -> 140 us (0.78)
  Pallas kernels: 101 us -> 73.6 us
  waiting for transfers between devices: 26.2 us -> 5.11 us
  blocking collectives: 15.7 us -> 35.9 us
  starting transfers between devices: 28.1 us -> 19.5 us
    all_to_all x0 -> x2, blocking collectives: none -> 20.5 us  [exchange(): return lax.all_to_all(array, GROUP, 0, 0, tiled=True)]
    all_to_all x3 -> x1, waiting for transfers between devices: 14.5 us -> 0.01 us  [exchange(): return lax.all_to_all(array, GROUP, 0, 0, tiled=True)]
    pallas_call x1, Pallas kernels: 36.6 us -> 23.3 us  [per_device(): pl.pallas_call(functools.partial(forward_kernel, plan), grid=(SECTIONS,),...]
    all_to_all x3 -> x1, starting transfers between devices: 12.1 us -> 3.37 us  [exchange(): return lax.all_to_all(array, GROUP, 0, 0, tiled=True)]
    pallas_call x7 -> x8, Pallas kernels: 41.2 us -> 34 us  [call(): pl.pallas_call(functools.partial(kernel, plan), out_shape=out_shape, in_s...]
    pallas_call x1, Pallas kernels: 23.3 us -> 16.3 us  [per_device(): pl.pallas_call(functools.partial(backward_kernel, plan), grid=(SECTIONS,)...]
    all_to_all x1, waiting for transfers between devices: 6.6 us -> 0.2 us  [everywhere(): return lax.all_to_all(array, ALL_AXES, 0, 0, tiled=True)]
    unnamed x23 -> x11, local copies, waits for them, and re-layouts: 4.1 us -> 3.29 us
  transfers between devices with their start and end apart: 10 -> 8, of which waited for: 4 -> 2; matrix products, arithmetic and copies ran while one was open for 1% -> 0% of each run, Pallas kernels for 13% -> 15%
where the time goes in v3:
time: 140 us; the launch traced here: 139 us
  Pallas kernels  73.6 us (53%)
  blocking collectives  35.9 us (26%)
  starting transfers between devices  19.5 us (14%)
  waiting for transfers between devices  5.11 us (4%)
  local copies, waits for them, and re-layouts  3.81 us (3%)
  between operations  1.45 us (1%)
    pallas_call x8, Pallas kernels, call(): pl.pallas_call(functools.partial(kernel, plan), out_shape=out_shape, in_s...  34 us
    pallas_call x1, Pallas kernels, per_device(): pl.pallas_call(functools.partial(forward_kernel, plan), grid=(SECTIONS,),...  23.3 us
    all_to_all x2, blocking collectives, exchange(): return lax.all_to_all(array, GROUP, 0, 0, tiled=True)  20.5 us
    pallas_call x1, Pallas kernels, per_device(): pl.pallas_call(functools.partial(backward_kernel, plan), grid=(SECTIONS,)...  16.3 us
    all_to_all x1, blocking collectives, everywhere(): return lax.all_to_all(array, ALL_AXES, 0, 0, tiled=True)  15.4 us
    ppermute x6, starting transfers between devices, hop(): return lax.ppermute(array, ALL_AXES, pairs)  13.6 us
    ppermute x6, waiting for transfers between devices, hop(): return lax.ppermute(array, ALL_AXES, pairs)  4.91 us
    all_to_all x1, starting transfers between devices, exchange(): return lax.all_to_all(array, GROUP, 0, 0, tiled=True)  3.37 us
  transfers between devices with their start and end apart: 8, of which 2 were waited for; matrix products, arithmetic and copies ran while one was open for 0% of the time, Pallas kernels for 15%

profile of v3, /device:TPU:0, one launch (start us, length us, event | category | flops | bytes accessed | tf_op | source)
XLA Modules:
  0.0 139.4 jit_solution(5548594186969900228)
XLA Ops:
  0.6 0.1 pad_add_fusion.pos_ref.refs_0_
  0.7 0.0 copy-start.2
  0.7 0.9 copy-done.2
  1.6 1.3 shard_map.75.label_ref
  2.9 0.0 copy-start
  2.9 1.6 %copy-done = bf16[32,16,16,128]{3,2,1,0:T(8,128)(2,1)S(1)} copy-done((bf16[32,16,16,128]{3,2,1,0:T(8,128)(2,1)S(1)}, bf16[32,16,16,128]{3,2,1,0:T(8,128)(2,1)}, u32[]{:S(2)}) %copy-start) | copy-done | bytes 2097176
  4.5 0.0 copy-start.3
  4.5 0.7 copy-done.3
  5.2 5.2 %shard_map.78 = f32[8,6,16,128]{3,2,1,0:T(8,128)S(1)} custom-call(s32[2]{0:T(128)S(1)} %pad_add_fusion.pos_ref.refs_0_, bf16[27,32]{1,0:T(8,128)(2,1)S(1)} %copy-done.3, bf16[32,16,16,128]{3,2,1,0:T(8,128)(2,1)S(1)} %copy-done, bf16[8,4,16,128]{3,2,1,0:T(8,128)(2,1)} %shard_map.75.label_ref), custom_call_target="tpu_custom_call" | custom-call | bytes 17500000 | tf_op jit(solution)/shard_map/pallas_call | solution.py:800
  10.4 12.8 %all_to_all.25.got_ref = f32[8,6,16,128]{3,2,1,0:T(8,128)S(1)} all-to-all(f32[8,6,16,128]{3,2,1,0:T(8,128)S(1)} %shard_map.78), channel_id=1, replica_groups=mesh['gx'=4,'gy'=2,'gz'=4] {'gx','gy'}, dimensions={0} | all-to-all | bytes 786432 | tf_op jit(solution)/shard_map/all_to_all | solution.py:810
  23.2 3.4 %all-to-all-start = ((bf16[8,4,16,128]{3,2,1,0:T(8,128)(2,1)}), bf16[8,4,16,128]{3,2,1,0:T(8,128)(2,1)S(1)}, u32[]{:S(2)}, u32[]{:S(2)}) async-start(bf16[8,4,16,128]{3,2,1,0:T(8,128)(2,1)} %shard_map.75.label_ref), calls=%async_computation | async-start | bytes 262144 | tf_op jit(solution)/shard_map/all_to_all | solution.py:810
  26.5 0.1 shard_map.79
  26.6 3.8 %collective-permute-start.2 = (f32[18,16,128]{2,1,0:T(8,128)S(1)}, f32[18,16,128]{2,1,0:T(8,128)S(1)}, u32[]{:S(2)}, u32[]{:S(2)}) collective-permute-start(f32[18,16,128]{2,1,0:T(8,128)S(1)} %bitcast.11), channel_id=1, source_target_pairs={{0,4},{4,8},{8,12},{12,16},{16,20},{20,24},{24,28},{28,1},{1,5},{5... | collective-permute-start | bytes 442376 | tf_op jit(solution)/shard_map/ppermute | solution.py:824
  30.5 1.3 collective-permute-start.4
  31.8 0.0 all-to-all-done.got_ref
  31.8 0.1 shard_map.76
  31.8 4.5 %collective-permute-start = (bf16[13,16,128]{2,1,0:T(8,128)(2,1)S(1)}, bf16[13,16,128]{2,1,0:T(8,128)(2,1)S(1)}, u32[]{:S(2)}, u32[]{:S(2)}) collective-permute-start(bf16[13,16,128]{2,1,0:T(8,128)(2,1)S(1)} %bitcast.19), channel_id=1, source_target_pairs={{0,4},{4,8},{8,12},{12,16},{16,20},{20,24},{24,28},{28,1},{1,5},{5... | collective-permute-start | bytes 159752 | tf_op jit(solution)/shard_map/ppermute | solution.py:824
  36.4 1.3 collective-permute-start.3
  37.7 1.3 collective-permute-start.5
  39.0 0.0 collective-permute-done.refs_2_
  39.0 1.3 collective-permute-start.1
  41.0 4.9 %collective-permute-done.1.refs_3_ = bf16[13,16,128]{2,1,0:T(8,128)(2,1)S(1)} collective-permute-done((bf16[13,16,128]{2,1,0:T(8,128)(2,1)S(1)}, bf16[13,16,128]{2,1,0:T(8,128)(2,1)S(1)}, u32[]{:S(2)}, u32[]{:S(2)}) %collective-permute-start.1) | collective-permute-done | bytes 53280 | tf_op jit(solution)/shard_map/ppermute | solution.py:824
  45.9 13.4 %shard_map.77 = (f32[42,16,128]{2,1,0:T(8,128)S(1)}, f32[18,16,128]{2,1,0:T(8,128)S(1)}) custom-call(s32[2]{0:T(128)S(1)} %pad_add_fusion.pos_ref.refs_0_, bf16[16,16,128]{2,1,0:T(8,128)(2,1)S(1)} %bitcast.14, bf16[13,16,128]{2,1,0:T(8,128)(2,1)S(1)} %collective-permute-done.refs_2_, bf16[13,16,128]{2,1,0:T(8,128)(2,1)S(1)} %collective-permute-done.1.refs_3_), custom_call_target="tpu_custom_call" | custom-call | bytes 35000000 | tf_op jit(solution)/shard_map/pallas_call | solution.py:800
  59.3 0.0 collective-permute-done.3.refs_6_
  59.3 0.0 collective-permute-done.5.refs_8_
  59.3 0.0 collective-permute-done.2.refs_5_
  59.3 0.0 collective-permute-done.4.refs_7_
  59.3 23.3 %shard_map.80 = (f32[11,42,16,128]{3,2,1,0:T(8,128)S(1)}, f32[11,42,16,128]{3,2,1,0:T(8,128)S(1)}, f32[11,42,16,128]{3,2,1,0:T(8,128)S(1)}, f32[11,42,16,128]{3,...) custom-call(s32[2]{0:T(128)S(1)} %pad_add_fusion.pos_ref.refs_0_, f32[1]{0:T(128)S(6)} %copy.9.refs_1_, ...), custom_call_target="tpu_custom_call" | custom-call | bytes 62500000 | tf_op jit(solution)/shard_map/pallas_call | solution.py:902
  82.6 15.4 %all_to_all.26.refs_1_ = f32[32,8,128]{2,1,0:T(8,128)S(1)} all-to-all(f32[32,8,128]{2,1,0:T(8,128)S(1)} %get-tuple-element.33), channel_id=1, replica_groups=mesh['gx'=4,'gy'=2,'gz'=4] {'gx','gy','gz'}, dimensions={0} | all-to-all | bytes 262144 | tf_op jit(solution)/shard_map/all_to_all | solution.py:813
  98.0 0.0 copy-start.1
  98.0 0.0 copy-start.4
  98.0 16.3 %shard_map.81 = (bf16[8,6,16,128]{3,2,1,0:T(8,128)(2,1)S(1)}, f32[8,128]{1,0:T(8,128)S(1)}, f32[8,128]{1,0:T(8,128)S(1)}) custom-call(s32[2]{0:T(128)S(1)} %pad_add_fusion.pos_ref.refs_0_, f32[32,8,128]{2,1,0:T(8,128)S(1)} %all_to_all.26.refs_1_, f32[11,42,16,128]{3,2,1,0:T(8,128)S(1)} %get-tuple-element.34.refs_2_, ...), custom_call_target="tpu_custom_call" | custom-call | bytes 50000000 | tf_op jit(solution)/shard_map/pallas_call | solution.py:930
  114.4 7.7 %all_to_all.27.got_ref = bf16[8,6,16,128]{3,2,1,0:T(8,128)(2,1)S(1)} all-to-all(bf16[8,6,16,128]{3,2,1,0:T(8,128)(2,1)S(1)} %get-tuple-element.41), channel_id=1, replica_groups=mesh['gx'=4,'gy'=2,'gz'=4] {'gx','gy'}, dimensions={0} | all-to-all | bytes 393216 | tf_op jit(solution)/shard_map/all_to_all | solution.py:810
  122.1 0.0 copy-done.1
  122.1 6.2 %shard_map.82 = (f32[32,8,128]{2,1,0:T(8,128)}, bf16[18,96,128]{2,1,0:T(8,128)(2,1)S(1)}) custom-call(s32[2]{0:T(128)S(1)} %pad_add_fusion.pos_ref.refs_0_, bf16[32,16,16,128]{3,2,1,0:T(8,128)(2,1)S(1)} %copy-done.1, f32[8,128]{1,0:T(8,128)S(1)} %get-tuple-element.40.bias_ref, bf16[8,6,16,128]{3,2,1,0:T(8,128)(2,1)S(1)} %all_to_all.27.got_ref), custom_call_target="tpu_custom_call" | custom-call | bytes 12500000 | tf_op jit(solution)/shard_map/pallas_call | solution.py:800
  128.3 2.6 %all-to-all-start.4 = ((f32[32,8,128]{2,1,0:T(8,128)}), f32[32,8,128]{2,1,0:T(8,128)S(1)}, u32[]{:S(2)}, u32[]{:S(2)}) async-start(f32[32,8,128]{2,1,0:T(8,128)} %get-tuple-element.43.after_ref), calls=%async_computation.4 | async-start | bytes 262144 | tf_op jit(solution)/shard_map/all_to_all | solution.py:813
  130.9 0.0 copy-done.4
  130.9 0.1 copy.8
  131.0 0.5 slice.3
  131.5 7.0 %shard_map.83 = bf16[32,16,16,128]{3,2,1,0:T(8,128)(2,1)} custom-call(s32[2]{0:T(128)S(1)} %pad_add_fusion.pos_ref.refs_0_, bf16[32,27]{1,0:T(8,128)(2,1)S(1)} %bitcast.15, bf16[18,96,128]{2,1,0:T(8,128)(2,1)S(1)} %get-tuple-element.42.g_ref, f32[32,8,128]{2,1,0:T(8,128)} %get-tuple-element.43.after_ref), custom_call_target="tpu_custom_call" | custom-call | bytes 12500000 | tf_op jit(solution)/shard_map/pallas_call | solution.py:800
  138.5 0.2 all-to-all-done.4.got_ref
  138.7 0.7 shard_map.84
Async XLA Ops:
  0.7 0.9 copy-start.2
  2.9 1.6 %copy-start = (bf16[32,16,16,128]{3,2,1,0:T(8,128)(2,1)S(1)}, bf16[32,16,16,128]{3,2,1,0:T(8,128)(2,1)}, u32[]{:S(2)}) copy-start(bf16[32,16,16,128]{3,2,1,0:T(8,128)(2,1)} %f_ref.3) | copy-start | bytes 6291460
  4.5 0.7 copy-start.3
  23.2 8.6 %all-to-all-start = ((bf16[8,4,16,128]{3,2,1,0:T(8,128)(2,1)}), bf16[8,4,16,128]{3,2,1,0:T(8,128)(2,1)S(1)}, u32[]{:S(2)}, u32[]{:S(2)}) async-start(bf16[8,4,16,128]{3,2,1,0:T(8,128)(2,1)} %shard_map.75.label_ref), calls=%async_computation | async-start | bytes 262144 | tf_op jit(solution)/shard_map/all_to_all | solution.py:810
  26.6 32.7 %collective-permute-start.2 = (f32[18,16,128]{2,1,0:T(8,128)S(1)}, f32[18,16,128]{2,1,0:T(8,128)S(1)}, u32[]{:S(2)}, u32[]{:S(2)}) collective-permute-start(f32[18,16,128]{2,1,0:T(8,128)S(1)} %bitcast.11), channel_id=1, source_target_pairs={{0,4},{4,8},{8,12},{12,16},{16,20},{20,24},{24,28},{28,1},{1,5},{5... | collective-permute-start | bytes 442376 | tf_op jit(solution)/shard_map/ppermute | solution.py:824
  30.5 28.8 %collective-permute-start.4 = (f32[18,16,128]{2,1,0:T(8,128)S(1)}, f32[18,16,128]{2,1,0:T(8,128)S(1)}, u32[]{:S(2)}, u32[]{:S(2)}) collective-permute-start(f32[18,16,128]{2,1,0:T(8,128)S(1)} %bitcast.12), channel_id=1, source_target_pairs={{4,0},{8,4},{12,8},{16,12},{20,16},{24,20},{28,24},{1,28},{5,1},{9... | collective-permute-start | bytes 442376 | tf_op jit(solution)/shard_map/ppermute | solution.py:824
  31.8 7.2 %collective-permute-start = (bf16[13,16,128]{2,1,0:T(8,128)(2,1)S(1)}, bf16[13,16,128]{2,1,0:T(8,128)(2,1)S(1)}, u32[]{:S(2)}, u32[]{:S(2)}) collective-permute-start(bf16[13,16,128]{2,1,0:T(8,128)(2,1)S(1)} %bitcast.19), channel_id=1, source_target_pairs={{0,4},{4,8},{8,12},{12,16},{16,20},{20,24},{24,28},{28,1},{1,5},{5... | collective-permute-start | bytes 159752 | tf_op jit(solution)/shard_map/ppermute | solution.py:824
  36.4 22.9 %collective-permute-start.3 = (f32[10,16,128]{2,1,0:T(8,128)S(1)}, f32[10,16,128]{2,1,0:T(8,128)S(1)}, u32[]{:S(2)}, u32[]{:S(2)}) collective-permute-start(f32[10,16,128]{2,1,0:T(8,128)S(1)} %bitcast.17), channel_id=1, source_target_pairs={{0,8},{4,12},{8,16},{12,20},{16,24},{20,28},{24,1},{28,5},{1,9},{5... | collective-permute-start | bytes 245768 | tf_op jit(solution)/shard_map/ppermute | solution.py:824
  37.7 21.6 %collective-permute-start.5 = (f32[10,16,128]{2,1,0:T(8,128)S(1)}, f32[10,16,128]{2,1,0:T(8,128)S(1)}, u32[]{:S(2)}, u32[]{:S(2)}) collective-permute-start(f32[10,16,128]{2,1,0:T(8,128)S(1)} %bitcast.16), channel_id=1, source_target_pairs={{8,0},{12,4},{16,8},{20,12},{24,16},{28,20},{1,24},{5,28},{9,1},{1... | collective-permute-start | bytes 245768 | tf_op jit(solution)/shard_map/ppermute | solution.py:824
  39.0 6.8 %collective-permute-start.1 = (bf16[13,16,128]{2,1,0:T(8,128)(2,1)S(1)}, bf16[13,16,128]{2,1,0:T(8,128)(2,1)S(1)}, u32[]{:S(2)}, u32[]{:S(2)}) collective-permute-start(bf16[13,16,128]{2,1,0:T(8,128)(2,1)S(1)} %bitcast.18), channel_id=1, source_target_pairs={{4,0},{8,4},{12,8},{16,12},{20,16},{24,20},{28,24},{1,28},{5,1},{9... | collective-permute-start | bytes 159752 | tf_op jit(solution)/shard_map/ppermute | solution.py:824
  98.0 24.1 %copy-start.1 = (bf16[32,16,16,128]{3,2,1,0:T(8,128)(2,1)S(1)}, bf16[32,16,16,128]{3,2,1,0:T(8,128)(2,1)}, u32[]{:S(2)}) copy-start(bf16[32,16,16,128]{3,2,1,0:T(8,128)(2,1)} %f_ref.3) | copy-start | bytes 6291460
  98.0 32.8 %copy-start.4 = (bf16[27,32]{1,0:T(8,128)(2,1)S(1)}, bf16[27,32]{1,0:T(8,128)(2,1)}, u32[]{:S(2)}) copy-start(bf16[27,32]{1,0:T(8,128)(2,1)} %w_ref.1) | copy-start | bytes 5188
  128.3 10.4 %all-to-all-start.4 = ((f32[32,8,128]{2,1,0:T(8,128)}), f32[32,8,128]{2,1,0:T(8,128)S(1)}, u32[]{:S(2)}, u32[]{:S(2)}) async-start(f32[32,8,128]{2,1,0:T(8,128)} %get-tuple-element.43.after_ref), calls=%async_computation.4 | async-start | bytes 262144 | tf_op jit(solution)/shard_map/all_to_all | solution.py:813

commit v4 on v3

--- a/solution.py
+++ b/solution.py
@@ -94,7 +94,7 @@
     return lower + upper
 
 
-def y_neighbours(plan, mask, cur):
+def y_neighbours(mask, cur):
     lower = jnp.where(mask[1], 0.0, pltpu.roll(cur, 1, 1))
     upper = jnp.where(mask[2], 0.0, pltpu.roll(cur, LANES - 1, 1))
     return lower + upper
@@ -144,8 +144,19 @@
     return own + member_y * plan.ny - y + 1
 
 
-def conv_kernel(plan, pos_ref, w_ref, f_ref, label_ref, out_ref, wide_ref, acc_ref):
+def conv_kernel(
+    plan, pos_ref, w_ref, far_ref, label_ref, out_ref, wide_ref, acc_ref, f_ref, sem_ref
+):
     del label_ref
+    parts = 4
+    width = plan.nx // parts
+    copies = []
+    for n in range(parts):
+        span = pl.ds(n * width, width)
+        copies.append(
+            pltpu.make_async_copy(far_ref.at[:, span], f_ref.at[:, span], sem_ref.at[n])
+        )
+        copies[-1].start()
     rows, inner = plan.Y, plan.ch * plan.ny
     spread = (
         lax.broadcasted_iota(jnp.int32, (plan.ch, inner), 0)
@@ -170,7 +181,9 @@
             acc_ref[x + 2 - i] += out[3 * i * rows : 3 * (i + 1) * rows]
         return carry
 
-    lax.fori_loop(0, plan.nx, at_x, 0)
+    for n in range(parts):
+        copies[n].wait()
+        lax.fori_loop(n * width, (n + 1) * width, at_x, 0)
 
     out_ref[...] = jnp.zeros_like(out_ref)
     places = {}
@@ -297,7 +310,7 @@
                 return e_ref[now, at, 8 + offset : 8 + offset + plan.tiles]
 
             total = cur + e_ref[now, at - 1, tiles] + e_ref[now, at + 1, tiles]
-            total = total + x_neighbours(plan, mask, load, cur) + y_neighbours(plan, mask, cur)
+            total = total + x_neighbours(plan, mask, load, cur) + y_neighbours(mask, cur)
             kind, outside = kind_of(plan, rank, plane + n)
             total = total * table_ref[kind]
             out.append((e_ref, (1 - now, at, tiles), total))
@@ -315,7 +328,7 @@
         values = [g_ref[now, plane + n + base] for n in range(-1, size + 1)]
         for n in range(size):
             part = values[n] + values[n + 1] + values[n + 2]
-            part = part + y_neighbours(plan, mask, part)
+            part = part + y_neighbours(mask, part)
             out.append((zy_ref, (plane + n - first, tiles), part))
         store_all(out)
 
@@ -464,6 +477,7 @@
     reach = REACH + 1 + ITERS - step
     erode(plan, rank, mask, e_ref, g_ref, cross_ref, now, base, -reach, zc + 2 * reach, size)
     spread(plan, mask, g_ref, 1 - now, zy_ref, base, -REACH, plan.win, size)
+
     def point(at, opening):
         out = []
         for n in range(size):
@@ -556,7 +570,7 @@
         out = []
         for n in range(size):
             part = values[n] + values[n + 1] + values[n + 2]
-            part = part + y_neighbours(plan, mask, part)
+            part = part + y_neighbours(mask, part)
             out.append((zy_ref, (at + n, tiles), part))
         store_all(out)
 
@@ -584,7 +598,7 @@
                 return pull_ref[spot + 1, 8 + offset : 8 + offset + plan.tiles]
 
             total = cur + pull_ref[spot, tiles] + pull_ref[spot + 2, tiles]
-            total = total + x_neighbours(plan, mask, load, cur) + y_neighbours(plan, mask, cur)
+            total = total + x_neighbours(plan, mask, load, cur) + y_neighbours(mask, cur)
             w = w_ref[spot]
             out.append((h_ref, spot, w * t_ref[0, spot] + total))
             out.append((w_ref, spot, w * m_ref[0, spot]))
@@ -757,6 +771,7 @@
 VMEM = pl.BlockSpec(memory_space=pltpu.VMEM)
 SMEM = pl.BlockSpec(memory_space=pltpu.SMEM)
 ANY = pl.BlockSpec(memory_space=pl.ANY)
+FAR = pl.BlockSpec(memory_space=pltpu.HBM)
 MIB = 1024 * 1024
 
 
@@ -775,10 +790,10 @@
     return total
 
 
-def limits(arrays, scratch, micros):
+def limits(arrays, scratch, micros, least=0):
     total = sum(held(a.shape, a.dtype) for a in arrays)
-    total += sum(held(a.shape, a.dtype) for a in scratch)
-    limit = min(63 * MIB, total + total // 8 + 4 * MIB)
+    total += sum(held(a.shape, a.dtype) for a in scratch if len(a.shape) > 1)
+    limit = max(least, min(63 * MIB, total + total // 8 + 4 * MIB))
     return dict(
         compiler_params=pltpu.CompilerParams(vmem_limit_bytes=limit),
         cost_estimate=pl.CostEstimate(
@@ -794,7 +809,7 @@
     place = (lax.axis_index("gz") * members + lax.axis_index(GROUP)).astype(jnp.int32)
     pos = jnp.stack([place, lax.axis_index("gy").astype(jnp.int32)])
 
-    def call(kernel, out_shape, in_specs, operands, micros, scratch=()):
+    def call(kernel, out_shape, in_specs, operands, micros, scratch=(), least=0):
         outs = jax.tree.leaves(out_shape)
         ins = [a for spec, a in zip(in_specs, operands) if spec is VMEM]
         return pl.pallas_call(
@@ -803,7 +818,7 @@
             in_specs=in_specs,
             out_specs=jax.tree.map(lambda s: VMEM, out_shape),
             scratch_shapes=list(scratch),
-            **limits(ins + outs, scratch, micros),
+            **limits(ins + outs, scratch, micros, least),
         )(*operands)
 
     def exchange(array):
@@ -829,13 +844,16 @@
     sent_logits = call(
         conv_kernel,
         shape((members, sent + plan.extra, plan.R, LANES)),
-        [SMEM, VMEM, VMEM, ANY],
+        [SMEM, VMEM, FAR, ANY],
         (pos, weight, features, label_sent),
         7,
         [
             pltpu.VMEM((bands, inner), bf16),
             pltpu.VMEM((plan.nx + 2, 3 * plan.Y, plan.nz), f32),
+            pltpu.VMEM(features.shape, bf16),
+            pltpu.SemaphoreType.DMA((4,)),
         ],
+        62 * MIB,
     )
 
     def planes(array):
@@ -967,10 +985,10 @@
 def solution(mesh):
     in_specs = (P(None, "gx", "gy", "gz"), P(), P(), P("gx", "gy", "gz"))
     out_specs = (P(), P(None, "gx", "gy", "gz"), P(), P())
+
+    def body(*args):
+        return per_device(dict(mesh.shape), *args)
+
     return jax.shard_map(
-        functools.partial(per_device, dict(mesh.shape)),
-        mesh=mesh,
-        in_specs=in_specs,
-        out_specs=out_specs,
-        check_vma=False,
+        body, mesh=mesh, in_specs=in_specs, out_specs=out_specs, check_vma=False
     )

time: 140 us -> 141 us (level)
    unnamed x11 -> x17, local copies, waits for them, and re-layouts: 3.29 us -> 2.95 us
where the time goes in v4:
time: 141 us; the launch traced here: 140 us
  Pallas kernels  74.6 us (53%)
  blocking collectives  36.1 us (26%)
  starting transfers between devices  19.5 us (14%)
  waiting for transfers between devices  5.1 us (4%)
  local copies, waits for them, and re-layouts  3.47 us (2%)
  between operations  1.49 us (1%)
    pallas_call x8, Pallas kernels, call(): pl.pallas_call(functools.partial(kernel, plan), out_shape=out_shape, in_s...  35 us
    pallas_call x1, Pallas kernels, per_device(): pl.pallas_call(functools.partial(forward_kernel, plan), grid=(SECTIONS,),...  23.2 us
    all_to_all x2, blocking collectives, exchange(): return lax.all_to_all(array, GROUP, 0, 0, tiled=True)  20.7 us
    pallas_call x1, Pallas kernels, per_device(): pl.pallas_call(functools.partial(backward_kernel, plan), grid=(SECTIONS,)...  16.3 us
    all_to_all x1, blocking collectives, everywhere(): return lax.all_to_all(array, ALL_AXES, 0, 0, tiled=True)  15.4 us
    ppermute x6, starting transfers between devices, hop(): return lax.ppermute(array, ALL_AXES, pairs)  13.6 us
    ppermute x6, waiting for transfers between devices, hop(): return lax.ppermute(array, ALL_AXES, pairs)  4.91 us
    all_to_all x1, starting transfers between devices, exchange(): return lax.all_to_all(array, GROUP, 0, 0, tiled=True)  3.37 us
  transfers between devices with their start and end apart: 8, of which 2 were waited for; matrix products, arithmetic and copies ran while one was open for 0% of the time, Pallas kernels for 15%

profile of v4, /device:TPU:0, one launch (start us, length us, event | category | flops | bytes accessed | tf_op | source)
XLA Modules:
  0.0 140.3 jit_solution(16390173148427223535)
XLA Ops:
  0.6 0.1 pad_add_fusion.pos_ref.refs_0_
  0.7 0.0 copy-start.2
  0.7 0.9 copy-done.2
  1.6 0.0 copy-start.3
  1.6 0.6 shard_map.75.label_ref
  2.3 0.0 copy-done.3
  2.3 0.0 copy-start.1
  2.3 0.6 copy-done.1
  2.9 6.9 %shard_map.78 = f32[8,6,16,128]{3,2,1,0:T(8,128)} custom-call(s32[2]{0:T(128)} %copy-done.3, bf16[27,32]{1,0:T(8,128)(2,1)} %w_ref.1, bf16[32,16,16,128]{3,2,1,0:T(8,128)(2,1)} %f_ref.1, bf16[8,4,16,128]{3,2,1,0:T(8,128)(2,1)} %copy-done.1), custom_call_target="tpu_custom_call" | custom-call | bytes 17500000 | tf_op jit(solution)/shard_map/pallas_call | solution.py:815
  9.8 13.0 %all_to_all.25.got_ref = f32[8,6,16,128]{3,2,1,0:T(8,128)S(1)} all-to-all(f32[8,6,16,128]{3,2,1,0:T(8,128)} %shard_map.78), channel_id=1, replica_groups=mesh['gx'=4,'gy'=2,'gz'=4] {'gx','gy'}, dimensions={0} | all-to-all | bytes 786432 | tf_op jit(solution)/shard_map/all_to_all | solution.py:825
  22.8 3.4 %all-to-all-start = ((bf16[8,4,16,128]{3,2,1,0:T(8,128)(2,1)}), bf16[8,4,16,128]{3,2,1,0:T(8,128)(2,1)S(1)}, u32[]{:S(2)}, u32[]{:S(2)}) async-start(bf16[8,4,16,128]{3,2,1,0:T(8,128)(2,1)} %copy-done.1), calls=%async_computation | async-start | bytes 262144 | tf_op jit(solution)/shard_map/all_to_all | solution.py:825
  26.2 0.1 shard_map.79
  26.3 3.8 %collective-permute-start.2 = (f32[18,16,128]{2,1,0:T(8,128)S(1)}, f32[18,16,128]{2,1,0:T(8,128)S(1)}, u32[]{:S(2)}, u32[]{:S(2)}) collective-permute-start(f32[18,16,128]{2,1,0:T(8,128)S(1)} %bitcast.11), channel_id=1, source_target_pairs={{0,4},{4,8},{8,12},{12,16},{16,20},{20,24},{24,28},{28,1},{1,5},{5... | collective-permute-start | bytes 442376 | tf_op jit(solution)/shard_map/ppermute | solution.py:839
  30.1 1.3 collective-permute-start.4
  31.4 0.0 all-to-all-done.got_ref
  31.4 0.1 shard_map.76
  31.5 4.5 %collective-permute-start = (bf16[13,16,128]{2,1,0:T(8,128)(2,1)S(1)}, bf16[13,16,128]{2,1,0:T(8,128)(2,1)S(1)}, u32[]{:S(2)}, u32[]{:S(2)}) collective-permute-start(bf16[13,16,128]{2,1,0:T(8,128)(2,1)S(1)} %bitcast.19), channel_id=1, source_target_pairs={{0,4},{4,8},{8,12},{12,16},{16,20},{20,24},{24,28},{28,1},{1,5},{5... | collective-permute-start | bytes 159752 | tf_op jit(solution)/shard_map/ppermute | solution.py:839
  36.0 1.3 collective-permute-start.3
  37.3 1.3 collective-permute-start.5
  38.6 0.0 collective-permute-done.refs_2_
  38.6 1.3 collective-permute-start.1
  40.6 4.9 %collective-permute-done.1.refs_3_ = bf16[13,16,128]{2,1,0:T(8,128)(2,1)S(1)} collective-permute-done((bf16[13,16,128]{2,1,0:T(8,128)(2,1)S(1)}, bf16[13,16,128]{2,1,0:T(8,128)(2,1)S(1)}, u32[]{:S(2)}, u32[]{:S(2)}) %collective-permute-start.1) | collective-permute-done | bytes 53280 | tf_op jit(solution)/shard_map/ppermute | solution.py:839
  45.5 0.0 copy-start.4
  45.5 0.7 copy-done.4
  46.1 13.4 %shard_map.77 = (f32[42,16,128]{2,1,0:T(8,128)S(1)}, f32[18,16,128]{2,1,0:T(8,128)S(1)}) custom-call(s32[2]{0:T(128)S(1)} %copy-done.4, bf16[16,16,128]{2,1,0:T(8,128)(2,1)S(1)} %bitcast.14, bf16[13,16,128]{2,1,0:T(8,128)(2,1)S(1)} %collective-permute-done.refs_2_, bf16[13,16,128]{2,1,0:T(8,128)(2,1)S(1)} %collective-permute-done.1.refs_3_), custom_call_target="tpu_custom_call" | custom-call | bytes 35000000 | tf_op jit(solution)/shard_map/pallas_call | solution.py:815
  59.6 0.0 collective-permute-done.3.refs_6_
  59.6 0.0 collective-permute-done.5.refs_8_
  59.6 0.0 collective-permute-done.2.refs_5_
  59.6 0.0 collective-permute-done.4.refs_7_
  59.6 0.0 copy-start.5
  59.6 0.6 copy-done.5
  60.3 23.2 %shard_map.80 = (f32[11,42,16,128]{3,2,1,0:T(8,128)S(1)}, f32[11,42,16,128]{3,2,1,0:T(8,128)S(1)}, f32[11,42,16,128]{3,2,1,0:T(8,128)S(1)}, f32[11,42,16,128]{3,...) custom-call(s32[2]{0:T(128)S(1)} %copy-done.5, f32[1]{0:T(128)S(6)} %copy.9.refs_1_, ...), custom_call_target="tpu_custom_call" | custom-call | bytes 62500000 | tf_op jit(solution)/shard_map/pallas_call | solution.py:920
  83.5 15.4 %all_to_all.26.refs_1_ = f32[32,8,128]{2,1,0:T(8,128)S(1)} all-to-all(f32[32,8,128]{2,1,0:T(8,128)S(1)} %get-tuple-element.33), channel_id=1, replica_groups=mesh['gx'=4,'gy'=2,'gz'=4] {'gx','gy','gz'}, dimensions={0} | all-to-all | bytes 262144 | tf_op jit(solution)/shard_map/all_to_all | solution.py:828
  98.9 0.0 copy-start
  98.9 0.0 copy-start.7
  98.9 0.0 copy-start.6
  98.9 16.3 %shard_map.81 = (bf16[8,6,16,128]{3,2,1,0:T(8,128)(2,1)S(1)}, f32[8,128]{1,0:T(8,128)S(1)}, f32[8,128]{1,0:T(8,128)S(1)}) custom-call(s32[2]{0:T(128)S(1)} %copy-done.5, f32[32,8,128]{2,1,0:T(8,128)S(1)} %all_to_all.26.refs_1_, f32[11,42,16,128]{3,2,1,0:T(8,128)S(1)} %get-tuple-element.34.refs_2_, f32[11,42,16,128]{3,2,1,0:T(8,128)S(1)} %get-tuple-element.35.refs_3_, ...), custom_call_target="tpu_custom_call" | custom-call | bytes 50000000 | tf_op jit(solution)/shard_map/pallas_call | solution.py:948
  115.3 7.7 %all_to_all.27.got_ref = bf16[8,6,16,128]{3,2,1,0:T(8,128)(2,1)S(1)} all-to-all(bf16[8,6,16,128]{3,2,1,0:T(8,128)(2,1)S(1)} %get-tuple-element.41), channel_id=1, replica_groups=mesh['gx'=4,'gy'=2,'gz'=4] {'gx','gy'}, dimensions={0} | all-to-all | bytes 393216 | tf_op jit(solution)/shard_map/all_to_all | solution.py:825
  123.0 0.0 copy-done
  123.0 6.2 %shard_map.82 = (f32[32,8,128]{2,1,0:T(8,128)}, bf16[18,96,128]{2,1,0:T(8,128)(2,1)S(1)}) custom-call(s32[2]{0:T(128)S(1)} %copy-done.5, bf16[32,16,16,128]{3,2,1,0:T(8,128)(2,1)S(1)} %copy-done, f32[8,128]{1,0:T(8,128)S(1)} %get-tuple-element.40.bias_ref, bf16[8,6,16,128]{3,2,1,0:T(8,128)(2,1)S(1)} %all_to_all.27.got_ref), custom_call_target="tpu_custom_call" | custom-call | bytes 12500000 | tf_op jit(solution)/shard_map/pallas_call | solution.py:815
  129.2 2.6 %all-to-all-start.4 = ((f32[32,8,128]{2,1,0:T(8,128)}), f32[32,8,128]{2,1,0:T(8,128)S(1)}, u32[]{:S(2)}, u32[]{:S(2)}) async-start(f32[32,8,128]{2,1,0:T(8,128)} %get-tuple-element.43.after_ref), calls=%async_computation.4 | async-start | bytes 262144 | tf_op jit(solution)/shard_map/all_to_all | solution.py:828
  131.8 0.0 copy-done.7
  131.8 0.1 copy.8
  131.9 0.5 slice.3
  132.4 0.0 copy-done.6
  132.4 7.0 %shard_map.83 = bf16[32,16,16,128]{3,2,1,0:T(8,128)(2,1)} custom-call(s32[2]{0:T(128)S(1)} %copy-done.6, bf16[32,27]{1,0:T(8,128)(2,1)S(1)} %bitcast.15, bf16[18,96,128]{2,1,0:T(8,128)(2,1)S(1)} %get-tuple-element.42.g_ref, f32[32,8,128]{2,1,0:T(8,128)} %get-tuple-element.43.after_ref), custom_call_target="tpu_custom_call" | custom-call | bytes 12500000 | tf_op jit(solution)/shard_map/pallas_call | solution.py:815
  139.4 0.2 all-to-all-done.4.got_ref
  139.6 0.7 shard_map.84
Async XLA Ops:
  0.7 0.9 copy-start.2
  1.6 0.7 copy-start.3
  2.3 0.6 copy-start.1
  22.8 8.6 %all-to-all-start = ((bf16[8,4,16,128]{3,2,1,0:T(8,128)(2,1)}), bf16[8,4,16,128]{3,2,1,0:T(8,128)(2,1)S(1)}, u32[]{:S(2)}, u32[]{:S(2)}) async-start(bf16[8,4,16,128]{3,2,1,0:T(8,128)(2,1)} %copy-done.1), calls=%async_computation | async-start | bytes 262144 | tf_op jit(solution)/shard_map/all_to_all | solution.py:825
  26.3 33.3 %collective-permute-start.2 = (f32[18,16,128]{2,1,0:T(8,128)S(1)}, f32[18,16,128]{2,1,0:T(8,128)S(1)}, u32[]{:S(2)}, u32[]{:S(2)}) collective-permute-start(f32[18,16,128]{2,1,0:T(8,128)S(1)} %bitcast.11), channel_id=1, source_target_pairs={{0,4},{4,8},{8,12},{12,16},{16,20},{20,24},{24,28},{28,1},{1,5},{5... | collective-permute-start | bytes 442376 | tf_op jit(solution)/shard_map/ppermute | solution.py:839
  30.1 29.5 %collective-permute-start.4 = (f32[18,16,128]{2,1,0:T(8,128)S(1)}, f32[18,16,128]{2,1,0:T(8,128)S(1)}, u32[]{:S(2)}, u32[]{:S(2)}) collective-permute-start(f32[18,16,128]{2,1,0:T(8,128)S(1)} %bitcast.12), channel_id=1, source_target_pairs={{4,0},{8,4},{12,8},{16,12},{20,16},{24,20},{28,24},{1,28},{5,1},{9... | collective-permute-start | bytes 442376 | tf_op jit(solution)/shard_map/ppermute | solution.py:839
  31.5 7.2 %collective-permute-start = (bf16[13,16,128]{2,1,0:T(8,128)(2,1)S(1)}, bf16[13,16,128]{2,1,0:T(8,128)(2,1)S(1)}, u32[]{:S(2)}, u32[]{:S(2)}) collective-permute-start(bf16[13,16,128]{2,1,0:T(8,128)(2,1)S(1)} %bitcast.19), channel_id=1, source_target_pairs={{0,4},{4,8},{8,12},{12,16},{16,20},{20,24},{24,28},{28,1},{1,5},{5... | collective-permute-start | bytes 159752 | tf_op jit(solution)/shard_map/ppermute | solution.py:839
  36.0 23.5 %collective-permute-start.3 = (f32[10,16,128]{2,1,0:T(8,128)S(1)}, f32[10,16,128]{2,1,0:T(8,128)S(1)}, u32[]{:S(2)}, u32[]{:S(2)}) collective-permute-start(f32[10,16,128]{2,1,0:T(8,128)S(1)} %bitcast.17), channel_id=1, source_target_pairs={{0,8},{4,12},{8,16},{12,20},{16,24},{20,28},{24,1},{28,5},{1,9},{5... | collective-permute-start | bytes 245768 | tf_op jit(solution)/shard_map/ppermute | solution.py:839
  37.3 22.3 %collective-permute-start.5 = (f32[10,16,128]{2,1,0:T(8,128)S(1)}, f32[10,16,128]{2,1,0:T(8,128)S(1)}, u32[]{:S(2)}, u32[]{:S(2)}) collective-permute-start(f32[10,16,128]{2,1,0:T(8,128)S(1)} %bitcast.16), channel_id=1, source_target_pairs={{8,0},{12,4},{16,8},{20,12},{24,16},{28,20},{1,24},{5,28},{9,1},{1... | collective-permute-start | bytes 245768 | tf_op jit(solution)/shard_map/ppermute | solution.py:839
  38.6 6.8 %collective-permute-start.1 = (bf16[13,16,128]{2,1,0:T(8,128)(2,1)S(1)}, bf16[13,16,128]{2,1,0:T(8,128)(2,1)S(1)}, u32[]{:S(2)}, u32[]{:S(2)}) collective-permute-start(bf16[13,16,128]{2,1,0:T(8,128)(2,1)S(1)} %bitcast.18), channel_id=1, source_target_pairs={{4,0},{8,4},{12,8},{16,12},{20,16},{24,20},{28,24},{1,28},{5,1},{9... | collective-permute-start | bytes 159752 | tf_op jit(solution)/shard_map/ppermute | solution.py:839
  45.5 0.7 copy-start.4
  59.6 0.7 copy-start.5
  98.9 24.1 %copy-start = (bf16[32,16,16,128]{3,2,1,0:T(8,128)(2,1)S(1)}, bf16[32,16,16,128]{3,2,1,0:T(8,128)(2,1)}, u32[]{:S(2)}) copy-start(bf16[32,16,16,128]{3,2,1,0:T(8,128)(2,1)} %f_ref.1) | copy-start | bytes 6291460
  98.9 32.8 %copy-start.7 = (bf16[27,32]{1,0:T(8,128)(2,1)S(1)}, bf16[27,32]{1,0:T(8,128)(2,1)}, u32[]{:S(2)}) copy-start(bf16[27,32]{1,0:T(8,128)(2,1)} %w_ref.1) | copy-start | bytes 5188
  98.9 33.5 %copy-start.6 = (s32[2]{0:T(128)S(1)}, s32[2]{0:T(128)}, u32[]{:S(2)}) copy-start(s32[2]{0:T(128)} %copy-done.3) | copy-start | bytes 28
  129.2 10.4 %all-to-all-start.4 = ((f32[32,8,128]{2,1,0:T(8,128)}), f32[32,8,128]{2,1,0:T(8,128)S(1)}, u32[]{:S(2)}, u32[]{:S(2)}) async-start(f32[32,8,128]{2,1,0:T(8,128)} %get-tuple-element.43.after_ref), calls=%async_computation.4 | async-start | bytes 262144 | tf_op jit(solution)/shard_map/all_to_all | solution.py:828

commit v5 on v4

--- a/solution.py
+++ b/solution.py
@@ -10,8 +10,9 @@
 ITERS = 10
 SECTIONS = ITERS + 1
 LANES = 128
+HALO = SECTIONS + 1
+BACK = SECTIONS + 1
 REACH = SECTIONS + 2
-HALO = 2 * SECTIONS + 3
 
 temper = 20.0
 sharpness = 40.0
@@ -51,17 +52,25 @@
         self.pad = self.tiles + 16
         self.win = self.zc + 2 * REACH
         self.span = self.zc + 2
-        self.block = self.blocks_of(self.win)
-        self.span_block = self.blocks_of(self.span)
+        self.block = self.blocks_of(self.zc, 16)
+        self.span_block = self.blocks_of(self.span, 32)
+        self.win_block = self.blocks_of(self.win, 32)
+        self.erode_block = max(1, 160 // self.tiles)
         self.base = HALO + 1
-        self.planes = self.zc + 2 * HALO + 2 + self.block
+        self.planes = self.zc + 2 * HALO + 2 + self.erode_block
+        self.pull_base = BACK + 2
+        self.pull_planes = self.zc + 2 * BACK + 4 + self.erode_block
         self.hops = -(-HALO // self.zc)
         self.rest = HALO - (self.hops - 1) * self.zc
         self.label_hops = -(-REACH // self.zc)
         self.label_rest = REACH - (self.label_hops - 1) * self.zc
-
-    def blocks_of(self, count):
-        fits = [n for n in range(1, count + 1) if count % n == 0 and n * self.tiles <= 256]
+        self.back_hops = -(-(BACK + 1) // self.zc)
+
+    def back_count(self, h):
+        return min(self.zc + BACK + 1 - h * self.zc, self.span)
+
+    def blocks_of(self, count, most):
+        fits = [n for n in range(1, count + 1) if count % n == 0 and n * self.tiles <= 8 * most]
         return fits[-1] if fits else 1
 
     def slot(self, x):
@@ -346,10 +355,10 @@
 
 def target_kernel(plan, *refs):
     hops = plan.label_hops
-    pos_ref, own_ref = refs[:2]
-    below, above = refs[2 : 2 + hops], refs[2 + hops : 2 + 2 * hops]
-    target_ref, ts_ref = refs[2 + 2 * hops : 4 + 2 * hops]
-    e_ref, g_ref, zy_ref, cross_ref, box_ref = refs[4 + 2 * hops :]
+    pos_ref, p_ref, own_ref = refs[:3]
+    below, above = refs[3 : 3 + hops], refs[3 + hops : 3 + 2 * hops]
+    target_ref, ts_ref, sums_ref = refs[3 + 2 * hops : 6 + 2 * hops]
+    all_ref, e_ref, g_ref, zy_ref, cross_ref, box_ref = refs[6 + 2 * hops :]
     zc, win, span = plan.zc, plan.win, plan.span
     size = plan.span_block
     base = REACH + 1
@@ -360,30 +369,31 @@
     e_ref[...] = jnp.zeros_like(e_ref)
     zy_ref[...] = jnp.zeros_like(zy_ref)
     g_ref[...] = jnp.zeros_like(g_ref)
-    target_ref[REACH : REACH + zc] = own_ref[...].astype(f32)
+    all_ref[REACH : REACH + zc] = own_ref[...].astype(f32)
     for h in range(1, hops + 1):
         n = zc if h < hops else plan.label_rest
         first = REACH - (h - 1) * zc - n
-        target_ref[first : first + n] = below[h - 1][...].astype(f32)
+        all_ref[first : first + n] = below[h - 1][...].astype(f32)
         first = REACH + h * zc
-        target_ref[first : first + n] = above[h - 1][...].astype(f32)
+        all_ref[first : first + n] = above[h - 1][...].astype(f32)
+    target_ref[...] = all_ref[REACH - 1 : REACH + zc + 1]
 
     def fill(plane):
         out = []
-        for n in range(plan.block):
+        for n in range(plan.win_block):
             at = plane + n
-            z = rank * zc + at - REACH
-            inside = ((z >= 0) & (z < plan.Z)).astype(f32)
-            out.append((e_ref, (0, at + 1, tiles), jnp.exp(-temper * target_ref[at]) * inside))
+            inside = 1.0 - kind_of(plan, rank, at - REACH)[1]
+            out.append((e_ref, (0, at + 1, tiles), jnp.exp(-temper * all_ref[at]) * inside))
         store_all(out)
 
-    over(0, win, plan.block, fill)
+    over(0, win, plan.win_block, fill)
 
     def section(step, carry):
         now = step % 2
         reach = 2 + ITERS - step
+        count = zc + 2 * reach
         erode(
-            plan, rank, mask, e_ref, g_ref, cross_ref, now, base, -reach, zc + 2 * reach, size
+            plan, rank, mask, e_ref, g_ref, cross_ref, now, base, -reach, count, plan.erode_block
         )
         spread(plan, mask, g_ref, 1 - now, zy_ref, base, -1, span, size)
 
@@ -411,14 +421,32 @@
 
     lax.fori_loop(0, SECTIONS, section, 0)
 
+    def add(n, totals):
+        ts = ts_ref[1 + n]
+        return totals[0] + ts * p_ref[1 + n], totals[1] + ts
+
+    zero = jnp.zeros((plan.tiles, LANES), f32)
+    put_sums(plan, sums_ref, lax.fori_loop(0, zc, add, (zero,) * 2))
+
+
+def put_sums(plan, ref, totals):
+    lines = [jnp.sum(total, axis=0, keepdims=True) for total in totals]
+    lines += [jnp.zeros((1, LANES), f32)] * (8 - len(lines))
+    ref[...] = jnp.broadcast_to(jnp.concatenate(lines, axis=0)[None], (plan.ranks, 8, LANES))
+
+
+def get_sums(ref, count):
+    lines = jnp.sum(jnp.sum(ref[...], axis=0), axis=1, keepdims=True)
+    return [lines[n : n + 1] for n in range(count)]
+
 
 def forward_kernel(plan, *refs):
     hops = plan.hops
-    pos_ref, bias_ref, target_ref, ts_ref, own_ref = refs[:5]
-    refs = refs[5:]
+    pos_ref, bias_ref, label_ref, own_ref = refs[:4]
+    refs = refs[4:]
     below, above = refs[:hops], refs[hops : 2 * hops]
     refs = refs[2 * hops :]
-    m_ref, q_ref, t_ref, g2_ref, p_ref, sums_ref = refs[:6]
+    m_ref, q_ref, t_ref, grown_ref, p_ref, sums_ref = refs[:6]
     e_ref, g_ref, zy_ref, s_ref, cross_ref, box_ref = refs[6:]
     base, zc, size = plan.base, plan.zc, plan.block
     tiles = slice(8, 8 + plan.tiles)
@@ -431,7 +459,6 @@
         e_ref[...] = jnp.zeros_like(e_ref)
         g_ref[...] = jnp.zeros_like(g_ref)
         zy_ref[...] = jnp.zeros_like(zy_ref)
-        s_ref[...] = jnp.zeros_like(s_ref)
         count_tables(plan, cross_ref, box_ref)
         e_ref[0, base : base + zc, tiles] = own_ref[:zc]
         for h in range(1, hops + 1):
@@ -462,215 +489,231 @@
 
         def fill(plane):
             out = []
-            for n in range(size):
+            for n in range(plan.erode_block):
                 at = plane + n
-                z = rank * zc + at - base
-                inside = ((z >= 0) & (z < plan.Z)).astype(f32)
+                inside = 1.0 - kind_of(plan, rank, at - base)[1]
                 predict = sigmoid(e_ref[0, at, tiles] + bias_ref[0])
                 out.append((e_ref, (0, at, tiles), jnp.exp(-temper * predict) * inside))
                 out.append((g_ref, (0, at), jnp.exp(temper * predict) * inside))
             store_all(out)
 
-        over(1, zc + 2 * HALO, size, fill)
+        over(1, zc + 2 * HALO, plan.erode_block, fill)
 
     now = step % 2
-    reach = REACH + 1 + ITERS - step
-    erode(plan, rank, mask, e_ref, g_ref, cross_ref, now, base, -reach, zc + 2 * reach, size)
-    spread(plan, mask, g_ref, 1 - now, zy_ref, base, -REACH, plan.win, size)
-
-    def point(at, opening):
+    reach = 1 + ITERS - step
+    count = zc + 2 * reach
+    erode(plan, rank, mask, e_ref, g_ref, cross_ref, now, base, -reach, count, plan.erode_block)
+    spread(plan, mask, g_ref, 1 - now, zy_ref, base, 0, zc, size)
+    grown_ref[0] = g_ref[1 - now, base - 1 : base + zc + 1]
+
+    def point(plane, opening):
         out = []
         for n in range(size):
-            spot = at + n
-            plane = spot - REACH
-            box = x_box(plan, mask, zy_ref, spot)
-            kind, outside = kind_of(plan, rank, plane)
-            e = e_ref[now, plane + base, tiles]
+            at = plane + n
+            box = x_box(plan, mask, zy_ref, at)
+            kind, outside = kind_of(plan, rank, at)
+            e = e_ref[now, at + base, tiles]
             over_box, slope, scaled = thin(e, box, box_ref[kind], outside)
             if opening:
                 grown, a = scaled * -LOG, slope
             else:
-                s = s_ref[spot]
+                s = s_ref[at]
                 grown, rate = lift(scaled, s)
                 a = rate * (1.0 - s) * slope
-                out.append((m_ref, (0, spot), 1.0 + rate * scaled * LOG))
-            after = g_ref[1 - now, plane + base]
-            out.append((s_ref, spot, grown))
-            out.append((q_ref, (0, spot), a * over_box))
-            out.append((t_ref, (0, spot), a * g_ref[now, plane + base]))
-            out.append((g2_ref, (0, spot), after * after))
+                out.append((m_ref, (0, at), 1.0 + rate * scaled * LOG))
+            out.append((s_ref, at, grown))
+            out.append((q_ref, (0, at), a * over_box))
+            out.append((t_ref, (0, at), a * g_ref[now, at + base]))
         store_all(out)
 
     @pl.when(step == 0)
     def _():
-        over(0, plan.win, size, lambda at: point(at, True))
+        over(0, zc, size, lambda at: point(at, True))
         m_ref[...] = jnp.ones_like(m_ref)
 
     @pl.when(step > 0)
     def _():
-        over(0, plan.win, size, lambda at: point(at, False))
+        over(0, zc, size, lambda at: point(at, False))
 
     @pl.when(step == SECTIONS - 1)
     def _():
         def add(n, totals):
-            ps, ts = s_ref[REACH + n], ts_ref[1 + n]
-            predict, target = p_ref[1 + n], target_ref[REACH + n]
-            terms = (ps * target, ps, ts * predict, ts, predict * target, predict, target)
+            ps, predict, target = s_ref[n], p_ref[1 + n], label_ref[n].astype(f32)
+            terms = (ps * target, ps, predict * target, predict, target)
             return tuple(total + term for total, term in zip(totals, terms))
 
-        start = (jnp.zeros((plan.tiles, LANES), f32),) * 7
-        totals = lax.fori_loop(0, zc, add, start)
-        lines = [jnp.sum(total, axis=0, keepdims=True) for total in totals]
-        lines.append(jnp.zeros((1, LANES), f32))
-        sums_ref[...] = jnp.broadcast_to(
-            jnp.concatenate(lines, axis=0)[None], (plan.ranks, 8, LANES)
-        )
+        zero = jnp.zeros((plan.tiles, LANES), f32)
+        put_sums(plan, sums_ref, lax.fori_loop(0, zc, add, (zero,) * 5))
 
 
 def backward_kernel(plan, *refs):
-    (
-        pos_ref, sums_ref, m_ref, q_ref, t_ref, g2_ref, p_ref, target_ref, ts_ref,
-        out_ref, loss_ref, bias_ref,
-        w_ref, h_ref, zy_ref, pull_ref, cross_ref, grad_ref,
-    ) = refs
+    hops = plan.back_hops
+    pos_ref, sums_ref, label_ref, m_ref, q_ref, t_ref, grown_ref = refs[:7]
+    mine_ref = refs[7]
+    up, down = refs[8 : 8 + hops], refs[8 + hops : 8 + 2 * hops]
+    w_ref, push_ref, wt_ref, zy_ref, pull_ref, cross_ref = refs[8 + 2 * hops :]
     step = pl.program_id(0)
     rank = pos_ref[0]
-    win, zc, size = plan.win, plan.zc, plan.block
+    zc, base = plan.zc, plan.pull_base
     tiles = slice(8, 8 + plan.tiles)
     mask = masks(plan)
-
-    lines = jnp.sum(jnp.sum(sums_ref[...], axis=0), axis=1, keepdims=True)
-    s1, s2, s3, s4, s5, s6, s7 = (lines[n : n + 1] for n in range(7))
+    now = step % 2
+
+    @pl.when(step == 0)
+    def _():
+        s1, s2 = get_sums(sums_ref, 2)
+        prec = (s1 + 1.0) / (s2 + 1.0)
+        push_ref[...] = jnp.zeros_like(push_ref)
+        wt_ref[...] = jnp.zeros_like(wt_ref)
+        zy_ref[...] = jnp.zeros_like(zy_ref)
+        pull_ref[...] = jnp.zeros_like(pull_ref)
+        count_tables(plan, cross_ref, None)
+        w_ref[...] = label_ref[...].astype(f32) - prec[None]
+
+    def push(at):
+        out = []
+        for n in range(plan.block):
+            w = w_ref[at + n]
+            out.append((push_ref, at + n + 2, w * q_ref[0, at + n]))
+            out.append((wt_ref, at + n + base, w * t_ref[0, at + n]))
+            out.append((w_ref, at + n, w * m_ref[0, at + n]))
+        store_all(out)
+
+    over(0, zc, plan.block, push)
+
+    def widen(at):
+        out = []
+        values = [push_ref[at + n] for n in range(plan.span_block + 2)]
+        for n in range(plan.span_block):
+            part = values[n] + values[n + 1] + values[n + 2]
+            out.append((zy_ref, (at + n, tiles), part + y_neighbours(mask, part)))
+        store_all(out)
+
+    over(0, plan.span, plan.span_block, widen)
+
+    def pull(at):
+        out = []
+        for n in range(plan.span_block):
+            box = x_box(plan, mask, zy_ref, at + n)
+            inverse = cross_ref[kind_of(plan, rank, at + n - 1)[0]]
+            grown = grown_ref[0, at + n]
+            spot = at + n - 1 + base
+            old = pull_ref[now, spot, tiles]
+            out.append((pull_ref, (now, spot, tiles), old - grown * grown * box * inverse))
+        store_all(out)
+
+    over(0, plan.span, plan.span_block, pull)
+    reach = 2 + step
+    last = step == SECTIONS - 1
+
+    def join(plane, ending):
+        out = []
+        for n in range(plan.erode_block):
+            at = plane + n + base
+            cur = pull_ref[now, at, tiles]
+
+            def load(offset, at=at):
+                return pull_ref[now, at, 8 + offset : 8 + offset + plan.tiles]
+
+            total = cur + pull_ref[now, at - 1, tiles] + pull_ref[now, at + 1, tiles]
+            total = total + x_neighbours(plan, mask, load, cur) + y_neighbours(mask, cur)
+            total = total + wt_ref[at]
+            if not ending:
+                total = total * cross_ref[kind_of(plan, rank, plane + n)[0]]
+            out.append((pull_ref, (1 - now, at, tiles), total))
+        store_all(out)
+
+    @pl.when(jnp.logical_not(last))
+    def _():
+        over(-reach, zc + 2 * reach, plan.erode_block, lambda plane: join(plane, False))
+
+    @pl.when(last)
+    def _():
+        over(-reach, zc + 2 * reach, plan.erode_block, lambda plane: join(plane, True))
+        mine_ref[...] = pull_ref[1 - now, base - 1 : base + zc + 1, tiles]
+        for h in range(1, hops + 1):
+            n = plan.back_count(h)
+            first = base + h * zc - 1
+            up[h - 1][...] = pull_ref[1 - now, first : first + n, tiles]
+            first = base + (1 - h) * zc - n + 1
+            down[h - 1][...] = pull_ref[1 - now, first : first + n, tiles]
+
+
+def finish_kernel(plan, *refs):
+    hops = plan.back_hops
+    pos_ref, sums_ref, skel_ref, p_ref, target_ref, ts_ref, mine_ref = refs[:7]
+    below, above = refs[7 : 7 + hops], refs[7 + hops : 7 + 2 * hops]
+    out_ref, loss_ref, bias_ref, h_ref, grad_ref = refs[7 + 2 * hops :]
+    rank = pos_ref[0]
+    zc = plan.zc
+    s1, s2, s5, s6, s7 = get_sums(sums_ref, 5)
+    s3, s4 = get_sums(skel_ref, 2)
     prec = (s1 + 1.0) / (s2 + 1.0)
     sens = (s3 + 1.0) / (s4 + 1.0)
-
-    @pl.when(step == 0)
-    def _():
-        zy_ref[...] = jnp.zeros_like(zy_ref)
-        pull_ref[...] = jnp.zeros_like(pull_ref)
-        h_ref[...] = jnp.zeros_like(h_ref)
-        count_tables(plan, cross_ref, None)
-        for n in range(win):
-            z = rank * zc + n - REACH
-            inside = ((z >= 0) & (z < plan.Z)).astype(f32)
-            w_ref[n] = (target_ref[n] - prec) * inside
-
-    def within(reach, body):
-        count = (zc + 2 * reach + size - 1) // size
-        first = jnp.minimum(REACH - reach, win - count * size)
-        over(first, count * size, size, body)
-
-    left = SECTIONS - 1 - step
-
-    def push(at):
-        values = []
-        for n in range(-1, size + 1):
-            spot = jnp.clip(at + n, 0, win - 1)
-            values.append(w_ref[spot] * q_ref[0, spot])
-        out = []
-        for n in range(size):
-            part = values[n] + values[n + 1] + values[n + 2]
-            part = part + y_neighbours(mask, part)
-            out.append((zy_ref, (at + n, tiles), part))
-        store_all(out)
-
-    within(left + 2, push)
-
-    def pull(at):
-        out = []
-        for n in range(size):
-            spot = at + n
-            box = x_box(plan, mask, zy_ref, spot)
-            inverse = cross_ref[kind_of(plan, rank, spot - REACH)[0]]
-            value = (h_ref[spot] - g2_ref[0, spot] * box) * inverse
-            out.append((pull_ref, (spot + 1, tiles), value))
-        store_all(out)
-
-    within(left + 2, pull)
-
-    def join(at):
-        out = []
-        for n in range(size):
-            spot = at + n
-            cur = pull_ref[spot + 1, tiles]
-
-            def load(offset, spot=spot):
-                return pull_ref[spot + 1, 8 + offset : 8 + offset + plan.tiles]
-
-            total = cur + pull_ref[spot, tiles] + pull_ref[spot + 2, tiles]
-            total = total + x_neighbours(plan, mask, load, cur) + y_neighbours(mask, cur)
-            w = w_ref[spot]
-            out.append((h_ref, spot, w * t_ref[0, spot] + total))
-            out.append((w_ref, spot, w * m_ref[0, spot]))
-        store_all(out)
-
-    within(left + 2, join)
-
-    @pl.when(step == SECTIONS - 1)
-    def _():
-        both = prec + sens
-        volume = s6 + s7 + 1.0
-        cl_loss = 1.0 - 2.0 * prec * sens / both
-        dice_loss = 1.0 - (2.0 * s5 + 1.0) / volume
-        loss_ref[...] = jnp.broadcast_to(0.5 * dice_loss + 0.5 * cl_loss, (8, LANES))
-        l0 = -(sens / both) * (sens / both) / (s2 + 1.0)
-        l2 = -(prec / both) * (prec / both) / (s4 + 1.0)
-        l4 = -1.0 / volume
-        l5 = 0.5 * (2.0 * s5 + 1.0) / (volume * volume)
-
-        def finish(n, total):
-            z = rank * zc + n - 1
-            inside = ((z >= 0) & (z < plan.Z)).astype(f32)
-            at = n + REACH - 1
-            predict = p_ref[n]
-            skel = l0 * jnp.exp(-temper * predict) * h_ref[at]
-            whole = skel + l2 * ts_ref[n] + l4 * target_ref[at] + l5
-            grad = whole * predict * (1.0 - predict) * inside
-            grad_ref[pl.ds(pl.multiple_of(n * plan.tiles, 8), plan.tiles)] = grad
-            mine = ((n >= 1) & (n <= zc)).astype(f32)
-            return total + grad * mine
-
-        total = lax.fori_loop(0, plan.span, finish, jnp.zeros((plan.tiles, LANES), f32))
-        bias_ref[...] = jnp.sum(total.reshape(-1, 8, LANES), axis=0)
-        lane = lane_iota((1, LANES))
-
-        def column(tile):
-            return [
-                grad_ref[pl.ds(plan.tiles + tile, zc, stride=plan.tiles)],
-                grad_ref[tile : tile + 1],
-                grad_ref[(zc + 1) * plan.tiles + tile : (zc + 1) * plan.tiles + tile + 1],
-            ]
-
-        for a in range(plan.gx):
-            pieces = [column(a * plan.own + q) for q in range(plan.own)]
-            zero = [jnp.zeros((zc, LANES), f32)] + [jnp.zeros((1, LANES), f32)] * 2
-            after = column((a + 1) * plan.own) if a < plan.gx - 1 else zero
-            before = column(a * plan.own - 1) if a > 0 else zero
-            if plan.shared:
-                pieces.append(
-                    [
-                        jnp.where(lane < plan.Y, x, 0.0)
-                        + jnp.where(lane >= LANES - plan.Y, y, 0.0)
-                        for x, y in zip(after, before)
-                    ]
-                )
-            else:
-                pieces += [after, before]
-            edges = [edge for piece in pieces for edge in piece[1:]]
-            rows = plan.R16
-            edges += [jnp.zeros((1, LANES), f32)] * (plan.extra16 * rows - len(edges))
-            whole = [piece[0] for piece in pieces]
-            if rows > zc:
-                fill = jnp.zeros((rows - zc, LANES), f32)
-                whole = [jnp.concatenate([piece, fill], axis=0) for piece in whole]
-            whole += [
-                jnp.concatenate(edges[n * rows : (n + 1) * rows], axis=0)
-                for n in range(plan.extra16)
-            ]
-            for q, piece in enumerate(whole):
-                piece = piece.astype(bf16)
-                for b in range(plan.gy):
-                    out_ref[a * plan.gy + b, q] = piece
+    both = prec + sens
+    volume = s6 + s7 + 1.0
+    cl_loss = 1.0 - 2.0 * prec * sens / both
+    dice_loss = 1.0 - (2.0 * s5 + 1.0) / volume
+    loss_ref[...] = jnp.broadcast_to(0.5 * dice_loss + 0.5 * cl_loss, (8, LANES))
+    l0 = -(sens / both) * (sens / both) / (s2 + 1.0)
+    l2 = -(prec / both) * (prec / both) / (s4 + 1.0)
+    l4 = -1.0 / volume
+    l5 = 0.5 * (2.0 * s5 + 1.0) / (volume * volume)
+
+    h_ref[...] = mine_ref[...]
+    for h in range(1, hops + 1):
+        n = plan.back_count(h)
+        h_ref[:n] += below[h - 1][...]
+        h_ref[plan.span - n :] += above[h - 1][...]
+
+    total = jnp.zeros((plan.tiles, LANES), f32)
+    for n in range(plan.span):
+        inside = 1.0 - kind_of(plan, rank, n - 1)[1]
+        predict = p_ref[n]
+        skel = l0 * jnp.exp(-temper * predict) * h_ref[n]
+        whole = skel + l2 * ts_ref[n] + l4 * target_ref[n] + l5
+        grad = whole * predict * (1.0 - predict) * inside
+        grad_ref[n * plan.tiles : (n + 1) * plan.tiles] = grad
+        if 1 <= n <= zc:
+            total = total + grad
+    bias_ref[...] = jnp.sum(total.reshape(-1, 8, LANES), axis=0)
+    lane = lane_iota((1, LANES))
+
+    def column(tile):
+        return [
+            grad_ref[pl.ds(plan.tiles + tile, zc, stride=plan.tiles)],
+            grad_ref[tile : tile + 1],
+            grad_ref[(zc + 1) * plan.tiles + tile : (zc + 1) * plan.tiles + tile + 1],
+        ]
+
+    for a in range(plan.gx):
+        pieces = [column(a * plan.own + q) for q in range(plan.own)]
+        zero = [jnp.zeros((zc, LANES), f32)] + [jnp.zeros((1, LANES), f32)] * 2
+        after = column((a + 1) * plan.own) if a < plan.gx - 1 else zero
+        before = column(a * plan.own - 1) if a > 0 else zero
+        if plan.shared:
+            pieces.append(
+                [
+                    jnp.where(lane < plan.Y, x, 0.0) + jnp.where(lane >= LANES - plan.Y, y, 0.0)
+                    for x, y in zip(after, before)
+                ]
+            )
+        else:
+            pieces += [after, before]
+        edges = [edge for piece in pieces for edge in piece[1:]]
+        rows = plan.R16
+        edges += [jnp.zeros((1, LANES), f32)] * (plan.extra16 * rows - len(edges))
+        whole = [piece[0] for piece in pieces]
+        if rows > zc:
+            fill = jnp.zeros((rows - zc, LANES), f32)
+            whole = [jnp.concatenate([piece, fill], axis=0) for piece in whole]
+        whole += [
+            jnp.concatenate(edges[n * rows : (n + 1) * rows], axis=0) for n in range(plan.extra16)
+        ]
+        for q, piece in enumerate(whole):
+            piece = piece.astype(bf16)
+            for b in range(plan.gy):
+                out_ref[a * plan.gy + b, q] = piece
 
 
 def weight_kernel(plan, pos_ref, f_ref, bias_ref, got_ref, gw_ref, g_ref, dw_ref):
@@ -773,6 +816,7 @@
 ANY = pl.BlockSpec(memory_space=pl.ANY)
 FAR = pl.BlockSpec(memory_space=pltpu.HBM)
 MIB = 1024 * 1024
+ALMOST_ALL = 65_680_000
 
 
 def shape(dims, dtype=f32):
@@ -853,7 +897,7 @@
             pltpu.VMEM(features.shape, bf16),
             pltpu.SemaphoreType.DMA((4,)),
         ],
-        62 * MIB,
+        ALMOST_ALL,
     )
 
     def planes(array):
@@ -888,17 +932,57 @@
     around = hops_of(parts, plan.hops)
     label_around = hops_of(label_parts, plan.label_hops)
 
-    window = (plan.win, tiles, LANES)
+    slab = (zc, tiles, LANES)
     span = (plan.span, tiles, LANES)
+    everyone = shape((plan.ranks, 8, LANES))
     table = pltpu.VMEM((3, tiles, LANES), f32)
-    room = plan.win + 2 + plan.span_block
-    target, ts = call(
+
+    def section_grid(kernel, operands, streamed, outs, records, micros, scratch, backwards):
+        def spec(dims):
+            if backwards:
+                return pl.BlockSpec((1,) + dims, lambda n: (SECTIONS - 1 - n, 0, 0, 0))
+            return pl.BlockSpec((1,) + dims, lambda n: (n, 0, 0, 0))
+
+        blocks = [shape(a.shape[1:]) for a in streamed] + [shape(r) for r in records]
+        fixed = [a for a in operands if a.ndim > 1]
+        return pl.pallas_call(
+            functools.partial(kernel, plan),
+            grid=(SECTIONS,),
+            out_shape=[shape((SECTIONS,) + r) for r in records] + outs,
+            in_specs=[VMEM if a.ndim > 1 else SMEM for a in operands]
+            + [spec(a.shape[1:]) for a in streamed],
+            out_specs=[spec(r) for r in records] + [VMEM] * len(outs),
+            scratch_shapes=scratch,
+            **limits(blocks * 2 + outs + fixed, scratch, micros, ALMOST_ALL),
+        )(*operands, *streamed)
+
+    m, q, t, grown, predict, sums = section_grid(
+        forward_kernel,
+        (pos, bias, label_parts[0], parts[0], *around),
+        (),
+        [shape(span), everyone],
+        [slab, slab, slab, span],
+        11,
+        [
+            pltpu.VMEM((2, plan.planes, plan.pad, LANES), f32),
+            pltpu.VMEM((2, plan.planes, tiles, LANES), f32),
+            pltpu.VMEM((zc, plan.pad, LANES), f32),
+            pltpu.VMEM(slab, f32),
+            table,
+            table,
+        ],
+        False,
+    )
+    sums = everywhere(sums)
+    room = plan.win + 2 + plan.erode_block
+    target, ts, skel_sums = call(
         target_kernel,
-        [shape(window), shape(span)],
-        [SMEM] + [VMEM] * (1 + 2 * plan.label_hops),
-        (pos, label_parts[0], *label_around),
-        14,
+        [shape(span), shape(span), everyone],
+        [SMEM] + [VMEM] * (2 + 2 * plan.label_hops),
+        (pos, predict, label_parts[0], *label_around),
+        13,
         [
+            pltpu.VMEM((plan.win, tiles, LANES), f32),
             pltpu.VMEM((2, room, plan.pad, LANES), f32),
             pltpu.VMEM((2, room, tiles, LANES), f32),
             pltpu.VMEM((plan.span, plan.pad, LANES), f32),
@@ -906,54 +990,43 @@
             table,
         ],
     )
-    record = pl.BlockSpec((1,) + window, lambda n: (n, 0, 0, 0))
-    operands = (pos, bias, target, ts, parts[0], *around)
-    scratch = [
-        pltpu.VMEM((2, plan.planes, plan.pad, LANES), f32),
-        pltpu.VMEM((2, plan.planes, tiles, LANES), f32),
-        pltpu.VMEM((plan.win, plan.pad, LANES), f32),
-        pltpu.VMEM(window, f32),
-        table,
-        table,
+    skel_sums = everywhere(skel_sums)
+    outer = [
+        shape((plan.back_count(h), tiles, LANES)) for h in range(1, plan.back_hops + 1)
     ]
-    small = [shape(span), shape((plan.ranks, 8, LANES))]
-    outs = pl.pallas_call(
-        functools.partial(forward_kernel, plan),
-        grid=(SECTIONS,),
-        out_shape=[shape((SECTIONS,) + window)] * 4 + small,
-        in_specs=[SMEM, SMEM] + [VMEM] * (len(operands) - 2),
-        out_specs=[record] * 4 + [VMEM] * 2,
-        scratch_shapes=scratch,
-        **limits([shape(window)] * 8 + small + list(operands[2:]), scratch, 25),
-    )(*operands)
-    m, q, t, g2, predict, sums = outs
-    sums = everywhere(sums)
-
-    back = pl.BlockSpec((1,) + window, lambda n: (SECTIONS - 1 - n, 0, 0, 0))
-    operands = (pos, sums, m, q, t, g2, predict, target, ts)
-    scratch = [
-        pltpu.VMEM(window, f32),
-        pltpu.VMEM(window, f32),
-        pltpu.VMEM((plan.win, plan.pad, LANES), f32),
-        pltpu.VMEM((plan.win + 2, plan.pad, LANES), f32),
-        table,
-        pltpu.VMEM((plan.span * tiles, LANES), f32),
-    ]
-    outs = [
-        shape((members, sent + plan.extra16, plan.R16, LANES), bf16),
-        shape((8, LANES)),
-        shape((8, LANES)),
-    ]
-    arrays = [shape(window)] * 8 + outs + [sums, predict, target, ts]
-    grad_sent, loss, bias_part = pl.pallas_call(
-        functools.partial(backward_kernel, plan),
-        grid=(SECTIONS,),
-        out_shape=outs,
-        in_specs=[SMEM, VMEM] + [back] * 4 + [VMEM] * 3,
-        out_specs=[VMEM] * 3,
-        scratch_shapes=scratch,
-        **limits(arrays, scratch, 20),
-    )(*operands)
+    mine, *outer = section_grid(
+        backward_kernel,
+        (pos, sums, label_parts[0]),
+        (m, q, t, grown),
+        [shape(span)] + outer * 2,
+        [],
+        11,
+        [
+            pltpu.VMEM(slab, f32),
+            pltpu.VMEM((zc + 4, tiles, LANES), f32),
+            pltpu.VMEM((plan.pull_planes, tiles, LANES), f32),
+            pltpu.VMEM((plan.span, plan.pad, LANES), f32),
+            pltpu.VMEM((2, plan.pull_planes, plan.pad, LANES), f32),
+            table,
+        ],
+        True,
+    )
+    beyond = []
+    for sign, arrays in ((1, outer[: plan.back_hops]), (-1, outer[plan.back_hops :])):
+        for h in range(1, plan.back_hops + 1):
+            beyond.append(hop(arrays[h - 1], sign * h))
+    grad_sent, loss, bias_part = call(
+        finish_kernel,
+        [
+            shape((members, sent + plan.extra16, plan.R16, LANES), bf16),
+            shape((8, LANES)),
+            shape((8, LANES)),
+        ],
+        [SMEM] + [VMEM] * (6 + 2 * plan.back_hops),
+        (pos, sums, skel_sums, predict, target, ts, mine, *beyond),
+        2,
+        [pltpu.VMEM(span, f32), pltpu.VMEM((plan.span * tiles, LANES), f32)],
+    )
 
     moved = shape((plan.nx + 2, 3 * plan.Y, plan.nz), bf16)
     partial, g = call(

time: 141 us -> 147 us (1.043)
  blocking collectives: 36.1 us -> 22.7 us
  starting transfers between devices: 19.5 us -> 32.9 us
  waiting for transfers between devices: 5.1 us -> 14.4 us
  Pallas kernels: 74.6 us -> 65.6 us
  local copies, waits for them, and re-layouts: 3.47 us -> 9.27 us
    all_to_all x1 -> x0, blocking collectives: 15.4 us -> none  [everywhere(): return lax.all_to_all(array, ALL_AXES, 0, 0, tiled=True)]
    all_to_all x1 -> x3, starting transfers between devices: 2.56 us -> 14.5 us  [everywhere(): return lax.all_to_all(array, ALL_AXES, 0, 0, tiled=True)]
    pallas_call x2, Pallas kernels: 39.6 us -> 29.4 us  [section_grid(): pl.pallas_call(functools.partial(kernel, plan), grid=(SECTIONS,), out_sha...]
    ppermute x6, waiting for transfers between devices: 4.91 us -> 14.2 us  [hop(): return lax.ppermute(array, ALL_AXES, pairs)]
    unnamed x17 -> x35, local copies, waits for them, and re-layouts: 2.95 us -> 8.75 us
    all_to_all x2, blocking collectives: 20.7 us -> 22.7 us  [exchange(): return lax.all_to_all(array, GROUP, 0, 0, tiled=True)]
    ppermute x6, starting transfers between devices: 13.6 us -> 15 us  [hop(): return lax.ppermute(array, ALL_AXES, pairs)]
    pallas_call x8 -> x9, Pallas kernels: 35 us -> 36.2 us  [call(): pl.pallas_call(functools.partial(kernel, plan), out_shape=out_shape, in_s...]
  transfers between devices with their start and end apart: 8 -> 10, of which waited for: 2 -> 6; matrix products, arithmetic and copies ran while one was open for 0% -> 0% of each run, Pallas kernels for 15% -> 24%
where the time goes in v5:
time: 147 us; the launch traced here: 146 us
  Pallas kernels  65.6 us (45%)
  starting transfers between devices  32.9 us (22%)
  blocking collectives  22.7 us (15%)
  waiting for transfers between devices  14.4 us (10%)
  local copies, waits for them, and re-layouts  9.27 us (6%)
  between operations  1.52 us (1%)
    pallas_call x9, Pallas kernels, call(): pl.pallas_call(functools.partial(kernel, plan), out_shape=out_shape, in_s...  36.2 us
    pallas_call x2, Pallas kernels, section_grid(): pl.pallas_call(functools.partial(kernel, plan), grid=(SECTIONS,), out_sha...  29.4 us
    all_to_all x2, blocking collectives, exchange(): return lax.all_to_all(array, GROUP, 0, 0, tiled=True)  22.7 us
    ppermute x6, starting transfers between devices, hop(): return lax.ppermute(array, ALL_AXES, pairs)  15 us
    all_to_all x3, starting transfers between devices, everywhere(): return lax.all_to_all(array, ALL_AXES, 0, 0, tiled=True)  14.5 us
    ppermute x6, waiting for transfers between devices, hop(): return lax.ppermute(array, ALL_AXES, pairs)  14.2 us
    unnamed x35, local copies, waits for them, and re-layouts  8.75 us
    all_to_all x1, starting transfers between devices, exchange(): return lax.all_to_all(array, GROUP, 0, 0, tiled=True)  3.37 us
  transfers between devices with their start and end apart: 10, of which 6 were waited for; matrix products, arithmetic and copies ran while one was open for 0% of the time, Pallas kernels for 24%

profile of v5, /device:TPU:0, one launch (start us, length us, event | category | flops | bytes accessed | tf_op | source)
XLA Modules:
  0.0 146.4 jit_solution(1769141816161803703)
XLA Ops:
  0.6 0.1 pad_add_fusion.pos_ref.refs_0_
  0.7 0.9 copy-done.10
  1.6 0.6 shard_map.75.label_ref
  2.3 0.6 copy-done.1
  2.9 6.9 %shard_map.77 = f32[8,6,16,128]{3,2,1,0:T(8,128)} custom-call(s32[2]{0:T(128)} %copy-done.11, bf16[27,32]{1,0:T(8,128)(2,1)} %w_ref.1, bf16[32,16,16,128]{3,2,1,0:T(8,128)(2,1)} %f_ref.1, bf16[8,4,16,128]{3,2,1,0:T(8,128)(2,1)} %copy-done.1), custom_call_target="tpu_custom_call" | custom-call | bytes 17500000 | tf_op jit(solution)/shard_map/pallas_call | solution.py:859
  9.8 0.0 copy-start.12
  9.8 13.0 %all_to_all.30.got_ref = f32[8,6,16,128]{3,2,1,0:T(8,128)S(1)} all-to-all(f32[8,6,16,128]{3,2,1,0:T(8,128)} %shard_map.77), channel_id=1, replica_groups=mesh['gx'=4,'gy'=2,'gz'=4] {'gx','gy'}, dimensions={0} | all-to-all | bytes 786432 | tf_op jit(solution)/shard_map/all_to_all | solution.py:869
  22.8 3.4 %all-to-all-start = ((bf16[8,4,16,128]{3,2,1,0:T(8,128)(2,1)}), bf16[8,4,16,128]{3,2,1,0:T(8,128)(2,1)S(1)}, u32[]{:S(2)}, u32[]{:S(2)}) async-start(bf16[8,4,16,128]{3,2,1,0:T(8,128)(2,1)} %copy-done.1), calls=%async_computation | async-start | bytes 262144 | tf_op jit(solution)/shard_map/all_to_all | solution.py:869
  26.2 0.1 shard_map.78
  26.3 0.7 copy-done.8
  27.0 3.8 %collective-permute-start = (f32[13,16,128]{2,1,0:T(8,128)S(1)}, f32[13,16,128]{2,1,0:T(8,128)S(1)}, u32[]{:S(2)}, u32[]{:S(2)}) collective-permute-start(f32[13,16,128]{2,1,0:T(8,128)S(1)} %bitcast.17), channel_id=1, source_target_pairs={{0,4},{4,8},{8,12},{12,16},{16,20},{20,24},{24,28},{28,1},{1,5},{5... | collective-permute-start | bytes 319496 | tf_op jit(solution)/shard_map/ppermute | solution.py:883
  30.8 1.3 collective-permute-start.1
  32.7 0.0 all-to-all-done.got_ref
  32.7 0.1 shard_map.76
  32.8 0.6 copy-done.4
  33.4 0.0 collective-permute-done.refs_4_
  33.4 4.0 %collective-permute-done.1.refs_5_ = f32[13,16,128]{2,1,0:T(8,128)S(1)} collective-permute-done((f32[13,16,128]{2,1,0:T(8,128)S(1)}, f32[13,16,128]{2,1,0:T(8,128)S(1)}, u32[]{:S(2)}, u32[]{:S(2)}) %collective-permute-start.1) | collective-permute-done | bytes 106528 | tf_op jit(solution)/shard_map/ppermute | solution.py:883
  37.4 0.6 copy-done.15
  38.1 15.2 %shard_map.79 = (f32[11,16,16,128]{3,2,1,0:T(8,128)}, f32[11,16,16,128]{3,2,1,0:T(8,128)}, f32[11,16,16,128]{3,2,1,0:T(8,128)}, f32[11,18,16,128]{3,2,1,0:T(8,12...) custom-call(s32[2]{0:T(128)} %copy-done.11, f32[1]{0:T(128)S(6)} %copy.9.refs_1_, bf16[16,16,128]{2,1,0:T(8,128)(2,1)} %bitcast.11, ...), custom_call_target="tpu_custom_call" | custom-call | bytes 27500000 | tf_op jit(solution)/shard_map/pallas_call | solution.py:948
  53.2 5.3 %all-to-all-start.2 = ((f32[32,8,128]{2,1,0:T(8,128)}), f32[32,8,128]{2,1,0:T(8,128)S(1)}, u32[]{:S(2)}, u32[]{:S(2)}) async-start(f32[32,8,128]{2,1,0:T(8,128)} %get-tuple-element.33), calls=%async_computation.2 | async-start | bytes 262144 | tf_op jit(solution)/shard_map/all_to_all | solution.py:872
  58.6 3.7 %collective-permute-start.2 = (bf16[13,16,128]{2,1,0:T(8,128)(2,1)S(1)}, bf16[13,16,128]{2,1,0:T(8,128)(2,1)S(1)}, u32[]{:S(2)}, u32[]{:S(2)}) collective-permute-start(bf16[13,16,128]{2,1,0:T(8,128)(2,1)S(1)} %bitcast.19), channel_id=1, source_target_pairs={{0,4},{4,8},{8,12},{12,16},{16,20},{20,24},{24,28},{28,1},{1,5},{5... | collective-permute-start | bytes 159752 | tf_op jit(solution)/shard_map/ppermute | solution.py:883
  62.3 1.3 collective-permute-start.3
  63.6 0.5 collective-permute-done.2.refs_3_
  64.1 4.2 %collective-permute-done.3.refs_4_ = bf16[13,16,128]{2,1,0:T(8,128)(2,1)S(1)} collective-permute-done((bf16[13,16,128]{2,1,0:T(8,128)(2,1)S(1)}, bf16[13,16,128]{2,1,0:T(8,128)(2,1)S(1)}, u32[]{:S(2)}, u32[]{:S(2)}) %collective-permute-start.3) | collective-permute-done | bytes 53280 | tf_op jit(solution)/shard_map/ppermute | solution.py:883
  68.3 0.8 copy-done.5
  69.1 0.9 copy-done.6
  70.0 13.7 %shard_map.80 = (f32[18,16,128]{2,1,0:T(8,128)S(1)}, f32[18,16,128]{2,1,0:T(8,128)S(1)}, f32[32,8,128]{2,1,0:T(8,128)}) custom-call(s32[2]{0:T(128)S(1)} %copy-done.12, f32[18,16,128]{2,1,0:T(8,128)S(1)} %copy-done.6, bf16[16,16,128]{2,1,0:T(8,128)(2,1)S(1)} %bitcast.13, bf16[13,16,128]{2,1,0:T(8,128)(2,1)S(1)} %collective-permute-done.2.refs_3_, ...), custom_call_target="tpu_custom_call" | custom-call | bytes 32500000 | tf_op jit(solution)/shard_map/pallas_call | solution.py:859
  83.8 0.0 all-to-all-done.2.refs_1_
  83.8 5.5 %all-to-all-start.3 = ((f32[32,8,128]{2,1,0:T(8,128)}), f32[32,8,128]{2,1,0:T(8,128)S(1)}, u32[]{:S(2)}, u32[]{:S(2)}) async-start(f32[32,8,128]{2,1,0:T(8,128)} %get-tuple-element.37), calls=%async_computation.3 | async-start | bytes 262144 | tf_op jit(solution)/shard_map/all_to_all | solution.py:872
  89.3 0.0 copy-start.13
  89.3 14.2 %shard_map.81 = (f32[18,16,128]{2,1,0:T(8,128)}, f32[13,16,128]{2,1,0:T(8,128)}, f32[13,16,128]{2,1,0:T(8,128)}) custom-call(s32[2]{0:T(128)} %copy-done.11, f32[32,8,128]{2,1,0:T(8,128)} %copy-done.2, bf16[16,16,128]{2,1,0:T(8,128)(2,1)} %bitcast.12, f32[11,16,16,128]{3,2,1,0:T(8,128)} %get-tuple-element.40.refs_3_, ...), custom_call_target="tpu_custom_call" | custom-call | bytes 27500000 | tf_op jit(solution)/shard_map/pallas_call | solution.py:948
  103.6 3.7 %collective-permute-start.4 = (f32[13,16,128]{2,1,0:T(8,128)}, f32[13,16,128]{2,1,0:T(8,128)S(1)}, u32[]{:S(2)}, u32[]{:S(2)}) collective-permute-start(f32[13,16,128]{2,1,0:T(8,128)} %get-tuple-element.45), channel_id=1, source_target_pairs={{0,4},{4,8},{8,12},{12,16},{16,20},{20,24},{24,28},{28,1},{1,5},{5... | collective-permute-start | bytes 319496 | tf_op jit(solution)/shard_map/ppermute | solution.py:883
  107.2 1.3 collective-permute-start.5
  108.5 1.5 %collective-permute-done.4.refs_7_ = f32[13,16,128]{2,1,0:T(8,128)S(1)} collective-permute-done((f32[13,16,128]{2,1,0:T(8,128)}, f32[13,16,128]{2,1,0:T(8,128)S(1)}, u32[]{:S(2)}, u32[]{:S(2)}) %collective-permute-start.4) | collective-permute-done | bytes 106528 | tf_op jit(solution)/shard_map/ppermute | solution.py:883
  110.0 4.0 %collective-permute-done.5.refs_8_ = f32[13,16,128]{2,1,0:T(8,128)S(1)} collective-permute-done((f32[13,16,128]{2,1,0:T(8,128)}, f32[13,16,128]{2,1,0:T(8,128)S(1)}, u32[]{:S(2)}, u32[]{:S(2)}) %collective-permute-start.5) | collective-permute-done | bytes 106528 | tf_op jit(solution)/shard_map/ppermute | solution.py:883
  114.1 0.9 copy-done.3
  115.0 0.9 copy-done.9
  115.9 0.8 shard_map.82
  116.7 0.0 copy-start.16
  116.7 9.7 %all_to_all.31.got_ref = bf16[8,6,16,128]{3,2,1,0:T(8,128)(2,1)S(1)} all-to-all(bf16[8,6,16,128]{3,2,1,0:T(8,128)(2,1)S(1)} %get-tuple-element.49), channel_id=1, replica_groups=mesh['gx'=4,'gy'=2,'gz'=4] {'gx','gy'}, dimensions={0} | all-to-all | bytes 393216 | tf_op jit(solution)/shard_map/all_to_all | solution.py:869
  126.4 1.6 %copy-done = bf16[32,16,16,128]{3,2,1,0:T(8,128)(2,1)S(1)} copy-done((bf16[32,16,16,128]{3,2,1,0:T(8,128)(2,1)S(1)}, bf16[32,16,16,128]{3,2,1,0:T(8,128)(2,1)}, u32[]{:S(2)}) %copy-start) | copy-done | bytes 2097176
  128.0 6.3 %shard_map.83 = (f32[32,8,128]{2,1,0:T(8,128)}, bf16[18,96,128]{2,1,0:T(8,128)(2,1)S(1)}) custom-call(s32[2]{0:T(128)S(1)} %copy-done.13, bf16[32,16,16,128]{3,2,1,0:T(8,128)(2,1)S(1)} %copy-done, f32[8,128]{1,0:T(8,128)S(1)} %get-tuple-element.48.bias_ref, bf16[8,6,16,128]{3,2,1,0:T(8,128)(2,1)S(1)} %all_to_all.31.got_ref), custom_call_target="tpu_custom_call" | custom-call | bytes 12500000 | tf_op jit(solution)/shard_map/pallas_call | solution.py:859
  134.2 3.7 %all-to-all-start.5 = ((f32[32,8,128]{2,1,0:T(8,128)}), f32[32,8,128]{2,1,0:T(8,128)S(1)}, u32[]{:S(2)}, u32[]{:S(2)}) async-start(f32[32,8,128]{2,1,0:T(8,128)} %get-tuple-element.51.after_ref), calls=%async_computation.5 | async-start | bytes 262144 | tf_op jit(solution)/shard_map/all_to_all | solution.py:872
  137.9 0.1 copy.8
  138.0 0.5 slice.3
  138.5 7.0 %shard_map.84 = bf16[32,16,16,128]{3,2,1,0:T(8,128)(2,1)} custom-call(s32[2]{0:T(128)S(1)} %copy-done.13, bf16[32,27]{1,0:T(8,128)(2,1)S(1)} %bitcast.15, bf16[18,96,128]{2,1,0:T(8,128)(2,1)S(1)} %get-tuple-element.50.g_ref, f32[32,8,128]{2,1,0:T(8,128)} %get-tuple-element.51.after_ref), custom_call_target="tpu_custom_call" | custom-call | bytes 12500000 | tf_op jit(solution)/shard_map/pallas_call | solution.py:859
  145.5 0.2 all-to-all-done.5.got_ref
  145.7 0.7 shard_map.85
  (22 shorter events, 0.0 us)
Async XLA Ops:
  0.7 0.9 copy-start.10
  1.6 0.7 copy-start.11
  2.3 0.6 copy-start.1
  9.8 58.5 %copy-start.12 = (s32[2]{0:T(128)S(1)}, s32[2]{0:T(128)}, u32[]{:S(2)}) copy-start(s32[2]{0:T(128)} %copy-done.11) | copy-start | bytes 28
  22.8 9.9 %all-to-all-start = ((bf16[8,4,16,128]{3,2,1,0:T(8,128)(2,1)}), bf16[8,4,16,128]{3,2,1,0:T(8,128)(2,1)S(1)}, u32[]{:S(2)}, u32[]{:S(2)}) async-start(bf16[8,4,16,128]{3,2,1,0:T(8,128)(2,1)} %copy-done.1), calls=%async_computation | async-start | bytes 262144 | tf_op jit(solution)/shard_map/all_to_all | solution.py:869
  26.3 0.7 copy-start.8
  27.0 6.5 %collective-permute-start = (f32[13,16,128]{2,1,0:T(8,128)S(1)}, f32[13,16,128]{2,1,0:T(8,128)S(1)}, u32[]{:S(2)}, u32[]{:S(2)}) collective-permute-start(f32[13,16,128]{2,1,0:T(8,128)S(1)} %bitcast.17), channel_id=1, source_target_pairs={{0,4},{4,8},{8,12},{12,16},{16,20},{20,24},{24,28},{28,1},{1,5},{5... | collective-permute-start | bytes 319496 | tf_op jit(solution)/shard_map/ppermute | solution.py:883
  30.8 6.6 %collective-permute-start.1 = (f32[13,16,128]{2,1,0:T(8,128)S(1)}, f32[13,16,128]{2,1,0:T(8,128)S(1)}, u32[]{:S(2)}, u32[]{:S(2)}) collective-permute-start(f32[13,16,128]{2,1,0:T(8,128)S(1)} %bitcast.16), channel_id=1, source_target_pairs={{4,0},{8,4},{12,8},{16,12},{20,16},{24,20},{28,24},{1,28},{5,1},{9... | collective-permute-start | bytes 319496 | tf_op jit(solution)/shard_map/ppermute | solution.py:883
  32.8 0.6 copy-start.4
  33.4 4.0 %copy-start.14 = (f32[13,16,128]{2,1,0:T(8,128)}, f32[13,16,128]{2,1,0:T(8,128)S(1)}, u32[]{:S(2)}) copy-start(f32[13,16,128]{2,1,0:T(8,128)S(1)} %collective-permute-done.refs_4_) | copy-start | bytes 319492
  37.4 0.6 copy-start.15
  53.2 30.5 %all-to-all-start.2 = ((f32[32,8,128]{2,1,0:T(8,128)}), f32[32,8,128]{2,1,0:T(8,128)S(1)}, u32[]{:S(2)}, u32[]{:S(2)}) async-start(f32[32,8,128]{2,1,0:T(8,128)} %get-tuple-element.33), calls=%async_computation.2 | async-start | bytes 262144 | tf_op jit(solution)/shard_map/all_to_all | solution.py:872
  58.6 5.5 %collective-permute-start.2 = (bf16[13,16,128]{2,1,0:T(8,128)(2,1)S(1)}, bf16[13,16,128]{2,1,0:T(8,128)(2,1)S(1)}, u32[]{:S(2)}, u32[]{:S(2)}) collective-permute-start(bf16[13,16,128]{2,1,0:T(8,128)(2,1)S(1)} %bitcast.19), channel_id=1, source_target_pairs={{0,4},{4,8},{8,12},{12,16},{16,20},{20,24},{24,28},{28,1},{1,5},{5... | collective-permute-start | bytes 159752 | tf_op jit(solution)/shard_map/ppermute | solution.py:883
  62.3 6.0 %collective-permute-start.3 = (bf16[13,16,128]{2,1,0:T(8,128)(2,1)S(1)}, bf16[13,16,128]{2,1,0:T(8,128)(2,1)S(1)}, u32[]{:S(2)}, u32[]{:S(2)}) collective-permute-start(bf16[13,16,128]{2,1,0:T(8,128)(2,1)S(1)} %bitcast.18), channel_id=1, source_target_pairs={{4,0},{8,4},{12,8},{16,12},{20,16},{24,20},{28,24},{1,28},{5,1},{9... | collective-permute-start | bytes 159752 | tf_op jit(solution)/shard_map/ppermute | solution.py:883
  68.3 0.8 copy-start.5
  69.1 0.9 copy-start.6
  83.8 5.5 %copy-start.2 = (f32[32,8,128]{2,1,0:T(8,128)}, f32[32,8,128]{2,1,0:T(8,128)S(1)}, u32[]{:S(2)}) copy-start(f32[32,8,128]{2,1,0:T(8,128)S(1)} %all-to-all-done.2.refs_1_) | copy-start | bytes 393220
  83.8 24.8 %all-to-all-start.3 = ((f32[32,8,128]{2,1,0:T(8,128)}), f32[32,8,128]{2,1,0:T(8,128)S(1)}, u32[]{:S(2)}, u32[]{:S(2)}) async-start(f32[32,8,128]{2,1,0:T(8,128)} %get-tuple-element.37), calls=%async_computation.3 | async-start | bytes 262144 | tf_op jit(solution)/shard_map/all_to_all | solution.py:872
  89.3 24.7 %copy-start.7 = (f32[18,16,128]{2,1,0:T(8,128)S(1)}, f32[18,16,128]{2,1,0:T(8,128)}, u32[]{:S(2)}) copy-start(f32[18,16,128]{2,1,0:T(8,128)} %get-tuple-element.34.refs_1_.refs_3_) | copy-start | bytes 442372
  89.3 24.7 %copy-start.13 = (s32[2]{0:T(128)S(1)}, s32[2]{0:T(128)}, u32[]{:S(2)}) copy-start(s32[2]{0:T(128)} %copy-done.11) | copy-start | bytes 28
  103.6 6.5 %collective-permute-start.4 = (f32[13,16,128]{2,1,0:T(8,128)}, f32[13,16,128]{2,1,0:T(8,128)S(1)}, u32[]{:S(2)}, u32[]{:S(2)}) collective-permute-start(f32[13,16,128]{2,1,0:T(8,128)} %get-tuple-element.45), channel_id=1, source_target_pairs={{0,4},{4,8},{8,12},{12,16},{16,20},{20,24},{24,28},{28,1},{1,5},{5... | collective-permute-start | bytes 319496 | tf_op jit(solution)/shard_map/ppermute | solution.py:883
  107.2 6.8 %collective-permute-start.5 = (f32[13,16,128]{2,1,0:T(8,128)}, f32[13,16,128]{2,1,0:T(8,128)S(1)}, u32[]{:S(2)}, u32[]{:S(2)}) collective-permute-start(f32[13,16,128]{2,1,0:T(8,128)} %get-tuple-element.46), channel_id=1, source_target_pairs={{4,0},{8,4},{12,8},{16,12},{20,16},{24,20},{28,24},{1,28},{5,1},{9... | collective-permute-start | bytes 319496 | tf_op jit(solution)/shard_map/ppermute | solution.py:883
  114.1 0.9 copy-start.3
  115.0 0.9 copy-start.9
  116.7 21.2 %copy-start.16 = (bf16[27,32]{1,0:T(8,128)(2,1)S(1)}, bf16[27,32]{1,0:T(8,128)(2,1)}, u32[]{:S(2)}) copy-start(bf16[27,32]{1,0:T(8,128)(2,1)} %w_ref.1) | copy-start | bytes 5188
  126.4 1.6 %copy-start = (bf16[32,16,16,128]{3,2,1,0:T(8,128)(2,1)S(1)}, bf16[32,16,16,128]{3,2,1,0:T(8,128)(2,1)}, u32[]{:S(2)}) copy-start(bf16[32,16,16,128]{3,2,1,0:T(8,128)(2,1)} %f_ref.1) | copy-start | bytes 6291460
  134.2 11.5 %all-to-all-start.5 = ((f32[32,8,128]{2,1,0:T(8,128)}), f32[32,8,128]{2,1,0:T(8,128)S(1)}, u32[]{:S(2)}, u32[]{:S(2)}) async-start(f32[32,8,128]{2,1,0:T(8,128)} %get-tuple-element.51.after_ref), calls=%async_computation.5 | async-start | bytes 262144 | tf_op jit(solution)/shard_map/all_to_all | solution.py:872
